TPU v7x, 512 devices: a whole 4x4x16 slice. The times are simulated.
512 devices in a mesh: shot: 16 (over z_hi, y), slab: 32 (over z_lo, x, core).
Axes of the slice: x: 4, y: 4, z: 16 (z_hi: 4, z_lo: 4; z = z_hi * 4 + z_lo), core: 2. Of those that a mesh axis runs over, the one named last changes fastest.
Arguments:
- wave_now: float32 [16, 512, 64, 128], P('shot', 'slab'), may hold values from -6 to 6
- wave_prev: float32 [16, 512, 64, 128], P('shot', 'slab'), may hold values from -6 to 6
- courant: float32 [512, 64, 128], P('slab'), may hold values from 0.05 to 0.2
- forward: bfloat16 [16, 3, 512, 64, 128], P('shot', None, 'slab'), may hold values from -6 to 6
- receivers: int32 [16, 3, 256], P('shot'), may hold values from 0 to 511, as said below
- residual: float32 [16, 3, 256], P('shot'), may hold values from -6 to 6
- aperture: int32 [16, 2], P('shot'), may hold values from 0 to 512, as said below
- latent: bfloat16 [256, 32, 4096], P('slab', 'shot')
- weight: float32 [64, 8], replicated, may hold values from -0.75 to 0.75
Outputs:
- wave_after: float32 [16, 512, 64, 128], P('shot', 'slab')
- wave_before: float32 [16, 512, 64, 128], P('shot', 'slab')
- latent_grad: float32 [256, 32, 4096], P('slab', 'shot')
- weight_grad: float32 [64, 8], replicated
Inputs may be any that keep to these rules, and one draw needn't show every extreme that they name: receivers[s,0,r], receivers[s,1,r], receivers[s,2,r] are an x, y and depth cell inside the grid. Each shot's aperture is a range of at least 512 // 4 x cells with aperture[s,0] < aperture[s,1].
All inputs are finite; a program needn't handle non-finite values.
Results may differ from a plain program's by a relative error of at most 0.0003.
Values sent between devices are 32-bit elements; how exact they have to be, the bound alone decides.
No kernel may reach another device: no remote copies, remote signals or barrier semaphores. Data moves between devices by JAX's collectives and lax.ppermute only.
A program may use at most 64 MiB of HBM per device.

v0:
```python
import math

import jax
import jax.numpy as jnp
from jax import lax
from jax.sharding import PartitionSpec as P

STEPS = 3


stencil_weights = (-205.0 / 72.0, 8.0 / 5.0, -1.0 / 5.0, 8.0 / 315.0, -1.0 / 560.0)


def extended(block, sides, width):
    for axis, dim in sides:
        count = lax.axis_size(axis)
        forward = [(i, i + 1) for i in range(count - 1)]
        backward = [(target, source) for source, target in forward]
        low = lax.ppermute(
            lax.slice_in_dim(block, block.shape[dim] - width, None, axis=dim), axis, forward
        )
        high = lax.ppermute(lax.slice_in_dim(block, 0, width, axis=dim), axis, backward)
        block = jnp.concatenate([low, block, high], axis=dim)
    return block


def laplace(padded):
    size_x = padded.shape[0] - 8
    size_y = padded.shape[1] - 8
    size_z = padded.shape[2] - 8

    def moved(shift_x, shift_y, shift_z):
        return padded[
            4 + shift_x : 4 + shift_x + size_x,
            4 + shift_y : 4 + shift_y + size_y,
            4 + shift_z : 4 + shift_z + size_z,
        ]

    total = 3.0 * stencil_weights[0] * moved(0, 0, 0)
    for offset in range(1, 5):
        cycle_sum = moved(offset, 0, 0) + moved(-offset, 0, 0)
        cycle_sum = cycle_sum + moved(0, offset, 0) + moved(0, -offset, 0)
        cycle_sum = cycle_sum + moved(0, 0, offset) + moved(0, 0, -offset)
        total = total + stencil_weights[offset] * cycle_sum
    return total


def pad_sides(field):
    return jnp.pad(field, ((0, 0), (4, 4), (4, 4)))


def inject(field, receivers, values, first_x):
    extent = field.shape[0]
    local_x = receivers[0, 0] - first_x
    valid = (local_x >= 0) & (local_x < extent)
    local_x = jnp.where(valid, local_x, extent)
    return field.at[local_x, receivers[0, 1], receivers[0, 2]].add(values, mode="drop")


def body(wave_now, wave_prev, courant, forward, receivers, residual, aperture, latent, weight):
    slab_cells = courant.shape[0]
    first_x = lax.axis_index("slab") * slab_cells
    current = wave_now[0]
    previous = wave_prev[0]
    accum = jnp.zeros(current.shape, jnp.float32)
    for instant in range(STEPS):
        padded = extended(current, (("slab", 0),), 4)
        advanced = 2.0 * current - previous + courant * laplace(pad_sides(padded))
        advanced = inject(advanced, receivers, residual[0, instant], first_x)
        accum = accum + advanced * forward[0, instant].astype(jnp.float32)
        previous = current
        current = advanced
    x_cells = first_x + jnp.arange(slab_cells, dtype=jnp.int32)
    inside = (x_cells >= aperture[0, 0]) & (x_cells < aperture[0, 1])
    image = jnp.where(inside[:, None, None], courant * accum, 0.0)
    image_rows = image.transpose(1, 0, 2)
    tile_rows = image_rows.shape[0] // lax.axis_size("shot")
    tile = lax.psum_scatter(image_rows, "shot", scatter_dimension=0, tiled=True).transpose(1, 0, 2)
    half_x = slab_cells // 2
    half_y = tile_rows // 2
    half_z = tile.shape[2] // 2
    taps = (
        tile.reshape(half_x, 2, half_y, 2, half_z, 2)
        .transpose(0, 2, 4, 1, 3, 5)
        .reshape(half_x, half_y, half_z, 8)
    )
    channels = weight.shape[0]
    latent_grad = jnp.einsum(
        "ijkq,cq->ijck", taps, weight, precision=lax.Precision.HIGHEST
    ).reshape(half_x, half_y, channels * half_z)
    latent_wide = latent.astype(jnp.float32).reshape(half_x, half_y, channels, half_z)
    partial_grad = jnp.einsum("ijck,ijkq->cq", latent_wide, taps, precision=lax.Precision.HIGHEST)
    latent_cells = (
        latent.shape[0] * lax.axis_size("slab") * latent.shape[1] * lax.axis_size("shot") * half_z
    )
    weight_grad = lax.psum(partial_grad, ("shot", "slab")) * (1.0 / math.sqrt(latent_cells))
    return (current[None], previous[None], latent_grad, weight_grad)


def solution(mesh):
    return jax.shard_map(
        body,
        mesh=mesh,
        in_specs=(
            P("shot", "slab", None, None),
            P("shot", "slab", None, None),
            P("slab", None, None),
            P("shot", None, "slab", None, None),
            P("shot", None, None),
            P("shot", None, None),
            P("shot", None),
            P("slab", "shot", None),
            P(),
        ),
        out_specs=(
            P("shot", "slab", None, None),
            P("shot", "slab", None, None),
            P("slab", "shot", None),
            P(),
        ),
        check_vma=False,
    )
```

profile of v0, /device:TPU:1, one launch (start us, length us, event | category | flops | bytes accessed | tf_op | source)
XLA Modules:
  0.0 334.6 jit_solution(5647150959445888792)
XLA Ops:
  7.2 0.0 copy-start
  7.2 0.0 copy-start.4
  7.2 0.0 reduce-scatter.2.cloned.1.call-start
  7.2 1.1 slice_bitcast_fusion.1
  8.3 8.8 %collective-permute-start = (f32[4,64,128]{2,1,0:T(8,128)S(1)}, f32[4,64,128]{2,1,0:T(8,128)S(1)}, u32[]{:S(2)}, u32[]{:S(2)}) collective-permute-start(f32[4,64,128]{2,1,0:T(8,128)S(1)} %get-tuple-element.24), channel_id=1, source_target_pairs={{1,0},{2,1},{3,2},{4,3},{5,4},{6,5},{7,6},{8,7},{9,8},{10,9},{11,1... | collective-permute-start | bytes 393224 | tf_op jit(solution)/shard_map/ppermute | solution.py:22
  17.1 1.9 collective-permute-start.1
  19.0 0.7 fusion.67
  19.8 0.7 or_select_fusion
  20.5 0.5 collective-permute-done.1
  21.0 0.7 copy-done.6
  21.6 1.6 select_maximum_fusion.4
  23.2 3.7 %fusion.13 = f32[16,64,128]{2,1,0:T(8,128)S(1)} fusion(f32[16,64,128]{2,1,0:T(8,128)S(1)} %copy-done.3, f32[16,64,128]{2,1,0:T(8,128)S(1)} %bitcast.63, f32[4,64,128]{2,1,0:T(8,128)} %copy-done.6, f32[4,64,128]{2,1,0:T(8,128)S(1)} %collective-permute-done, f32[24,72,136]{2,1,0:T(8,128)S(1)} %select_maximum_fusion.4, f32[1,16,64,128]{3,2,1,0:T(8,128)} %param.10), kind=kLoop, calls=%fused_computation.40 | loop fusion | flops 5373952 | bytes 10747904 | tf_op jit(solution)/shard_map/add | solution.py:68
  26.9 15.6 %scatter_fusion = f32[16,64,128]{2,1,0:T(8,128)S(1)} fusion(f32[16,64,128]{2,1,0:T(8,128)S(1)} %fusion.13, s32[256]{0:T(256)S(1)} %bitcast.56, f32[256]{0:T(256)S(1)} %bitcast.69), kind=kCustom, calls=%fused_computation | custom fusion | flops 256 | bytes 6144 | tf_op jit(solution)/shard_map/scatter-add | solution.py:57
  42.5 4.4 %collective-permute-start.3 = (f32[4,64,128]{2,1,0:T(8,128)S(1)}, f32[4,64,128]{2,1,0:T(8,128)S(1)}, u32[]{:S(2)}, u32[]{:S(2)}) collective-permute-start(f32[4,64,128]{2,1,0:T(8,128)S(1)} %get-tuple-element.22), channel_id=1, source_target_pairs={{0,1},{1,2},{2,3},{3,4},{4,5},{5,6},{6,7},{7,8},{8,9},{9,10},{10,1... | collective-permute-start | bytes 393224 | tf_op jit(solution)/shard_map/ppermute | solution.py:19
  46.8 1.9 collective-permute-start.2
  48.8 0.0 collective-permute-done.3
  48.8 0.1 constant_dynamic-update-slice_fusion.1
  48.9 4.2 %collective-permute-done.2 = f32[4,64,128]{2,1,0:T(8,128)S(1)} collective-permute-done((f32[4,64,128]{2,1,0:T(8,128)S(1)}, f32[4,64,128]{2,1,0:T(8,128)S(1)}, u32[]{:S(2)}, u32[]{:S(2)}) %collective-permute-start.2) | collective-permute-done | bytes 131104 | tf_op jit(solution)/shard_map/ppermute | solution.py:22
  53.1 0.5 select_maximum_fusion.2
  53.7 2.1 fusion.46
  55.8 0.0 copy-start.8
  55.8 15.6 %scatter_fusion.1 = f32[16,64,128]{2,1,0:T(8,128)S(1)} fusion(f32[16,64,128]{2,1,0:T(8,128)S(1)} %fusion.46, s32[256]{0:T(256)S(1)} %bitcast.57, f32[256]{0:T(256)S(1)} %bitcast.68), kind=kCustom, calls=%fused_computation.1 | custom fusion | flops 256 | bytes 6144 | tf_op jit(solution)/shard_map/scatter-add | solution.py:57
  71.4 0.0 copy-start.1
  71.4 1.9 collective-permute-start.5
  73.3 0.6 fusion.68
  73.9 1.3 compare_and_fusion
  75.2 2.6 collective-permute-start.4
  77.9 0.1 constant_dynamic-update-slice_fusion.5
  78.0 3.5 %collective-permute-done.4 = f32[4,64,128]{2,1,0:T(8,128)S(1)} collective-permute-done((f32[4,64,128]{2,1,0:T(8,128)S(1)}, f32[4,64,128]{2,1,0:T(8,128)S(1)}, u32[]{:S(2)}, u32[]{:S(2)}) %collective-permute-start.4) | collective-permute-done | bytes 131104 | tf_op jit(solution)/shard_map/ppermute | solution.py:22
  81.5 0.5 select_maximum_fusion
  82.1 2.1 fusion.36
  84.2 0.0 copy-start.5
  84.2 15.6 %scatter_fusion.2 = f32[16,64,128]{2,1,0:T(8,128)S(1)} fusion(f32[16,64,128]{2,1,0:T(8,128)S(1)} %fusion.36, s32[256]{0:T(256)S(1)} %bitcast.58, f32[256]{0:T(256)S(1)} %bitcast.67), kind=kCustom, calls=%fused_computation.2 | custom fusion | flops 256 | bytes 6144 | tf_op jit(solution)/shard_map/scatter-add | solution.py:57
  99.8 0.0 copy-start.2
  99.8 0.0 copy-start.7
  99.8 0.3 fusion.58
  100.1 1.1 copy.23
  101.2 0.0 reduce-scatter.2.cloned.1.call-update
  101.2 0.2 reshape.127
  101.4 118.0 %reduce-scatter.2.cloned.1.call-done = f32[4,16,128]{2,1,0:T(8,128)} async-done(((f32[64,16,128]{2,1,0:T(8,128)}), f32[4,16,128]{2,1,0:T(8,128)}) %reduce-scatter.2.cloned.1.call-update) | async-done | bytes 32784 | tf_op jit(solution)/shard_map/reduce_scatter | solution.py:78
  219.5 2.8 reshape.124
  222.3 0.7 copy.24
  223.0 1.0 convolution_bitcast_fusion
  224.1 0.2 copy.31
  224.3 1.0 reshape.151
  225.2 0.3 convolution_bitcast_fusion.1
  225.5 101.6 %psum.7 = f32[64,8]{0,1:T(8,128)S(1)} all-reduce(f32[64,8]{0,1:T(8,128)S(1)} %convolution_bitcast_fusion.1), channel_id=1, replica_groups=mesh['shot'=16,'slab'=32] {'shot','slab'}, use_global_device_ids=true, to_apply=%region_4.5 | all-reduce | flops 512 | bytes 4096 | tf_op jit(solution)/shard_map/psum | solution.py:96
  327.2 0.6 broadcast_multiply_fusion
  (18 shorter events, 0.1 us)
Async XLA Ops:
  7.2 215.8 %copy-start = (f32[64,8]{0,1:T(8,128)S(1)}, f32[64,8]{0,1:T(8,128)}, u32[]{:S(2)}) copy-start(f32[64,8]{0,1:T(8,128)} %param.17) | copy-start | bytes 6148
  7.2 16.0 %copy-start.4 = (f32[1,16,64,128]{3,2,1,0:T(8,128)S(1)}, f32[1,16,64,128]{3,2,1,0:T(8,128)}, u32[]{:S(2)}) copy-start(f32[1,16,64,128]{3,2,1,0:T(8,128)} %param.9) | copy-start | bytes 1572868
  7.2 16.0 %copy-start.3 = (f32[16,64,128]{2,1,0:T(8,128)S(1)}, f32[16,64,128]{2,1,0:T(8,128)}, u32[]{:S(2)}) copy-start(f32[16,64,128]{2,1,0:T(8,128)} %param.11) | copy-start | bytes 1572868
  7.2 212.3 %reduce-scatter.2.cloned.1.call-start = ((), (), s32[]{:S(2)}) async-start(), calls=%async_computation.1 | async-start | bytes 557056 | tf_op jit(solution)/shard_map/reduce_scatter | solution.py:78
  8.3 12.2 %collective-permute-start = (f32[4,64,128]{2,1,0:T(8,128)S(1)}, f32[4,64,128]{2,1,0:T(8,128)S(1)}, u32[]{:S(2)}, u32[]{:S(2)}) collective-permute-start(f32[4,64,128]{2,1,0:T(8,128)S(1)} %get-tuple-element.24), channel_id=1, source_target_pairs={{1,0},{2,1},{3,2},{4,3},{5,4},{6,5},{7,6},{8,7},{9,8},{10,9},{11,1... | collective-permute-start | bytes 393224 | tf_op jit(solution)/shard_map/ppermute | solution.py:22
  17.1 3.9 %collective-permute-start.1 = (f32[4,64,128]{2,1,0:T(8,128)S(1)}, f32[4,64,128]{2,1,0:T(8,128)S(1)}, u32[]{:S(2)}, u32[]{:S(2)}) collective-permute-start(f32[4,64,128]{2,1,0:T(8,128)S(1)} %get-tuple-element.25), channel_id=1, source_target_pairs={{0,1},{1,2},{2,3},{3,4},{4,5},{5,6},{6,7},{7,8},{8,9},{9,10},{10,1... | collective-permute-start | bytes 393224 | tf_op jit(solution)/shard_map/ppermute | solution.py:19
  21.0 0.7 copy-start.6
  42.5 6.3 %collective-permute-start.3 = (f32[4,64,128]{2,1,0:T(8,128)S(1)}, f32[4,64,128]{2,1,0:T(8,128)S(1)}, u32[]{:S(2)}, u32[]{:S(2)}) collective-permute-start(f32[4,64,128]{2,1,0:T(8,128)S(1)} %get-tuple-element.22), channel_id=1, source_target_pairs={{0,1},{1,2},{2,3},{3,4},{4,5},{5,6},{6,7},{7,8},{8,9},{9,10},{10,1... | collective-permute-start | bytes 393224 | tf_op jit(solution)/shard_map/ppermute | solution.py:19
  46.8 6.3 %collective-permute-start.2 = (f32[4,64,128]{2,1,0:T(8,128)S(1)}, f32[4,64,128]{2,1,0:T(8,128)S(1)}, u32[]{:S(2)}, u32[]{:S(2)}) collective-permute-start(f32[4,64,128]{2,1,0:T(8,128)S(1)} %get-tuple-element.23), channel_id=1, source_target_pairs={{1,0},{2,1},{3,2},{4,3},{5,4},{6,5},{7,6},{8,7},{9,8},{10,9},{11,1... | collective-permute-start | bytes 393224 | tf_op jit(solution)/shard_map/ppermute | solution.py:22
  55.8 17.5 %copy-start.8 = (s32[1,2]{1,0:T(1,128)S(1)}, s32[1,2]{1,0:T(1,128)}, u32[]{:S(2)}) copy-start(s32[1,2]{1,0:T(1,128)} %param.15) | copy-start | bytes 28
  71.4 28.4 %copy-start.1 = (f32[16,64,128]{2,1,0:T(8,128)}, f32[16,64,128]{2,1,0:T(8,128)S(1)}, u32[]{:S(2)}) copy-start(f32[16,64,128]{2,1,0:T(8,128)S(1)} %scatter_fusion.1) | copy-start | bytes 1572868
  71.4 6.4 %collective-permute-start.5 = (f32[4,64,128]{2,1,0:T(8,128)S(1)}, f32[4,64,128]{2,1,0:T(8,128)S(1)}, u32[]{:S(2)}, u32[]{:S(2)}) collective-permute-start(f32[4,64,128]{2,1,0:T(8,128)S(1)} %get-tuple-element.18), channel_id=1, source_target_pairs={{0,1},{1,2},{2,3},{3,4},{4,5},{5,6},{6,7},{7,8},{8,9},{9,10},{10,1... | collective-permute-start | bytes 393224 | tf_op jit(solution)/shard_map/ppermute | solution.py:19
  75.2 6.3 %collective-permute-start.4 = (f32[4,64,128]{2,1,0:T(8,128)S(1)}, f32[4,64,128]{2,1,0:T(8,128)S(1)}, u32[]{:S(2)}, u32[]{:S(2)}) collective-permute-start(f32[4,64,128]{2,1,0:T(8,128)S(1)} %get-tuple-element.19), channel_id=1, source_target_pairs={{1,0},{2,1},{3,2},{4,3},{5,4},{6,5},{7,6},{8,7},{9,8},{10,9},{11,1... | collective-permute-start | bytes 393224 | tf_op jit(solution)/shard_map/ppermute | solution.py:22
  84.2 15.6 %copy-start.5 = (bf16[1,3,16,64,128]{4,3,2,1,0:T(8,128)(2,1)S(1)}, bf16[1,3,16,64,128]{4,3,2,1,0:T(8,128)(2,1)}, u32[]{:S(2)}) copy-start(bf16[1,3,16,64,128]{4,3,2,1,0:T(8,128)(2,1)} %param.12) | copy-start | bytes 2359300
  99.8 1.4 copy-start.2
  99.8 1.4 copy-start.7
Sparse Core Ops, SparseCore 0:
  101.3 118.1 reduce-scatter.1
where the time goes:
time: 335 us
  waiting for transfers between devices  126 us (38%)
  blocking collectives  102 us (30%)
  other arithmetic  60 us (18%)
  starting transfers between devices  21.5 us (6%)
  between operations  14.4 us (4%)
  local copies, waits for them, and re-layouts  9.37 us (3%)
    reduce_scatter x1, waiting for transfers between devices, body(): lax.psum_scatter(image_rows, 'shot', scatter_dimension=0, tiled=True)  118 us
    psum x1, blocking collectives, body(): lax.psum(partial_grad, ('shot', 'slab')) * (1.0 / math.sqrt(latent_cells))  102 us
    scatter-add x3, other arithmetic, inject(): field.at[local_x, receivers[0, 1], receivers[0, 2]].add(values, mode='drop')  46.6 us
    ppermute x3, starting transfers between devices, extended(): lax.ppermute(lax.slice_in_dim(block, 0, width, axis=dim), axis, backward)  13.3 us
    ppermute x3, starting transfers between devices, extended(): lax.ppermute(lax.slice_in_dim(block, block.shape[dim] - width, None, axis...  8.21 us
    add x3, other arithmetic, body(): advanced = 2.0 * current - previous + courant * laplace(pad_sides(padded))  7.87 us
    ppermute x3, waiting for transfers between devices, extended(): lax.ppermute(lax.slice_in_dim(block, 0, width, axis=dim), axis, backward)  7.76 us
  transfers between devices with their start and end apart: 7, of which 4 were waited for; matrix products, arithmetic and copies ran while one was open for 1% of the time, Pallas kernels for 0%

commit v1 on v0

v1 whole, which is shorter than its diff:
```python
import math

import jax
import jax.numpy as jnp
from jax import lax
from jax.sharding import Mesh, PartitionSpec as P

STEPS = 3
PARTS = ("zh", "y", "zl", "x", "c")
SHOT = ("zh", "y")
SLAB = ("zl", "x", "c")


stencil_weights = (-205.0 / 72.0, 8.0 / 5.0, -1.0 / 5.0, 8.0 / 315.0, -1.0 / 560.0)


def extended(block, axis, dim, width):
    count = lax.axis_size(axis)
    forward = [(i, i + 1) for i in range(count - 1)]
    backward = [(target, source) for source, target in forward]
    low = lax.ppermute(
        lax.slice_in_dim(block, block.shape[dim] - width, None, axis=dim), axis, forward
    )
    high = lax.ppermute(lax.slice_in_dim(block, 0, width, axis=dim), axis, backward)
    return jnp.concatenate([low, block, high], axis=dim)


def laplace(padded):
    size_x = padded.shape[0] - 8
    size_y = padded.shape[1] - 8
    size_z = padded.shape[2] - 8

    def moved(shift_x, shift_y, shift_z):
        return padded[
            4 + shift_x : 4 + shift_x + size_x,
            4 + shift_y : 4 + shift_y + size_y,
            4 + shift_z : 4 + shift_z + size_z,
        ]

    total = 3.0 * stencil_weights[0] * moved(0, 0, 0)
    for offset in range(1, 5):
        cycle_sum = moved(offset, 0, 0) + moved(-offset, 0, 0)
        cycle_sum = cycle_sum + moved(0, offset, 0) + moved(0, -offset, 0)
        cycle_sum = cycle_sum + moved(0, 0, offset) + moved(0, 0, -offset)
        total = total + stencil_weights[offset] * cycle_sum
    return total


def pad_sides(field):
    return jnp.pad(field, ((0, 0), (4, 4), (4, 4)))


def injections(receivers, residual, first_x, extent, size_y, size_z):
    local_x = receivers[0, 0] - first_x
    valid = (local_x >= 0) & (local_x < extent)
    row = jnp.where(valid, local_x * size_y + receivers[0, 1], -1)
    rows = (row[None, :] == jnp.arange(extent * size_y, dtype=jnp.int32)[:, None]).astype(jnp.float32)
    cols = (receivers[0, 2][:, None] == jnp.arange(size_z, dtype=jnp.int32)[None, :]).astype(jnp.float32)
    spread = residual[0][:, :, None] * cols[None]
    out = jnp.einsum("mr,trz->tmz", rows, spread, precision=lax.Precision.HIGHEST)
    return out.reshape(STEPS, extent, size_y, size_z)


def scatter_sum(chunks, axis):
    return lax.all_to_all(chunks, axis, 0, 0, tiled=True).sum(0)


def share_sum(block, axis):
    count = lax.axis_size(axis)
    wide = jnp.broadcast_to(block[None], (count,) + block.shape)
    return lax.all_to_all(wide, axis, 0, 0, tiled=True).sum(0)


def body(wave_now, wave_prev, courant, forward, receivers, residual, aperture, latent, weight):
    slab_cells = courant.shape[0]
    first_x = lax.axis_index(SLAB) * slab_cells
    current = wave_now[0]
    previous = wave_prev[0]
    added = injections(receivers, residual, first_x, *current.shape)
    accum = jnp.zeros(current.shape, jnp.float32)
    for instant in range(STEPS):
        padded = extended(current, SLAB, 0, 4)
        advanced = 2.0 * current - previous + courant * laplace(pad_sides(padded)) + added[instant]
        accum = accum + advanced * forward[0, instant].astype(jnp.float32)
        previous = current
        current = advanced
    x_cells = first_x + jnp.arange(slab_cells, dtype=jnp.int32)
    inside = (x_cells >= aperture[0, 0]) & (x_cells < aperture[0, 1])
    image = jnp.where(inside[:, None, None], courant * accum, 0.0)
    far, near = lax.axis_size("zh"), lax.axis_size("y")
    tile_rows = image.shape[1] // (far * near)
    rows = image.reshape(slab_cells, far, near, tile_rows, image.shape[2]).transpose(2, 1, 3, 0, 4)
    tile = scatter_sum(scatter_sum(rows, "y"), "zh").transpose(1, 0, 2)
    half_x = slab_cells // 2
    half_y = tile_rows // 2
    half_z = tile.shape[2] // 2
    taps = (
        tile.reshape(half_x, 2, half_y, 2, half_z, 2)
        .transpose(0, 2, 4, 1, 3, 5)
        .reshape(half_x, half_y, half_z, 8)
    )
    channels = weight.shape[0]
    latent_grad = jnp.einsum(
        "ijkq,cq->ijck", taps, weight, precision=lax.Precision.HIGHEST
    ).reshape(half_x, half_y, channels * half_z)
    latent_wide = latent.astype(jnp.float32).reshape(half_x, half_y, channels, half_z)
    partial_grad = jnp.einsum("ijck,ijkq->cq", latent_wide, taps, precision=lax.Precision.HIGHEST)
    latent_cells = (
        latent.shape[0] * lax.axis_size(SLAB) * latent.shape[1] * lax.axis_size(SHOT) * half_z
    )
    total_grad = share_sum(share_sum(partial_grad, ("zh", "zl")), ("y", "x", "c"))
    weight_grad = total_grad * (1.0 / math.sqrt(latent_cells))
    return (current[None], previous[None], latent_grad, weight_grad)


def solution(mesh):
    fine = Mesh(mesh.devices.reshape(4, 4, 4, 4, 2), PARTS)
    return jax.shard_map(
        body,
        mesh=fine,
        in_specs=(
            P(SHOT, SLAB, None, None),
            P(SHOT, SLAB, None, None),
            P(SLAB, None, None),
            P(SHOT, None, SLAB, None, None),
            P(SHOT, None, None),
            P(SHOT, None, None),
            P(SHOT, None),
            P(SLAB, SHOT, None),
            P(),
        ),
        out_specs=(
            P(SHOT, SLAB, None, None),
            P(SHOT, SLAB, None, None),
            P(SLAB, SHOT, None),
            P(),
        ),
        check_vma=False,
    )
```

time: 335 us -> 126 us (0.38)
  waiting for transfers between devices: 126 us -> 19.6 us
  blocking collectives: 102 us -> 29.2 us
  other arithmetic: 60 us -> 14.6 us
  starting transfers between devices: 21.5 us -> 47 us
  between operations: 14.4 us -> 1.01 us
    reduce_scatter x1 -> x0, waiting for transfers between devices: 118 us -> none  [body(): lax.psum_scatter(image_rows, 'shot', scatter_dimension=0, tiled=True)]
    psum x1 -> x0, blocking collectives: 102 us -> none  [body(): lax.psum(partial_grad, ('shot', 'slab')) * (1.0 / math.sqrt(latent_cells))]
    scatter-add x3 -> x0, other arithmetic: 46.6 us -> none  [inject(): field.at[local_x, receivers[0, 1], receivers[0, 2]].add(values, mode='drop')]
    all_to_all x0 -> x2, blocking collectives: none -> 29.2 us  [the longest x1 18.5 us: share_sum(): return lax.all_to_all(wide, axis, 0, 0, tiled=True).sum(0)]
    all_to_all x0 -> x2, starting transfers between devices: none -> 24.5 us  [the longest x1 12.4 us: scatter_sum(): return lax.all_to_all(chunks, axis, 0, 0, tiled=True).sum(0)]
    all_to_all x0 -> x2, waiting for transfers between devices: none -> 17.8 us  [the longest x1 12.6 us: scatter_sum(): return lax.all_to_all(chunks, axis, 0, 0, tiled=True).sum(0)]
    ppermute x3, waiting for transfers between devices: 7.76 us -> 0.73 us  [extended(): lax.ppermute(lax.slice_in_dim(block, 0, width, axis=dim), axis, backward)]
    select_n x0 -> x1, other arithmetic: none -> 3.48 us  [body(): image = jnp.where(inside[:, None, None], courant * accum, 0.0)]
  transfers between devices with their start and end apart: 7 -> 8, of which waited for: 4 -> 4; matrix products, arithmetic and copies ran while one was open for 1% -> 6% of each run, Pallas kernels for 0% -> 0%
where the time goes in v1:
time: 126 us; the launch traced here: 125 us
  starting transfers between devices  47 us (37%)
  blocking collectives  29.2 us (23%)
  waiting for transfers between devices  19.6 us (16%)
  other arithmetic  14.6 us (12%)
  local copies, waits for them, and re-layouts  11.5 us (9%)
  matrix products  2.21 us (2%)
    all_to_all x1, blocking collectives, share_sum(): return lax.all_to_all(wide, axis, 0, 0, tiled=True).sum(0)  18.5 us
    ppermute x3, starting transfers between devices, extended(): lax.ppermute(lax.slice_in_dim(block, 0, width, axis=dim), axis, backward)  13.1 us
    all_to_all x1, waiting for transfers between devices, scatter_sum(): return lax.all_to_all(chunks, axis, 0, 0, tiled=True).sum(0)  12.6 us
    all_to_all x1, starting transfers between devices, scatter_sum(): return lax.all_to_all(chunks, axis, 0, 0, tiled=True).sum(0)  12.4 us
    all_to_all x1, starting transfers between devices, share_sum(): return lax.all_to_all(wide, axis, 0, 0, tiled=True).sum(0)  12.1 us
    all_to_all x1, blocking collectives, scatter_sum(): return lax.all_to_all(chunks, axis, 0, 0, tiled=True).sum(0)  10.7 us
    ppermute x3, starting transfers between devices, extended(): lax.ppermute(lax.slice_in_dim(block, block.shape[dim] - width, None, axis...  9.43 us
    all_to_all x1, waiting for transfers between devices, share_sum(): return lax.all_to_all(wide, axis, 0, 0, tiled=True).sum(0)  5.23 us
  transfers between devices with their start and end apart: 8, of which 4 were waited for; matrix products, arithmetic and copies ran while one was open for 6% of the time, Pallas kernels for 0%

profile of v1, /device:TPU:1, one launch (start us, length us, event | category | flops | bytes accessed | tf_op | source)
XLA Modules:
  0.0 125.1 jit_solution(3612171145473229165)
XLA Ops:
  0.6 1.6 %slice_bitcast_fusion.1 = (f32[4,64,128]{2,1,0:T(8,128)}, f32[4,64,128]{2,1,0:T(8,128)S(1)}) fusion(f32[1,16,64,128]{3,2,1,0:T(8,128)} %param.9), kind=kLoop, calls=%fused_computation.186 | loop fusion | bytes 524288 | tf_op jit(solution)/shard_map/slice | solution.py:24
  2.3 8.8 %collective-permute-start = (f32[4,64,128]{2,1,0:T(8,128)}, f32[4,64,128]{2,1,0:T(8,128)S(1)}, u32[]{:S(2)}, u32[]{:S(2)}) collective-permute-start(f32[4,64,128]{2,1,0:T(8,128)} %get-tuple-element.29), channel_id=1, source_target_pairs={{1,0},{2,1},{3,2},{4,3},{5,4},{6,5},{7,6},{8,7},{9,8},{10,9},{11,1... | collective-permute-start | bytes 393224 | tf_op jit(solution)/shard_map/ppermute | solution.py:24
  11.1 1.9 %collective-permute-start.1 = (f32[4,64,128]{2,1,0:T(8,128)S(1)}, f32[4,64,128]{2,1,0:T(8,128)S(1)}, u32[]{:S(2)}, u32[]{:S(2)}) collective-permute-start(f32[4,64,128]{2,1,0:T(8,128)S(1)} %get-tuple-element.30), channel_id=1, source_target_pairs={{0,1},{1,2},{2,3},{3,4},{4,5},{5,6},{6,7},{7,8},{8,9},{9,10},{10,1... | collective-permute-start | bytes 393224 | tf_op jit(solution)/shard_map/ppermute | solution.py:21
  13.0 0.7 fusion.120
  13.8 0.7 copy.69
  14.4 0.9 convolution_bitcast_fusion
  15.3 0.2 fusion.117
  15.5 0.2 copy.42
  15.8 0.6 copy-done.1
  16.4 0.5 select_maximum_fusion.4
  16.9 2.6 %fusion.78 = f32[16,64,128]{2,1,0:T(8,128)S(1)} fusion(f32[16,64,128]{2,1,0:T(8,128)S(1)} %bitcast.74, f32[16,64,128]{2,1,0:T(8,128)S(1)} %copy-done.3, f32[16,64,128]{2,1,0:T(8,128)S(1)} %bitcast.71, f32[4,64,128]{2,1,0:T(8,128)S(1)} %collective-permute-done.1, f32[4,64,128]{2,1,0:T(8,128)S(1)} %collective-permute-done, ...), kind=kLoop, calls=%fused_computation.127 | loop fusion | flops 5505024 | bytes 11272192 | tf_op jit(solution)/shard_map/add | solution.py:83
  19.5 0.7 fusion.119
  20.2 2.4 %collective-permute-start.2 = (f32[4,64,128]{2,1,0:T(8,128)}, f32[4,64,128]{2,1,0:T(8,128)S(1)}, u32[]{:S(2)}, u32[]{:S(2)}) collective-permute-start(f32[4,64,128]{2,1,0:T(8,128)} %get-tuple-element.27), channel_id=1, source_target_pairs={{1,0},{2,1},{3,2},{4,3},{5,4},{6,5},{7,6},{8,7},{9,8},{10,9},{11,1... | collective-permute-start | bytes 393224 | tf_op jit(solution)/shard_map/ppermute | solution.py:24
  22.6 3.2 %collective-permute-start.3 = (f32[4,64,128]{2,1,0:T(8,128)S(1)}, f32[4,64,128]{2,1,0:T(8,128)S(1)}, u32[]{:S(2)}, u32[]{:S(2)}) collective-permute-start(f32[4,64,128]{2,1,0:T(8,128)S(1)} %get-tuple-element.28), channel_id=1, source_target_pairs={{0,1},{1,2},{2,3},{3,4},{4,5},{5,6},{6,7},{7,8},{8,9},{9,10},{10,1... | collective-permute-start | bytes 393224 | tf_op jit(solution)/shard_map/ppermute | solution.py:21
  25.7 0.2 copy.43
  25.9 0.7 collective-permute-done.2
  26.7 1.0 collective-permute-done.3
  27.7 0.5 select_maximum_fusion.2
  28.2 2.6 %fusion.47 = f32[16,64,128]{2,1,0:T(8,128)S(1)} fusion(f32[16,64,128]{2,1,0:T(8,128)S(1)} %bitcast.75, f32[16,64,128]{2,1,0:T(8,128)S(1)} %copy-done.3, f32[16,64,128]{2,1,0:T(8,128)S(1)} %fusion.78, f32[4,64,128]{2,1,0:T(8,128)S(1)} %collective-permute-done.3, f32[4,64,128]{2,1,0:T(8,128)S(1)} %collective-permute-done.2, ...), kind=kLoop, calls=%fused_computation.96 | loop fusion | flops 5505024 | bytes 11272192 | tf_op jit(solution)/shard_map/add | solution.py:83
  30.8 1.9 %collective-permute-start.4 = (f32[4,64,128]{2,1,0:T(8,128)S(1)}, f32[4,64,128]{2,1,0:T(8,128)S(1)}, u32[]{:S(2)}, u32[]{:S(2)}) collective-permute-start(f32[4,64,128]{2,1,0:T(8,128)S(1)} %get-tuple-element.26), channel_id=1, source_target_pairs={{1,0},{2,1},{3,2},{4,3},{5,4},{6,5},{7,6},{8,7},{9,8},{10,9},{11,1... | collective-permute-start | bytes 393224 | tf_op jit(solution)/shard_map/ppermute | solution.py:24
  32.8 4.4 %collective-permute-start.5 = (f32[4,64,128]{2,1,0:T(8,128)S(1)}, f32[4,64,128]{2,1,0:T(8,128)S(1)}, u32[]{:S(2)}, u32[]{:S(2)}) collective-permute-start(f32[4,64,128]{2,1,0:T(8,128)S(1)} %get-tuple-element.25), channel_id=1, source_target_pairs={{0,1},{1,2},{2,3},{3,4},{4,5},{5,6},{6,7},{7,8},{8,9},{9,10},{10,1... | collective-permute-start | bytes 393224 | tf_op jit(solution)/shard_map/ppermute | solution.py:21
  37.1 0.6 fusion.121
  37.7 0.2 copy.44
  37.9 1.4 %compare_and_fusion = pred[16]{0:T(512)(128)(4,1)S(1)} fusion(s32[]{:T(128)} %bitcast.14, s32[]{:T(128)} %bitcast.13, s32[]{:T(128)S(6)} %mul.129), kind=kLoop, calls=%fused_computation.194 | loop fusion | flops 64 | bytes 28 | tf_op jit(solution)/shard_map/and | solution.py:88
  39.3 0.5 select_maximum_fusion
  39.9 3.5 %fusion.106 = (f32[16,64,128]{2,1,0:T(8,128)S(1)}, f32[16,64,128]{2,1,0:T(8,128)}) fusion(f32[16,64,128]{2,1,0:T(8,128)S(1)} %copy-done.3, f32[16,64,128]{2,1,0:T(8,128)S(1)} %fusion.47, f32[16,64,128]{2,1,0:T(8,128)S(1)} %fusion.78, bf16[1,3,16,64,128]{4,3,2,1,0:T(8,128)(2,1)S(1)} %copy-done.4, pred[16]{0:T(512)(128)(4,1)S(1)} %compare_and_fusion, ...), kind=kLoop, calls=%fused_computation.174 | loop fusion | flops 6815744 | bytes 12582928 | tf_op jit(solution)/shard_map/jit(_where)/select_n | solution.py:89
  43.4 0.1 copy.68
  43.5 10.7 %all_to_all.20 = f32[4,4,4,16,128]{4,2,1,3,0:T(4,128)S(1)} all-to-all(f32[4,4,4,16,128]{4,2,1,3,0:T(4,128)S(1)} %bitcast.77), channel_id=1, replica_groups=mesh['zh'=4,'y'=4,'zl'=4,'x'=4,'c'=2] {'y'}, dimensions={0} | all-to-all | bytes 1048576 | tf_op jit(solution)/shard_map/all_to_all | solution.py:65
  54.1 0.1 reduce_sum.36
  54.3 0.7 copy.47
  54.9 12.4 %all-to-all-start.1 = ((f32[4,4,16,128]{3,1,2,0:T(4,128)}), f32[4,4,16,128]{3,1,2,0:T(4,128)S(1)}, u32[]{:S(2)}, u32[]{:S(2)}) async-start(f32[4,4,16,128]{3,1,2,0:T(4,128)} %copy.47), calls=%async_computation.1 | async-start | bytes 262144 | tf_op jit(solution)/shard_map/all_to_all | solution.py:65
  67.3 0.2 reshape.101
  67.5 12.6 %all-to-all-done.1 = f32[4,4,16,128]{3,1,2,0:T(4,128)S(1)} async-done(((f32[4,4,16,128]{3,1,2,0:T(4,128)}), f32[4,4,16,128]{3,1,2,0:T(4,128)S(1)}, u32[]{:S(2)}, u32[]{:S(2)}) %all-to-all-start.1) | async-done | bytes 131104 | tf_op jit(solution)/shard_map/all_to_all | solution.py:65
  80.2 2.1 %reshape.98 = f32[8,2,2,2,64,2]{5,4,1,0,3,2:T(8,128)S(1)} reshape(f32[16,4,128]{2,0,1:T(8,128)S(1)} %copy.49) | data formatting | bytes 65536 | tf_op jit(solution)/shard_map/reshape | solution.py:98
  82.3 0.7 copy.50
  83.0 0.3 convolution_bitcast_fusion.2
  83.3 0.1 reshape.109
  83.4 18.5 %all_to_all.21 = f32[16,1,512]{2,1,0:T(1,128)S(1)} all-to-all(f32[16,1,512]{2,1,0:T(1,128)S(1)} %reshape.109), channel_id=1, replica_groups=mesh['zh'=4,'y'=4,'zl'=4,'x'=4,'c'=2] {'zh','zl'}, dimensions={0} | all-to-all | bytes 65536 | tf_op jit(solution)/shard_map/all_to_all | solution.py:71
  101.9 0.5 broadcast.173
  102.4 0.7 reduce
  103.3 0.7 reshape.111
  104.0 12.1 %all-to-all-start.3 = ((f32[32,1,512]{2,1,0:T(1,128)}), f32[32,1,512]{2,1,0:T(1,128)S(1)}, u32[]{:S(2)}, u32[]{:S(2)}) async-start(f32[32,1,512]{2,1,0:T(1,128)} %reshape.111), calls=%async_computation.3 | async-start | bytes 131072 | tf_op jit(solution)/shard_map/all_to_all | solution.py:71
  116.1 1.0 convolution_bitcast_fusion.1
  117.2 0.2 copy.57
  117.4 1.0 reshape.108
  118.3 5.2 %all-to-all-done.3 = f32[32,1,512]{2,1,0:T(1,128)S(1)} async-done(((f32[32,1,512]{2,1,0:T(1,128)}), f32[32,1,512]{2,1,0:T(1,128)S(1)}, u32[]{:S(2)}, u32[]{:S(2)}) %all-to-all-start.3) | async-done | bytes 65568 | tf_op jit(solution)/shard_map/all_to_all | solution.py:71
  123.6 0.8 reduce.1
  124.5 0.6 broadcast_multiply_fusion
  (29 shorter events, 0.4 us)
Async XLA Ops:
  0.6 115.5 %copy-start = (f32[64,8]{0,1:T(8,128)S(1)}, f32[64,8]{0,1:T(8,128)}, u32[]{:S(2)}) copy-start(f32[64,8]{0,1:T(8,128)} %param.17) | copy-start | bytes 6148
  2.3 13.4 %collective-permute-start = (f32[4,64,128]{2,1,0:T(8,128)}, f32[4,64,128]{2,1,0:T(8,128)S(1)}, u32[]{:S(2)}, u32[]{:S(2)}) collective-permute-start(f32[4,64,128]{2,1,0:T(8,128)} %get-tuple-element.29), channel_id=1, source_target_pairs={{1,0},{2,1},{3,2},{4,3},{5,4},{6,5},{7,6},{8,7},{9,8},{10,9},{11,1... | collective-permute-start | bytes 393224 | tf_op jit(solution)/shard_map/ppermute | solution.py:24
  11.1 4.7 %collective-permute-start.1 = (f32[4,64,128]{2,1,0:T(8,128)S(1)}, f32[4,64,128]{2,1,0:T(8,128)S(1)}, u32[]{:S(2)}, u32[]{:S(2)}) collective-permute-start(f32[4,64,128]{2,1,0:T(8,128)S(1)} %get-tuple-element.30), channel_id=1, source_target_pairs={{0,1},{1,2},{2,3},{3,4},{4,5},{5,6},{6,7},{7,8},{8,9},{9,10},{10,1... | collective-permute-start | bytes 393224 | tf_op jit(solution)/shard_map/ppermute | solution.py:21
  15.3 1.0 copy-start.1
  15.5 1.4 %copy-start.3 = (f32[16,64,128]{2,1,0:T(8,128)S(1)}, f32[16,64,128]{2,1,0:T(8,128)}, u32[]{:S(2)}) copy-start(f32[16,64,128]{2,1,0:T(8,128)} %param.11) | copy-start | bytes 1572868
  15.7 1.2 copy-start.5
  20.2 6.5 %collective-permute-start.2 = (f32[4,64,128]{2,1,0:T(8,128)}, f32[4,64,128]{2,1,0:T(8,128)S(1)}, u32[]{:S(2)}, u32[]{:S(2)}) collective-permute-start(f32[4,64,128]{2,1,0:T(8,128)} %get-tuple-element.27), channel_id=1, source_target_pairs={{1,0},{2,1},{3,2},{4,3},{5,4},{6,5},{7,6},{8,7},{9,8},{10,9},{11,1... | collective-permute-start | bytes 393224 | tf_op jit(solution)/shard_map/ppermute | solution.py:24
  22.6 5.1 %collective-permute-start.3 = (f32[4,64,128]{2,1,0:T(8,128)S(1)}, f32[4,64,128]{2,1,0:T(8,128)S(1)}, u32[]{:S(2)}, u32[]{:S(2)}) collective-permute-start(f32[4,64,128]{2,1,0:T(8,128)S(1)} %get-tuple-element.28), channel_id=1, source_target_pairs={{0,1},{1,2},{2,3},{3,4},{4,5},{5,6},{6,7},{7,8},{8,9},{9,10},{10,1... | collective-permute-start | bytes 393224 | tf_op jit(solution)/shard_map/ppermute | solution.py:21
  28.2 8.9 %copy-start.7 = (s32[1,2]{1,0:T(1,128)S(1)}, s32[1,2]{1,0:T(1,128)}, u32[]{:S(2)}) copy-start(s32[1,2]{1,0:T(1,128)} %param.15) | copy-start | bytes 28
  30.8 9.1 %copy-start.2 = (f32[16,64,128]{2,1,0:T(8,128)}, f32[16,64,128]{2,1,0:T(8,128)S(1)}, u32[]{:S(2)}) copy-start(f32[16,64,128]{2,1,0:T(8,128)S(1)} %fusion.47) | copy-start | bytes 1572868
  30.8 8.5 %collective-permute-start.4 = (f32[4,64,128]{2,1,0:T(8,128)S(1)}, f32[4,64,128]{2,1,0:T(8,128)S(1)}, u32[]{:S(2)}, u32[]{:S(2)}) collective-permute-start(f32[4,64,128]{2,1,0:T(8,128)S(1)} %get-tuple-element.26), channel_id=1, source_target_pairs={{1,0},{2,1},{3,2},{4,3},{5,4},{6,5},{7,6},{8,7},{9,8},{10,9},{11,1... | collective-permute-start | bytes 393224 | tf_op jit(solution)/shard_map/ppermute | solution.py:24
  32.8 6.6 %collective-permute-start.5 = (f32[4,64,128]{2,1,0:T(8,128)S(1)}, f32[4,64,128]{2,1,0:T(8,128)S(1)}, u32[]{:S(2)}, u32[]{:S(2)}) collective-permute-start(f32[4,64,128]{2,1,0:T(8,128)S(1)} %get-tuple-element.25), channel_id=1, source_target_pairs={{0,1},{1,2},{2,3},{3,4},{4,5},{5,6},{6,7},{7,8},{8,9},{9,10},{10,1... | collective-permute-start | bytes 393224 | tf_op jit(solution)/shard_map/ppermute | solution.py:21
  37.9 2.0 %copy-start.4 = (bf16[1,3,16,64,128]{4,3,2,1,0:T(8,128)(2,1)S(1)}, bf16[1,3,16,64,128]{4,3,2,1,0:T(8,128)(2,1)}, u32[]{:S(2)}) copy-start(bf16[1,3,16,64,128]{4,3,2,1,0:T(8,128)(2,1)} %param.12) | copy-start | bytes 2359300
  43.4 24.0 %copy-start.6 = (bf16[8,2,4096]{2,1,0:T(2,128)(2,1)S(1)}, bf16[8,2,4096]{2,1,0:T(2,128)(2,1)}, u32[]{:S(2)}) copy-start(bf16[8,2,4096]{2,1,0:T(2,128)(2,1)} %param.16) | copy-start | bytes 393220
  54.9 25.2 %all-to-all-start.1 = ((f32[4,4,16,128]{3,1,2,0:T(4,128)}), f32[4,4,16,128]{3,1,2,0:T(4,128)S(1)}, u32[]{:S(2)}, u32[]{:S(2)}) async-start(f32[4,4,16,128]{3,1,2,0:T(4,128)} %copy.47), calls=%async_computation.1 | async-start | bytes 262144 | tf_op jit(solution)/shard_map/all_to_all | solution.py:65
  104.0 19.5 %all-to-all-start.3 = ((f32[32,1,512]{2,1,0:T(1,128)}), f32[32,1,512]{2,1,0:T(1,128)S(1)}, u32[]{:S(2)}, u32[]{:S(2)}) async-start(f32[32,1,512]{2,1,0:T(1,128)} %reshape.111), calls=%async_computation.3 | async-start | bytes 131072 | tf_op jit(solution)/shard_map/all_to_all | solution.py:71

commit v2 on v1

v2 whole, which is shorter than its diff:
```python
import math

import jax
import jax.numpy as jnp
import numpy as np
from jax import lax
from jax.experimental import pallas as pl
from jax.experimental.pallas import tpu as pltpu
from jax.sharding import Mesh, PartitionSpec as P

STEPS = 3
PARTS = ("zh", "y", "zl", "x", "c")
SHOT = ("zh", "y")
SLAB = ("zl", "x", "c")
EXT = 16
NY = 64
NZ = 128
F32 = jnp.float32
BF16 = jnp.bfloat16

stencil_weights = (-205.0 / 72.0, 8.0 / 5.0, -1.0 / 5.0, 8.0 / 315.0, -1.0 / 560.0)


def high_low(values):
    high = values.astype(BF16)
    return high, (values - high.astype(np.float32)).astype(BF16)


def band(size, center):
    out = np.zeros((size, size), np.float32)
    for k in range(5):
        for i in range(size - k):
            value = center if k == 0 else stencil_weights[k]
            out[i, i + k] = value
            out[i + k, i] = value
    return out


def constants():
    zh, zl = high_low(band(NZ, 3.0 * stencil_weights[0]))
    yh, yl = high_low(band(NY, 0.0))
    along_z = np.concatenate([zh, zh, zl], axis=0)
    along_y = np.concatenate([yh, yh, yl], axis=1)
    spread = np.zeros((NZ, 2, 2, 2, NZ // 2), np.float32)
    for k in range(NZ // 2):
        for c in range(2):
            for h in range(2):
                spread[2 * k + c, h, c, h, k] = 1.0
    spread = spread.reshape(NZ, 4 * NZ).astype(BF16)
    place = np.zeros((2, 64, 128), np.float32)
    for h in range(2):
        for j in range(2):
            for t in range(32):
                place[h, 32 * j + t, 2 * t + h] = 1.0
    pick = np.zeros((8, 32), np.float32)
    for row in range(32):
        c, a, b = (row >> 3) & 1, (row >> 2) & 1, row & 1
        pick[4 * a + 2 * b + c, row] = 1.0
    return along_z, along_y, spread, place, pick


ALONG_Z, ALONG_Y, SPREAD, PLACE, PICK = constants()


def flat_laplace(u, along_z, along_y):
    high = u.astype(BF16)
    low = (u - high.astype(F32)).astype(BF16)
    rows_h, rows_l = high.reshape(2 * NY, NZ), low.reshape(2 * NY, NZ)
    z_part = jnp.dot(
        jnp.concatenate([rows_h, rows_l, rows_h], axis=1), along_z, preferred_element_type=F32
    )
    wide_h = jnp.concatenate([high[0], high[1]], axis=1)
    wide_l = jnp.concatenate([low[0], low[1]], axis=1)
    y_part = jnp.dot(
        along_y, jnp.concatenate([wide_h, wide_l, wide_h], axis=0), preferred_element_type=F32
    )
    z_part = z_part.reshape(2, NY, NZ)
    return z_part[0] + y_part[:, :NZ], z_part[1] + y_part[:, NZ:]


def across(ref, at):
    total = stencil_weights[1] * (ref[at + 1] + ref[at - 1])
    for k in range(2, 5):
        total = total + stencil_weights[k] * (ref[at + k] + ref[at - k])
    return total


def three_parts(v):
    high = v.astype(BF16)
    rest = v - high.astype(F32)
    mid = rest.astype(BF16)
    low = (rest - mid.astype(F32)).astype(BF16)
    return high, mid, low


def injected(rec, res, first_x, start, planes, steps):
    local = rec[0:1] - first_x - start
    valid = (local >= 0) & (local < planes)
    row = jnp.where(valid, local * NY + rec[1:2], -1)
    count = rec.shape[1]
    cells = lax.broadcasted_iota(jnp.int32, (planes * NY, count), 0)
    rows = jnp.where(cells == row, 1.0, 0.0).astype(BF16)
    depth = lax.broadcasted_iota(jnp.int32, (NZ, count), 0)
    at_depth = depth == rec[2:3]
    out = []
    for t in steps:
        value = jnp.where(at_depth, res[t : t + 1], 0.0)
        total = None
        for part in three_parts(value):
            piece = lax.dot_general(
                rows, part, (((1,), (1,)), ((), ())), preferred_element_type=F32
            )
            total = piece if total is None else total + piece
        out.append(total)
    return out


def head_kernel(
    place, cur, prev, cour, rec, res, along_z, along_y, up_msg, down_msg, middle
):
    tz, ty = along_z[...], along_y[...]
    (added,) = injected(rec[...], res[...], place[0], 4, 8, (0,))
    added = added.reshape(8, NY, NZ)
    for pair in range(4):
        at = 4 + 2 * pair
        flat = flat_laplace(cur[at : at + 2], tz, ty)
        for e in range(2):
            lap = flat[e] + across(cur, at + e)
            value = 2.0 * cur[at + e] - prev[at + e] + cour[at + e] * lap
            middle[2 * pair + e] = value + added[2 * pair + e]
    up_msg[0:4] = middle[4:8]
    up_msg[4:12] = cur[8:16]
    up_msg[12:16] = prev[12:16]
    up_msg[16:20] = cour[12:16]
    down_msg[0:4] = middle[0:4]
    down_msg[4:12] = cur[0:8]
    down_msg[12:16] = prev[0:4]
    down_msg[16:20] = cour[0:4]


def inject_kernel(place, rec, res, out):
    fields = injected(rec[...], res[...], place[0], -4, EXT + 8, range(STEPS))
    for t in range(STEPS):
        out[t] = fields[t].reshape(EXT + 8, NY, NZ)


def wave_kernel(
    place, cur, prev, cour, fwd, middle, added, low_msg, high_msg, along_z, along_y,
    rows, after, before, c0, c1, c2, co, pv,
):
    c0[0:8] = low_msg[4:12]
    c0[8:24] = cur[...]
    c0[24:32] = high_msg[4:12]
    co[0:4] = low_msg[16:20]
    co[4:20] = cour[...]
    co[20:24] = high_msg[16:20]
    pv[0:4] = low_msg[12:16]
    pv[4:20] = prev[...]
    pv[20:24] = high_msg[12:16]
    c1[0:4] = low_msg[0:4]
    c1[12:20] = middle[...]
    c1[28:32] = high_msg[0:4]
    tz, ty = along_z[...], along_y[...]
    for x in (-4, -2, 0, 2, 12, 14, 16, 18):
        flat = flat_laplace(c0[x + 8 : x + 10], tz, ty)
        for e in range(2):
            i = x + e
            lap = flat[e] + across(c0, i + 8)
            value = 2.0 * c0[i + 8] - pv[i + 4] + co[i + 4] * lap
            c1[i + 8] = value + added[0, i + 4]
    for x in range(-4, EXT + 4, 2):
        flat = flat_laplace(c1[x + 8 : x + 10], tz, ty)
        for e in range(2):
            i = x + e
            lap = flat[e] + across(c1, i + 8)
            value = 2.0 * c1[i + 8] - c0[i + 8] + co[i + 4] * lap + added[1, i + 4]
            c2[i + 4] = value
            if 0 <= i < EXT:
                before[i] = value
    lower = lax.broadcasted_iota(jnp.int32, (NY, NZ), 0) % 8 < 4
    for x in range(0, EXT, 2):
        flat = flat_laplace(c2[x + 4 : x + 6], tz, ty)
        images = []
        for e in range(2):
            i = x + e
            lap = flat[e] + across(c2, i + 4)
            value = 2.0 * c2[i + 4] - c1[i + 8] + co[i + 4] * lap + added[2, i + 4]
            after[i] = value
            acc = c1[i + 8] * fwd[0, i].astype(F32)
            acc = acc + c2[i + 4] * fwd[1, i].astype(F32)
            acc = acc + value * fwd[2, i].astype(F32)
            at = place[0] + i
            inside = (at >= place[1]) & (at < place[2])
            images.append(jnp.where(inside, co[i + 4] * acc, 0.0))
        first, second = images
        even = jnp.where(lower, first, pltpu.roll(second, 4, 0)).reshape(4, 2, 8, NZ)
        odd = jnp.where(lower, pltpu.roll(first, NY - 4, 0), second).reshape(4, 2, 8, NZ)
        for far in range(4):
            for half in range(2):
                rows[2 * half, far, x // 2] = even[far, half]
                rows[2 * half + 1, far, x // 2] = odd[far, half]


def decode_kernel(pieces, spread, latent, place, pick, taps, shares):
    tile = ((pieces[0] + pieces[1]) + (pieces[2] + pieces[3])).reshape(64, NZ)
    wide = None
    for part in three_parts(tile):
        piece = jnp.dot(part, spread[...], preferred_element_type=F32)
        wide = piece if wide is None else wide + piece
    for i in range(8):
        for block in range(4):
            taps[8 * block : 8 * block + 8, NZ * i : NZ * (i + 1)] = wide[
                8 * i : 8 * i + 8, NZ * block : NZ * (block + 1)
            ]
    grad = None
    for part in three_parts(taps[...]):
        piece = lax.dot_general(
            part, latent[...], (((1,), (1,)), ((), ())), preferred_element_type=F32
        )
        grad = piece if grad is None else grad + piece
    tap_j = (lax.broadcasted_iota(jnp.int32, (32, 64), 0) >> 1) & 1
    lane_j = lax.broadcasted_iota(jnp.int32, (32, 64), 1) >> 5
    grad = jnp.where(tap_j == lane_j, grad, 0.0)
    exact = dict(preferred_element_type=F32, precision=lax.Precision.HIGHEST)
    moved = jnp.concatenate(
        [jnp.dot(grad[:16], place[0], **exact), jnp.dot(grad[16:], place[1], **exact)], axis=0
    )
    total = jnp.dot(pick[...], moved, **exact)
    shares[...] = jnp.broadcast_to(total[None], shares.shape)


def latent_kernel(mix, taps, out):
    wide = jnp.dot(
        mix[...], taps[...], preferred_element_type=F32, precision=lax.Precision.HIGHEST
    )
    for i in range(8):
        out[64 * i : 64 * (i + 1)] = wide[:, NZ * i : NZ * (i + 1)]


def share_kernel(pieces, shares):
    total = jnp.sum(pieces[...], axis=0, keepdims=True)
    shares[...] = jnp.broadcast_to(total, shares.shape)


def final_kernel(pieces, out, *, scale):
    out[...] = jnp.sum(pieces[...], axis=0)[:, :64] * scale


VM = pl.BlockSpec(memory_space=pltpu.VMEM)
SM = pl.BlockSpec(memory_space=pltpu.SMEM)


def call(kernel, name, args, outs, scratch=(), scalars=0, interpret=False):
    return pl.pallas_call(
        kernel,
        name=name,
        in_specs=[SM] * scalars + [VM] * (len(args) - scalars),
        out_specs=[VM] * len(outs),
        out_shape=[jax.ShapeDtypeStruct(*o) for o in outs],
        scratch_shapes=list(scratch),
        compiler_params=pltpu.CompilerParams(vmem_limit_bytes=48 << 20),
        interpret=interpret,
    )(*args)


def head(place, cur, prev, cour, rec, res, **kw):
    plane = (NY, NZ)
    return call(
        head_kernel, "head", (place, cur, prev, cour, rec, res, ALONG_Z, ALONG_Y),
        [((20,) + plane, F32), ((20,) + plane, F32), ((8,) + plane, F32)], scalars=1, **kw,
    )


def inject(place, rec, res, **kw):
    outs = [((STEPS, EXT + 8, NY, NZ), F32)]
    return call(inject_kernel, "inject", (place, rec, res), outs, scalars=1, **kw)[0]


def wave(place, cur, prev, cour, fwd, middle, added, low_msg, high_msg, **kw):
    plane = (NY, NZ)
    return call(
        wave_kernel, "wave",
        (place, cur, prev, cour, fwd, middle, added, low_msg, high_msg, ALONG_Z, ALONG_Y),
        [((4, 4, 8, 8, NZ), F32), ((EXT,) + plane, F32), ((EXT,) + plane, F32)],
        [pltpu.VMEM((n,) + plane, F32) for n in (32, 32, 24, 24, 24)], scalars=1, **kw,
    )


def decode(pieces, latent, **kw):
    return call(
        decode_kernel, "decode", (pieces, SPREAD, latent, PLACE, PICK),
        [((32, 8 * NZ), F32), ((16, 8, 128), F32)], **kw,
    )


def latent_rows(latent):
    return latent.reshape(8, 2, 32, NZ).transpose(1, 2, 0, 3).reshape(64, 8 * NZ)


def mixing(weight):
    taps = weight.reshape(32, 2, 2, 2, 2).transpose(0, 1, 4, 2, 3)
    same = np.eye(2, dtype=np.float32)[None, :, None, None, None, :, None]
    return (taps[:, None, :, :, :, None, :] * same).reshape(64, 32)


def latent_out(mix, taps, **kw):
    flat = call(latent_kernel, "latent", (mix, taps), [((512, NZ), F32)], **kw)[0]
    return flat.reshape(8, 32, 2, NZ).transpose(0, 2, 1, 3).reshape(8, 2, 4096)


def body(wave_now, wave_prev, courant, forward, receivers, residual, aperture, latent, weight):
    first_x = lax.axis_index(SLAB) * EXT
    place = jnp.concatenate([first_x[None].astype(jnp.int32), aperture[0]])
    cur, prev = wave_now[0], wave_prev[0]
    rec, res = receivers[0], residual[0]
    up_msg, down_msg, middle = head(place, cur, prev, courant, rec, res)
    count = lax.axis_size(SLAB)
    pairs = [(i, i + 1) for i in range(count - 1)]
    low_msg = lax.ppermute(up_msg, SLAB, pairs)
    high_msg = lax.ppermute(down_msg, SLAB, [(b, a) for a, b in pairs])
    added = inject(place, rec, res)
    lat = latent_rows(latent)
    mix = mixing(weight)
    rows, after, before = wave(
        place, cur, prev, courant, forward[0], middle, added, low_msg, high_msg
    )
    near = lax.all_to_all(rows, "y", 0, 0, tiled=True).sum(0)
    pieces = lax.all_to_all(near, "zh", 0, 0, tiled=True)
    taps, shares = decode(pieces, lat)
    shares = lax.all_to_all(shares, ("zh", "zl"), 0, 0, tiled=True)
    shares = call(share_kernel, "share", (shares,), [((32, 8, 128), F32)])[0]
    shares = lax.all_to_all(shares, ("y", "x", "c"), 0, 0, tiled=True)
    latent_grad = latent_out(mix, taps)

    def last(pieces, out):
        final_kernel(pieces, out, scale=1.0 / math.sqrt(256 * 32 * 64))

    weight_grad = call(last, "total", (shares,), [((8, 64), F32)])[0].T
    return (after[None], before[None], latent_grad, weight_grad)


def solution(mesh):
    fine = Mesh(mesh.devices.reshape(4, 4, 4, 4, 2), PARTS)
    return jax.shard_map(
        body,
        mesh=fine,
        in_specs=(
            P(SHOT, SLAB, None, None),
            P(SHOT, SLAB, None, None),
            P(SLAB, None, None),
            P(SHOT, None, SLAB, None, None),
            P(SHOT, None, None),
            P(SHOT, None, None),
            P(SHOT, None),
            P(SLAB, SHOT, None),
            P(),
        ),
        out_specs=(
            P(SHOT, SLAB, None, None),
            P(SHOT, SLAB, None, None),
            P(SLAB, SHOT, None),
            P(),
        ),
        check_vma=False,
    )
```

time: 126 us -> 108 us (0.86)
  blocking collectives: 29.2 us -> 11 us
  other arithmetic: 14.6 us -> 1.55 us
  Pallas kernels: 0 us -> 12.6 us
  waiting for transfers between devices: 19.6 us -> 31.6 us
  starting transfers between devices: 47 us -> 41.1 us
  local copies, waits for them, and re-layouts: 11.5 us -> 8.46 us
  matrix products: 2.21 us -> 0 us
    all_to_all x2 -> x1, blocking collectives: 29.2 us -> 11 us  [body(): near = lax.all_to_all(rows, 'y', 0, 0, tiled=True).sum(0)]
    pallas_call x0 -> x7, Pallas kernels: none -> 12.6 us  [call(): pl.pallas_call(kernel, name=name, in_specs=[SM] * scalars + [VM] * (len(a...]
    ppermute x6 -> x2, starting transfers between devices: 22.5 us -> 10.1 us  [the longest x1 5.61 us: body(): high_msg = lax.ppermute(down_msg, SLAB, [(b, a) for a, b in pairs])]
    all_to_all x2 -> x3, waiting for transfers between devices: 17.8 us -> 29.4 us  [the longest x1 12 us: body(): pieces = lax.all_to_all(near, 'zh', 0, 0, tiled=True)]
    all_to_all x2 -> x3, starting transfers between devices: 24.5 us -> 30.9 us  [the longest x1 14.8 us: body(): pieces = lax.all_to_all(near, 'zh', 0, 0, tiled=True)]
    add x2 -> x0, other arithmetic: 5.15 us -> none  [body(): 2.0 * current - previous + courant * laplace(pad_sides(padded))]
    unnamed x25 -> x39, local copies, waits for them, and re-layouts: 3.57 us -> 7.66 us
    slice x8 -> x0, local copies, waits for them, and re-layouts: 3.66 us -> none  [the longest x2 2.32 us: extended(): lax.slice_in_dim(block, 0, width, axis=dim)]
  transfers between devices with their start and end apart: 8 -> 5, of which waited for: 4 -> 4; matrix products, arithmetic and copies ran while one was open for 6% -> 1% of each run, Pallas kernels for 0% -> 3%
where the time goes in v2:
time: 108 us; the launch traced here: 107 us
  starting transfers between devices  41.1 us (38%)
  waiting for transfers between devices  31.6 us (29%)
  Pallas kernels  12.6 us (12%)
  blocking collectives  11 us (10%)
  local copies, waits for them, and re-layouts  8.46 us (8%)
  other arithmetic  1.55 us (1%)
    all_to_all x1, starting transfers between devices, body(): pieces = lax.all_to_all(near, 'zh', 0, 0, tiled=True)  14.8 us
    pallas_call x7, Pallas kernels, call(): pl.pallas_call(kernel, name=name, in_specs=[SM] * scalars + [VM] * (len(a...  12.6 us
    all_to_all x1, waiting for transfers between devices, body(): pieces = lax.all_to_all(near, 'zh', 0, 0, tiled=True)  12 us
    all_to_all x1, waiting for transfers between devices, body(): shares = lax.all_to_all(shares, ('zh', 'zl'), 0, 0, tiled=True)  11.3 us
    all_to_all x1, blocking collectives, body(): near = lax.all_to_all(rows, 'y', 0, 0, tiled=True).sum(0)  11 us
    all_to_all x1, starting transfers between devices, body(): shares = lax.all_to_all(shares, ('y', 'x', 'c'), 0, 0, tiled=True)  11 us
    unnamed x39, local copies, waits for them, and re-layouts  7.66 us
    all_to_all x1, waiting for transfers between devices, body(): shares = lax.all_to_all(shares, ('y', 'x', 'c'), 0, 0, tiled=True)  6.05 us
  transfers between devices with their start and end apart: 5, of which 4 were waited for; matrix products, arithmetic and copies ran while one was open for 1% of the time, Pallas kernels for 3%

profile of v2, /device:TPU:1, one launch (start us, length us, event | category | flops | bytes accessed | tf_op | source)
XLA Modules:
  0.0 107.2 jit_solution(452987208056491912)
XLA Ops:
  0.6 0.0 copy-start.11
  0.6 0.7 copy.33
  1.3 0.7 copy.34
  2.0 0.7 pad_add_fusion.place
  2.8 1.0 copy-done.1
  3.8 1.0 copy-done.3
  4.8 1.0 copy-done.5
  5.9 0.9 copy-done.8
  6.8 0.8 copy-done.10
  7.5 0.0 copy-start.9
  7.6 1.2 %head.1 = (f32[20,64,128]{2,1,0:T(8,128)S(1)}, f32[20,64,128]{2,1,0:T(8,128)S(1)}, f32[8,64,128]{2,1,0:T(8,128)S(1)}) custom-call(s32[3]{0:T(128)S(1)} %pad_add_fusion.place, f32[16,64,128]{2,1,0:T(8,128)S(1)} %bitcast.32, f32[16,64,128]{2,1,0:T(8,128)S(1)} %bitcast.34, f32[16,64,128]{2,1,0:T(8,128)S(1)} %copy-done.5, s32[3,256]{1,0:T(4,128)S(1)} %bitcast.40, ...), custom_call_target="tpu_custom_call" | custom-call | tf_op jit(solution)/shard_map/head/pallas_call | solution.py:254
  8.7 4.5 %collective-permute-start = (f32[20,64,128]{2,1,0:T(8,128)S(1)}, f32[20,64,128]{2,1,0:T(8,128)S(1)}, u32[]{:S(2)}, u32[]{:S(2)}) collective-permute-start(f32[20,64,128]{2,1,0:T(8,128)S(1)} %get-tuple-element.13), channel_id=1, source_target_pairs={{0,1},{1,2},{2,3},{3,4},{4,5},{5,6},{6,7},{7,8},{8,9},{9,10},{10,1... | collective-permute-start | bytes 1966088 | tf_op jit(solution)/shard_map/ppermute | solution.py:319
  13.2 5.6 %collective-permute-start.1 = (f32[20,64,128]{2,1,0:T(8,128)S(1)}, f32[20,64,128]{2,1,0:T(8,128)S(1)}, u32[]{:S(2)}, u32[]{:S(2)}) collective-permute-start(f32[20,64,128]{2,1,0:T(8,128)S(1)} %get-tuple-element.14), channel_id=1, source_target_pairs={{1,0},{2,1},{3,2},{4,3},{5,4},{6,5},{7,6},{8,7},{9,8},{10,9},{11,1... | collective-permute-start | bytes 1966088 | tf_op jit(solution)/shard_map/ppermute | solution.py:320
  18.9 2.6 %inject.1.added = f32[3,24,64,128]{3,2,1,0:T(8,128)S(1)} custom-call(s32[3]{0:T(128)S(1)} %pad_add_fusion.place, s32[3,256]{1,0:T(4,128)S(1)} %bitcast.41, f32[3,256]{1,0:T(4,128)S(1)} %bitcast.39), custom_call_target="tpu_custom_call" | custom-call | tf_op jit(solution)/shard_map/inject/pallas_call | solution.py:254
  21.4 0.0 copy-start
  21.4 1.4 %copy-done = f32[3,24,64,128]{3,2,1,0:T(8,128)} copy-done((f32[3,24,64,128]{3,2,1,0:T(8,128)}, f32[3,24,64,128]{3,2,1,0:T(8,128)S(1)}, u32[]{:S(2)}) %copy-start) | copy-done | bytes 2359320
  22.9 0.0 collective-permute-done.low_msg
  22.9 2.3 %collective-permute-done.1.high_msg = f32[20,64,128]{2,1,0:T(8,128)S(1)} collective-permute-done((f32[20,64,128]{2,1,0:T(8,128)S(1)}, f32[20,64,128]{2,1,0:T(8,128)S(1)}, u32[]{:S(2)}, u32[]{:S(2)}) %collective-permute-start.1) | collective-permute-done | bytes 655392 | tf_op jit(solution)/shard_map/ppermute | solution.py:320
  25.2 0.0 copy-done.11
  25.2 0.0 copy-done.2
  25.2 0.0 copy-done.6
  25.2 0.0 copy-done.7
  25.2 0.0 copy-done.9
  25.2 0.0 copy-start.15
  25.2 5.0 %wave.1 = (f32[4,4,8,8,128]{4,3,2,1,0:T(8,128)S(1)}, f32[16,64,128]{2,1,0:T(8,128)}, f32[16,64,128]{2,1,0:T(8,128)}) custom-call(s32[3]{0:T(128)S(1)} %pad_add_fusion.place, f32[16,64,128]{2,1,0:T(8,128)S(1)} %bitcast.33, f32[16,64,128]{2,1,0:T(8,128)S(1)} %bitcast.35, f32[16,64,128]{2,1,0:T(8,128)S(1)} %copy-done.6, bf16[3,16,64,128]{3,2,1,0:T(8,128)(2,1)S(1)} %bitcast.36, ...), custom_call_target="tpu_custom_call" | custom-call | tf_op jit(solution)/shard_map/wave/pallas_call | solution.py:254
  30.2 0.0 copy-start.16
  30.2 0.0 copy-start.17
  30.2 11.0 %all_to_all.20 = f32[4,4,8,8,128]{4,3,2,1,0:T(8,128)S(1)} all-to-all(f32[4,4,8,8,128]{4,3,2,1,0:T(8,128)S(1)} %get-tuple-element.17), channel_id=1, replica_groups=mesh['zh'=4,'y'=4,'zl'=4,'x'=4,'c'=2] {'y'}, dimensions={0} | all-to-all | bytes 1048576 | tf_op jit(solution)/shard_map/all_to_all | solution.py:327
  41.3 0.7 reduce_sum.9
  42.0 14.8 %all-to-all-start.1 = ((f32[4,8,8,128]{3,2,1,0:T(8,128)}), f32[4,8,8,128]{3,2,1,0:T(8,128)S(1)}, u32[]{:S(2)}, u32[]{:S(2)}) async-start(f32[4,8,8,128]{3,2,1,0:T(8,128)} %reduce_sum.9), calls=%async_computation.1 | async-start | bytes 262144 | tf_op jit(solution)/shard_map/all_to_all | solution.py:328
  56.8 0.0 copy-done.15
  56.8 0.1 reshape.29
  56.9 0.1 copy.23
  57.0 12.0 %all-to-all-done.1.pieces = f32[4,8,8,128]{3,2,1,0:T(8,128)S(1)} async-done(((f32[4,8,8,128]{3,2,1,0:T(8,128)}), f32[4,8,8,128]{3,2,1,0:T(8,128)S(1)}, u32[]{:S(2)}, u32[]{:S(2)}) %all-to-all-start.1) | async-done | bytes 131104 | tf_op jit(solution)/shard_map/all_to_all | solution.py:328
  69.0 0.0 copy-done.13
  69.0 1.5 %decode.1 = (f32[32,1024]{1,0:T(8,128)S(1)}, f32[16,8,128]{2,1,0:T(8,128)}) custom-call(f32[4,8,8,128]{3,2,1,0:T(8,128)S(1)} %all-to-all-done.1.pieces, bf16[128,512]{1,0:T(8,128)(2,1)S(1)} %copy-done.12, bf16[64,1024]{1,0:T(8,128)(2,1)S(1)} %bitcast.37, f32[2,64,128]{2,1,0:T(8,128)S(1)} %copy-done.13, f32[8,32]{1,0:T(8,128)S(1)} %copy-done.14), custom_call_target="tpu_custom_call" | custom-call | tf_op jit(solution)/shard_map/decode/pallas_call | solution.py:254
  70.5 5.1 %all-to-all-start.2 = ((f32[16,8,128]{2,1,0:T(8,128)}), f32[16,8,128]{2,1,0:T(8,128)S(1)}, u32[]{:S(2)}, u32[]{:S(2)}) async-start(f32[16,8,128]{2,1,0:T(8,128)} %get-tuple-element.19), calls=%async_computation.2 | async-start | bytes 131072 | tf_op jit(solution)/shard_map/all_to_all | solution.py:330
  75.7 0.1 reshape.28
  75.8 0.1 copy.22
  75.9 11.3 %all-to-all-done.2.pieces = f32[16,8,128]{2,1,0:T(8,128)S(1)} async-done(((f32[16,8,128]{2,1,0:T(8,128)}), f32[16,8,128]{2,1,0:T(8,128)S(1)}, u32[]{:S(2)}, u32[]{:S(2)}) %all-to-all-start.2) | async-done | bytes 65568 | tf_op jit(solution)/shard_map/all_to_all | solution.py:330
  87.2 0.7 share.1
  87.9 11.0 %all-to-all-start.3 = ((f32[32,8,128]{2,1,0:T(8,128)}), f32[32,8,128]{2,1,0:T(8,128)S(1)}, u32[]{:S(2)}, u32[]{:S(2)}) async-start(f32[32,8,128]{2,1,0:T(8,128)} %share.1), calls=%async_computation.3 | async-start | bytes 262144 | tf_op jit(solution)/shard_map/all_to_all | solution.py:332
  98.9 0.1 broadcast_multiply_fusion
  99.1 0.3 mul.35
  99.3 0.1 copy.24.mix
  99.4 1.1 latent.1
  100.5 6.1 %all-to-all-done.3.pieces = f32[32,8,128]{2,1,0:T(8,128)S(1)} async-done(((f32[32,8,128]{2,1,0:T(8,128)}), f32[32,8,128]{2,1,0:T(8,128)S(1)}, u32[]{:S(2)}, u32[]{:S(2)}) %all-to-all-start.3) | async-done | bytes 131104 | tf_op jit(solution)/shard_map/all_to_all | solution.py:332
  106.5 0.6 total.1
  (18 shorter events, 0.1 us)
Async XLA Ops:
  0.6 24.5 %copy-start.11 = (bf16[64,192]{1,0:T(8,128)(2,1)S(1)}, bf16[64,192]{1,0:T(8,128)(2,1)}, u32[]{:S(2)}) copy-start(bf16[64,192]{1,0:T(8,128)(2,1)} %constant.32.clone.along_y) | copy-start | bytes 73732
  2.8 1.0 copy-start.1
  3.8 1.0 copy-start.3
  4.8 1.0 copy-start.5
  5.9 0.9 copy-start.8
  6.8 0.8 copy-start.10
  7.5 17.6 %copy-start.2 = (f32[1,16,64,128]{3,2,1,0:T(8,128)S(1)}, f32[1,16,64,128]{3,2,1,0:T(8,128)}, u32[]{:S(2)}) copy-start(f32[1,16,64,128]{3,2,1,0:T(8,128)} %param.15) | copy-start | bytes 1572868
  7.5 17.6 %copy-start.4 = (f32[1,16,64,128]{3,2,1,0:T(8,128)S(1)}, f32[1,16,64,128]{3,2,1,0:T(8,128)}, u32[]{:S(2)}) copy-start(f32[1,16,64,128]{3,2,1,0:T(8,128)} %param.16) | copy-start | bytes 1572868
  7.5 17.6 %copy-start.6 = (f32[16,64,128]{2,1,0:T(8,128)S(1)}, f32[16,64,128]{2,1,0:T(8,128)}, u32[]{:S(2)}) copy-start(f32[16,64,128]{2,1,0:T(8,128)} %cour.3) | copy-start | bytes 1572868
  7.5 17.6 %copy-start.7 = (bf16[1,3,16,64,128]{4,3,2,1,0:T(8,128)(2,1)S(1)}, bf16[1,3,16,64,128]{4,3,2,1,0:T(8,128)(2,1)}, u32[]{:S(2)}) copy-start(bf16[1,3,16,64,128]{4,3,2,1,0:T(8,128)(2,1)} %param.18) | copy-start | bytes 2359300
  7.5 17.6 %copy-start.9 = (bf16[384,128]{1,0:T(8,128)(2,1)S(1)}, bf16[384,128]{1,0:T(8,128)(2,1)}, u32[]{:S(2)}) copy-start(bf16[384,128]{1,0:T(8,128)(2,1)} %constant.31.clone.along_z) | copy-start | bytes 294916
  8.7 14.2 %collective-permute-start = (f32[20,64,128]{2,1,0:T(8,128)S(1)}, f32[20,64,128]{2,1,0:T(8,128)S(1)}, u32[]{:S(2)}, u32[]{:S(2)}) collective-permute-start(f32[20,64,128]{2,1,0:T(8,128)S(1)} %get-tuple-element.13), channel_id=1, source_target_pairs={{0,1},{1,2},{2,3},{3,4},{4,5},{5,6},{6,7},{7,8},{8,9},{9,10},{10,1... | collective-permute-start | bytes 1966088 | tf_op jit(solution)/shard_map/ppermute | solution.py:319
  13.2 11.9 %collective-permute-start.1 = (f32[20,64,128]{2,1,0:T(8,128)S(1)}, f32[20,64,128]{2,1,0:T(8,128)S(1)}, u32[]{:S(2)}, u32[]{:S(2)}) collective-permute-start(f32[20,64,128]{2,1,0:T(8,128)S(1)} %get-tuple-element.14), channel_id=1, source_target_pairs={{1,0},{2,1},{3,2},{4,3},{5,4},{6,5},{7,6},{8,7},{9,8},{10,9},{11,1... | collective-permute-start | bytes 1966088 | tf_op jit(solution)/shard_map/ppermute | solution.py:320
  21.4 1.4 %copy-start = (f32[3,24,64,128]{3,2,1,0:T(8,128)}, f32[3,24,64,128]{3,2,1,0:T(8,128)S(1)}, u32[]{:S(2)}) copy-start(f32[3,24,64,128]{3,2,1,0:T(8,128)S(1)} %inject.1.added) | copy-start | bytes 7077892
  25.2 31.6 %copy-start.15 = (bf16[8,2,4096]{2,1,0:T(2,128)(2,1)S(1)}, bf16[8,2,4096]{2,1,0:T(2,128)(2,1)}, u32[]{:S(2)}) copy-start(bf16[8,2,4096]{2,1,0:T(2,128)(2,1)} %param.22) | copy-start | bytes 393220
  30.2 38.8 %copy-start.12 = (bf16[128,512]{1,0:T(8,128)(2,1)S(1)}, bf16[128,512]{1,0:T(8,128)(2,1)}, u32[]{:S(2)}) copy-start(bf16[128,512]{1,0:T(8,128)(2,1)} %constant.34.clone.spread) | copy-start | bytes 393220
  30.2 38.8 %copy-start.13 = (f32[2,64,128]{2,1,0:T(8,128)S(1)}, f32[2,64,128]{2,1,0:T(8,128)}, u32[]{:S(2)}) copy-start(f32[2,64,128]{2,1,0:T(8,128)} %constant.35.clone.place) | copy-start | bytes 196612
  30.2 38.8 %copy-start.14 = (f32[8,32]{1,0:T(8,128)S(1)}, f32[8,32]{1,0:T(8,128)}, u32[]{:S(2)}) copy-start(f32[8,32]{1,0:T(8,128)} %constant.36.clone.pick) | copy-start | bytes 3076
  30.2 45.4 %copy-start.16 = (f32[64,8]{0,1:T(8,128)S(1)}, f32[64,8]{0,1:T(8,128)}, u32[]{:S(2)}) copy-start(f32[64,8]{0,1:T(8,128)} %param.23) | copy-start | bytes 6148
  30.2 68.7 %copy-start.17 = (f32[2,2]{0,1:T(2,128)S(1)}, f32[2,2]{0,1:T(2,128)}, u32[]{:S(2)}) copy-start(f32[2,2]{0,1:T(2,128)} %constant.45) | copy-start | bytes 52
  42.0 27.1 %all-to-all-start.1 = ((f32[4,8,8,128]{3,2,1,0:T(8,128)}), f32[4,8,8,128]{3,2,1,0:T(8,128)S(1)}, u32[]{:S(2)}, u32[]{:S(2)}) async-start(f32[4,8,8,128]{3,2,1,0:T(8,128)} %reduce_sum.9), calls=%async_computation.1 | async-start | bytes 262144 | tf_op jit(solution)/shard_map/all_to_all | solution.py:328
  70.5 16.7 %all-to-all-start.2 = ((f32[16,8,128]{2,1,0:T(8,128)}), f32[16,8,128]{2,1,0:T(8,128)S(1)}, u32[]{:S(2)}, u32[]{:S(2)}) async-start(f32[16,8,128]{2,1,0:T(8,128)} %get-tuple-element.19), calls=%async_computation.2 | async-start | bytes 131072 | tf_op jit(solution)/shard_map/all_to_all | solution.py:330
  87.9 18.6 %all-to-all-start.3 = ((f32[32,8,128]{2,1,0:T(8,128)}), f32[32,8,128]{2,1,0:T(8,128)S(1)}, u32[]{:S(2)}, u32[]{:S(2)}) async-start(f32[32,8,128]{2,1,0:T(8,128)} %share.1), calls=%async_computation.3 | async-start | bytes 262144 | tf_op jit(solution)/shard_map/all_to_all | solution.py:332

commit v3 on v2

v3 whole, which is shorter than its diff:
```python
import math

import jax
import jax.numpy as jnp
import numpy as np
from jax import lax
from jax.experimental import pallas as pl
from jax.experimental.pallas import tpu as pltpu
from jax.sharding import Mesh, PartitionSpec as P

STEPS = 3
PARTS = ("zh", "y", "zl", "x", "c")
SHOT = ("zh", "y")
SLAB = ("zl", "x", "c")
EXT = 16
NY = 64
NZ = 128
F32 = jnp.float32
BF16 = jnp.bfloat16

stencil_weights = (-205.0 / 72.0, 8.0 / 5.0, -1.0 / 5.0, 8.0 / 315.0, -1.0 / 560.0)


def high_low(values):
    high = values.astype(BF16)
    return high, (values - high.astype(np.float32)).astype(BF16)


def band(size, center):
    out = np.zeros((size, size), np.float32)
    for k in range(5):
        for i in range(size - k):
            value = center if k == 0 else stencil_weights[k]
            out[i, i + k] = value
            out[i + k, i] = value
    return out


def constants():
    zh, zl = high_low(band(NZ, 3.0 * stencil_weights[0]))
    yh, yl = high_low(band(NY, 0.0))
    along_z = np.concatenate([zh, zh, zl], axis=0)
    along_y = np.concatenate([yh, yh, yl], axis=1)
    spread = np.zeros((NZ, 2, 2, 2, NZ // 2), np.float32)
    for k in range(NZ // 2):
        for c in range(2):
            for h in range(2):
                spread[2 * k + c, h, c, h, k] = 1.0
    spread = spread.reshape(NZ, 4 * NZ).astype(BF16)
    place = np.zeros((2, 64, 128), np.float32)
    for h in range(2):
        for j in range(2):
            for t in range(32):
                place[h, 32 * j + t, 2 * t + h] = 1.0
                place[h, 32 * j + t, 64 + 2 * t + h] = 1.0
    pick = np.zeros((8, 32), np.float32)
    for row in range(32):
        c, a, b = (row >> 3) & 1, (row >> 2) & 1, row & 1
        pick[4 * a + 2 * b + c, row] = 1.0
    return along_z, along_y, spread, place, pick


ALONG_Z, ALONG_Y, SPREAD, PLACE, PICK = constants()


def flat_laplace(planes, along_z, along_y):
    count = len(planes)
    high = [u.astype(BF16) for u in planes]
    low = [(u - h.astype(F32)).astype(BF16) for u, h in zip(planes, high)]
    rows_h, rows_l = jnp.concatenate(high, axis=0), jnp.concatenate(low, axis=0)
    z_part = jnp.dot(
        jnp.concatenate([rows_h, rows_l, rows_h], axis=1), along_z, preferred_element_type=F32
    )
    wide_h, wide_l = jnp.concatenate(high, axis=1), jnp.concatenate(low, axis=1)
    y_part = jnp.dot(
        along_y, jnp.concatenate([wide_h, wide_l, wide_h], axis=0), preferred_element_type=F32
    )
    return [z_part[NY * e : NY * (e + 1)] + y_part[:, NZ * e : NZ * (e + 1)] for e in range(count)]


def across(get, at):
    total = stencil_weights[1] * (get(at + 1) + get(at - 1))
    for k in range(2, 5):
        total = total + stencil_weights[k] * (get(at + k) + get(at - k))
    return total


def three_parts(v):
    high = v.astype(BF16)
    rest = v - high.astype(F32)
    mid = rest.astype(BF16)
    low = (rest - mid.astype(F32)).astype(BF16)
    return high, mid, low


def injected(rec, res, first_x, start, planes, steps):
    local = rec[0] - first_x - start
    valid = (local >= 0) & (local < planes)
    row = jnp.where(valid, local * NY + rec[1], -1)
    count = rec.shape[2]
    cells = lax.broadcasted_iota(jnp.int32, (planes * NY, count), 0)
    rows = jnp.where(cells == row, 1.0, 0.0).astype(BF16)
    depth = lax.broadcasted_iota(jnp.int32, (NZ, count), 0)
    at_depth = depth == rec[2]
    out = []
    for t in steps:
        value = jnp.where(at_depth, res[t], 0.0)
        total = None
        for part in three_parts(value):
            piece = lax.dot_general(
                rows, part, (((1,), (1,)), ((), ())), preferred_element_type=F32
            )
            total = piece if total is None else total + piece
        out.append(total)
    return out


def head_kernel(
    first_x, cur_in, prev_in, cour_in, rec_in, res_in, z_in, y_in, outer, inner, begun,
    cur, prev, cour, rec, res, along_z, along_y, sems,
):
    copies = [
        pltpu.make_async_copy(source, target, sems.at[k])
        for k, (source, target) in enumerate(
            (
                (rec_in, rec),
                (res_in, res),
                (cur_in, cur.at[4:20]),
                (z_in, along_z),
                (y_in, along_y),
                (prev_in, prev),
                (cour_in, cour),
            )
        )
    ]
    for copy in copies:
        copy.start()
    zero = jnp.zeros((4, NY, NZ), F32)
    cur[0:4] = zero
    cur[20:24] = zero
    copies[0].wait()
    copies[1].wait()
    (added,) = injected(rec[...], res[...], first_x[0], 0, EXT, (0,))
    for copy in copies[2:]:
        copy.wait()
    tz, ty = along_z[...], along_y[...]
    for group in range(0, EXT, 4):
        flat = flat_laplace([cur[group + e + 4] for e in range(4)], tz, ty)
        for e in range(4):
            i = group + e
            lap = flat[e] + across(lambda at: cur[at + 4], i)
            value = 2.0 * cur[i + 4] - prev[i] + cour[i] * lap
            begun[i] = value + added[NY * i : NY * (i + 1)]
    odd = (first_x[0] >> 4) & 1
    for message, side in ((outer, odd), (inner, 1 - odd)):
        message[0:8] = begun[pl.ds(8 * side, 8)]
        message[8:12] = cur[pl.ds(4 + 12 * side, 4)]
        message[12:16] = cour[pl.ds(12 * side, 4)]


def inject_kernel(first_x, rec, res, second, third):
    one, two = injected(rec[...], res[...], first_x[0], -4, EXT + 8, (1, 2))
    second[...] = one.reshape(EXT + 8, NY, NZ)
    third[...] = two.reshape(EXT + 8, NY, NZ)[4:20]


def wave_kernel(
    first_x, aperture, cur, cour, fwd_in, begun, second, third, outer, inner, along_z, along_y,
    rows, after, before, far_u, far_c, far_k, near_u, mid, fwd, sem,
):
    copy = pltpu.make_async_copy(fwd_in, fwd, sem)
    copy.start()
    odd = (first_x[0] >> 4) & 1
    for message, side in ((outer, odd), (inner, 1 - odd)):
        far_u[pl.ds(8 * side, 8)] = message[0:8]
        far_c[pl.ds(4 * side, 4)] = message[8:12]
        far_k[pl.ds(4 * side, 4)] = message[12:16]

    def courant_at(i):
        return far_k[i + 4] if i < 0 else far_k[i - 12] if i >= EXT else cour[i]

    def now_at(i):
        return far_c[i + 4] if i < 0 else far_c[i - 12] if i >= EXT else cur[i]

    def step_at(i):
        if i < 0:
            return far_u[i + 8]
        if i >= EXT:
            return far_u[i - 8]
        if i < 4:
            return near_u[i]
        return near_u[i - 8] if i >= 12 else begun[i]

    def missing(i, others):
        total = None
        for k in range(1, 5):
            for at in (i - k, i + k):
                if at in others:
                    term = stencil_weights[k] * now_at(at)
                    total = term if total is None else total + term
        return courant_at(i) * total

    for i in range(4):
        near_u[i] = begun[i] + missing(i, range(-4, 0))
        near_u[i + 4] = begun[i + 12] + missing(i + 12, range(16, 20))
        far_u[i + 4] = far_u[i + 4] + missing(i - 4, range(0, 4))
        far_u[i + 8] = far_u[i + 8] + missing(i + 16, range(12, 16))
    tz, ty = along_z[...], along_y[...]
    for group in range(-4, EXT + 4, 4):
        flat = flat_laplace([step_at(group + e) for e in range(4)], tz, ty)
        for e in range(4):
            i = group + e
            lap = flat[e] + across(step_at, i)
            value = 2.0 * step_at(i) - now_at(i) + courant_at(i) * lap + second[i + 4]
            mid[i + 4] = value
            if 0 <= i < EXT:
                before[i] = value
    copy.wait()
    lower = lax.broadcasted_iota(jnp.int32, (NY, NZ), 0) % 8 < 4
    for group in range(0, EXT, 4):
        flat = flat_laplace([mid[group + e + 4] for e in range(4)], tz, ty)
        images = []
        for e in range(4):
            i = group + e
            lap = flat[e] + across(lambda at: mid[at + 4], i)
            value = 2.0 * mid[i + 4] - step_at(i) + cour[i] * lap + third[i]
            after[i] = value
            acc = step_at(i) * fwd[0, i].astype(F32)
            acc = acc + mid[i + 4] * fwd[1, i].astype(F32)
            acc = acc + value * fwd[2, i].astype(F32)
            at = first_x[0] + i
            inside = (at >= aperture[0, 0]) & (at < aperture[0, 1])
            images.append(jnp.where(inside, cour[i] * acc, 0.0))
        for p in range(2):
            first, next_one = images[2 * p : 2 * p + 2]
            even = jnp.where(lower, first, pltpu.roll(next_one, 4, 0)).reshape(4, 2, 8, NZ)
            odds = jnp.where(lower, pltpu.roll(first, NY - 4, 0), next_one).reshape(4, 2, 8, NZ)
            for far in range(4):
                for half in range(2):
                    rows[2 * half, far, group // 2 + p] = even[far, half]
                    rows[2 * half + 1, far, group // 2 + p] = odds[far, half]


def decode_kernel(pieces, spread, latent, place, pick, taps, shares):
    tile = ((pieces[0] + pieces[1]) + (pieces[2] + pieces[3])).reshape(64, NZ)
    wide = None
    for part in three_parts(tile):
        piece = jnp.dot(part, spread[...], preferred_element_type=F32)
        wide = piece if wide is None else wide + piece
    for i in range(8):
        for block in range(4):
            taps[8 * block : 8 * block + 8, NZ * i : NZ * (i + 1)] = wide[
                8 * i : 8 * i + 8, NZ * block : NZ * (block + 1)
            ]
    grad = None
    for part in three_parts(taps[...]):
        piece = lax.dot_general(
            part, latent[...], (((1,), (1,)), ((), ())), preferred_element_type=F32
        )
        grad = piece if grad is None else grad + piece
    tap_j = (lax.broadcasted_iota(jnp.int32, (32, 64), 0) >> 1) & 1
    lane_j = lax.broadcasted_iota(jnp.int32, (32, 64), 1) >> 5
    grad = jnp.where(tap_j == lane_j, grad, 0.0)
    exact = dict(preferred_element_type=F32, precision=lax.Precision.HIGHEST)
    moved = jnp.concatenate(
        [jnp.dot(grad[:16], place[0], **exact), jnp.dot(grad[16:], place[1], **exact)], axis=0
    )
    total = jnp.dot(pick[...], moved, **exact)
    left = lax.broadcasted_iota(jnp.int32, (4, 128), 1) < 64
    packed = jnp.where(left, total[0:4], total[4:8])
    shares[...] = jnp.broadcast_to(packed[None], shares.shape)


def latent_kernel(mix, taps, out):
    wide = jnp.dot(
        mix[...], taps[...], preferred_element_type=F32, precision=lax.Precision.HIGHEST
    )
    for i in range(8):
        out[64 * i : 64 * (i + 1)] = wide[:, NZ * i : NZ * (i + 1)]


def share_kernel(pieces, shares):
    total = jnp.sum(pieces[...], axis=0, keepdims=True)
    shares[...] = jnp.broadcast_to(total, shares.shape)


def final_kernel(pieces, out, *, scale):
    total = jnp.sum(pieces[...], axis=0) * scale
    out[0:4] = total[:, :64]
    out[4:8] = total[:, 64:]


VM = pl.BlockSpec(memory_space=pltpu.VMEM)
SM = pl.BlockSpec(memory_space=pltpu.SMEM)


HB = pl.BlockSpec(memory_space=pltpu.HBM)


def call(kernel, name, args, outs, scratch=(), scalars=0, stay=(), interpret=False):
    specs = [SM] * scalars + [VM] * (len(args) - scalars)
    args = list(args)
    for k in stay:
        specs[k] = HB
        if not interpret:
            args[k] = pltpu.with_memory_space_constraint(jnp.asarray(args[k]), pltpu.HBM)
    return pl.pallas_call(
        kernel,
        name=name,
        in_specs=specs,
        out_specs=[VM] * len(outs),
        out_shape=[jax.ShapeDtypeStruct(*o) for o in outs],
        scratch_shapes=list(scratch),
        compiler_params=pltpu.CompilerParams(vmem_limit_bytes=16 << 20),
        interpret=interpret,
    )(*args)


def planes(count):
    return (count, NY, NZ)


def head(first_x, cur, prev, cour, rec, res, **kw):
    return call(
        head_kernel, "head", (first_x, cur, prev, cour, rec, res, ALONG_Z, ALONG_Y),
        [(planes(EXT), F32)] * 3,
        [
            pltpu.VMEM(planes(EXT + 8), F32), pltpu.VMEM(planes(EXT), F32),
            pltpu.VMEM(planes(EXT), F32), pltpu.VMEM(rec.shape, jnp.int32),
            pltpu.VMEM(res.shape, F32), pltpu.VMEM(ALONG_Z.shape, BF16),
            pltpu.VMEM(ALONG_Y.shape, BF16), pltpu.SemaphoreType.DMA((7,)),
        ],
        scalars=1, stay=range(1, 8), **kw,
    )


def inject(first_x, rec, res, **kw):
    outs = [(planes(EXT + 8), F32), (planes(EXT), F32)]
    return call(inject_kernel, "inject", (first_x, rec, res), outs, scalars=1, **kw)


def wave(first_x, aperture, cur, cour, fwd, begun, second, third, outer, inner, **kw):
    return call(
        wave_kernel, "wave",
        (first_x, aperture, cur, cour, fwd, begun, second, third, outer, inner, ALONG_Z, ALONG_Y),
        [((4, 4, 8, 8, NZ), F32), (planes(EXT), F32), (planes(EXT), F32)],
        [pltpu.VMEM(planes(n), F32) for n in (16, 8, 8, 8, 24)]
        + [pltpu.VMEM(fwd.shape, BF16), pltpu.SemaphoreType.DMA(())],
        scalars=2, stay=(4,), **kw,
    )


def decode(pieces, latent, **kw):
    return call(
        decode_kernel, "decode", (pieces, SPREAD, latent, PLACE, PICK),
        [((32, 8 * NZ), F32), ((16, 4, 128), F32)], **kw,
    )


def latent_rows(latent):
    return latent.reshape(8, 2, 32, NZ).transpose(1, 2, 0, 3).reshape(64, 8 * NZ)


def mixing(weight):
    taps = weight.reshape(32, 2, 2, 2, 2).transpose(0, 1, 4, 2, 3)
    same = np.eye(2, dtype=np.float32)[None, :, None, None, None, :, None]
    return (taps[:, None, :, :, :, None, :] * same).reshape(64, 32)


def latent_out(mix, taps, **kw):
    flat = call(latent_kernel, "latent", (mix, taps), [((512, NZ), F32)], **kw)[0]
    return flat.reshape(8, 32, 2, NZ).transpose(0, 2, 1, 3).reshape(8, 2, 4096)


def swaps(lower):
    return [pair for i in lower for pair in ((i, i + 1), (i + 1, i))]


def body(wave_now, wave_prev, courant, forward, receivers, residual, aperture, latent, weight):
    first_x = (lax.axis_index(SLAB) * EXT).astype(jnp.int32).reshape(1)
    cur, prev = wave_now[0], wave_prev[0]
    rec, res = receivers.transpose(1, 0, 2), residual.transpose(1, 0, 2)
    outer, inner, begun = head(first_x, cur, prev, courant, rec, res)
    count = lax.axis_size(SLAB)
    outer = lax.ppermute(outer, SLAB, swaps(range(1, count - 1, 2)))
    inner = lax.ppermute(inner, SLAB, swaps(range(0, count, 2)))
    second, third = inject(first_x, rec, res)
    lat = latent_rows(latent)
    mix = mixing(weight)
    rows, after, before = wave(
        first_x, aperture, cur, courant, forward[0], begun, second, third, outer, inner
    )
    near = lax.all_to_all(rows, "y", 0, 0, tiled=True).sum(0)
    pieces = lax.all_to_all(near, "zh", 0, 0, tiled=True)
    taps, shares = decode(pieces, lat)
    shares = lax.all_to_all(shares, ("zh", "zl"), 0, 0, tiled=True)
    shares = call(share_kernel, "share", (shares,), [((32, 4, 128), F32)])[0]
    shares = lax.all_to_all(shares, ("y", "x", "c"), 0, 0, tiled=True)
    latent_grad = latent_out(mix, taps)

    def last(pieces, out):
        final_kernel(pieces, out, scale=1.0 / math.sqrt(256 * 32 * 64))

    weight_grad = call(last, "total", (shares,), [((8, 64), F32)])[0].T
    return (after[None], before[None], latent_grad, weight_grad)


def solution(mesh):
    fine = Mesh(mesh.devices.reshape(4, 4, 4, 4, 2), PARTS)
    return jax.shard_map(
        body,
        mesh=fine,
        in_specs=(
            P(SHOT, SLAB, None, None),
            P(SHOT, SLAB, None, None),
            P(SLAB, None, None),
            P(SHOT, None, SLAB, None, None),
            P(SHOT, None, None),
            P(SHOT, None, None),
            P(SHOT, None),
            P(SLAB, SHOT, None),
            P(),
        ),
        out_specs=(
            P(SHOT, SLAB, None, None),
            P(SHOT, SLAB, None, None),
            P(SLAB, SHOT, None),
            P(),
        ),
        check_vma=False,
    )
```

time: 108 us -> 97 us (0.90)
  local copies, waits for them, and re-layouts: 8.46 us -> 1.5 us
  starting transfers between devices: 41.1 us -> 39 us
  blocking collectives: 11 us -> 12.6 us
  Pallas kernels: 12.6 us -> 11.1 us
    unnamed x39 -> x27, local copies, waits for them, and re-layouts: 7.66 us -> 0.71 us
    ppermute x2, waiting for transfers between devices: 2.27 us -> 0.43 us  [the longest x1 0.42 us: body(): outer = lax.ppermute(outer, SLAB, swaps(range(1, count - 1, 2)))]
    all_to_all x1, blocking collectives: 11 us -> 12.6 us  [body(): near = lax.all_to_all(rows, 'y', 0, 0, tiled=True).sum(0)]
    pallas_call x7, Pallas kernels: 12.6 us -> 11.1 us  [call(): pl.pallas_call(kernel, name=name, in_specs=specs, out_specs=[VM] * len(ou...]
    all_to_all x1, starting transfers between devices: 5.11 us -> 3.63 us  [body(): shares = lax.all_to_all(shares, ('zh', 'zl'), 0, 0, tiled=True)]
    all_to_all x1, waiting for transfers between devices: 12 us -> 13.4 us  [body(): pieces = lax.all_to_all(near, 'zh', 0, 0, tiled=True)]
where the time goes in v3:
time: 97 us; the launch traced here: 96.5 us
  starting transfers between devices  39 us (40%)
  waiting for transfers between devices  30.6 us (32%)
  blocking collectives  12.6 us (13%)
  Pallas kernels  11.1 us (11%)
  local copies, waits for them, and re-layouts  1.5 us (2%)
    all_to_all x1, starting transfers between devices, body(): pieces = lax.all_to_all(near, 'zh', 0, 0, tiled=True)  13.9 us
    all_to_all x1, waiting for transfers between devices, body(): pieces = lax.all_to_all(near, 'zh', 0, 0, tiled=True)  13.4 us
    all_to_all x1, blocking collectives, body(): near = lax.all_to_all(rows, 'y', 0, 0, tiled=True).sum(0)  12.6 us
    all_to_all x1, starting transfers between devices, body(): shares = lax.all_to_all(shares, ('y', 'x', 'c'), 0, 0, tiled=True)  12 us
    all_to_all x1, waiting for transfers between devices, body(): shares = lax.all_to_all(shares, ('zh', 'zl'), 0, 0, tiled=True)  11.1 us
    pallas_call x7, Pallas kernels, call(): pl.pallas_call(kernel, name=name, in_specs=specs, out_specs=[VM] * len(ou...  11.1 us
    all_to_all x1, waiting for transfers between devices, body(): shares = lax.all_to_all(shares, ('y', 'x', 'c'), 0, 0, tiled=True)  5.75 us
    ppermute x1, starting transfers between devices, body(): inner = lax.ppermute(inner, SLAB, swaps(range(0, count, 2)))  4.97 us
  transfers between devices with their start and end apart: 5, of which 4 were waited for; matrix products, arithmetic and copies ran while one was open for 1% of the time, Pallas kernels for 3%

profile of v3, /device:TPU:1, one launch (start us, length us, event | category | flops | bytes accessed | tf_op | source)
XLA Modules:
  0.0 96.5 jit_solution(1964776197153391712)
XLA Ops:
  0.6 0.0 copy-start.7
  0.7 0.0 copy-start
  0.7 0.0 copy-start.1
  0.7 0.0 copy-start.2
  0.7 0.0 copy-start.3
  0.7 2.4 %head.1 = (f32[16,64,128]{2,1,0:T(8,128)S(1)}, f32[16,64,128]{2,1,0:T(8,128)S(1)}, f32[16,64,128]{2,1,0:T(8,128)S(1)}) custom-call(s32[1]{0:T(128)} %bitcast.first_x, f32[16,64,128]{2,1,0:T(8,128)} %bitcast.27, f32[16,64,128]{2,1,0:T(8,128)} %bitcast.35, f32[16,64,128]{2,1,0:T(8,128)} %cour.1, s32[3,1,256]{2,1,0:T(1,128)} %bitcast.30, ...), custom_call_target="tpu_custom_call" | custom-call | tf_op jit(solution)/shard_map/head/pallas_call | solution.py:307
  3.1 0.0 copy-start.6
  3.1 4.5 %collective-permute-start = (f32[16,64,128]{2,1,0:T(8,128)S(1)}, f32[16,64,128]{2,1,0:T(8,128)S(1)}, u32[]{:S(2)}, u32[]{:S(2)}) collective-permute-start(f32[16,64,128]{2,1,0:T(8,128)S(1)} %get-tuple-element.17), channel_id=1, source_target_pairs={{1,2},{2,1},{3,4},{4,3},{5,6},{6,5},{7,8},{8,7},{9,10},{10,9},{11,... | collective-permute-start | bytes 1572872 | tf_op jit(solution)/shard_map/ppermute | solution.py:385
  7.6 5.0 %collective-permute-start.1 = (f32[16,64,128]{2,1,0:T(8,128)S(1)}, f32[16,64,128]{2,1,0:T(8,128)S(1)}, u32[]{:S(2)}, u32[]{:S(2)}) collective-permute-start(f32[16,64,128]{2,1,0:T(8,128)S(1)} %get-tuple-element.18), channel_id=1, source_target_pairs={{0,1},{1,0},{2,3},{3,2},{4,5},{5,4},{6,7},{7,6},{8,9},{9,8},{10,11... | collective-permute-start | bytes 1572872 | tf_op jit(solution)/shard_map/ppermute | solution.py:386
  12.6 0.0 copy-done.7
  12.6 0.0 copy-done.6
  12.6 1.4 %inject.1 = (f32[24,64,128]{2,1,0:T(8,128)S(1)}, f32[16,64,128]{2,1,0:T(8,128)S(1)}) custom-call(s32[1]{0:T(128)} %bitcast.first_x, s32[3,1,256]{2,1,0:T(1,128)S(1)} %bitcast.31, f32[3,1,256]{2,1,0:T(1,128)S(1)} %bitcast.33), custom_call_target="tpu_custom_call" | custom-call | tf_op jit(solution)/shard_map/inject/pallas_call | solution.py:307
  14.0 0.4 collective-permute-done.outer
  14.4 0.0 collective-permute-done.1.inner
  14.4 0.0 copy-done
  14.4 0.0 copy-done.1
  14.5 0.0 copy-done.2
  14.5 0.0 copy-done.3
  14.5 0.6 copy-done.9
  15.1 3.4 %wave.1 = (f32[4,4,8,8,128]{4,3,2,1,0:T(8,128)S(1)}, f32[16,64,128]{2,1,0:T(8,128)}, f32[16,64,128]{2,1,0:T(8,128)}) custom-call(s32[1]{0:T(128)} %bitcast.first_x, s32[1,2]{1,0:T(1,128)S(1)} %copy-done.9, f32[16,64,128]{2,1,0:T(8,128)S(1)} %bitcast.28, f32[16,64,128]{2,1,0:T(8,128)S(1)} %copy-done.1, bf16[3,16,64,128]{3,2,1,0:T(8,128)(2,1)} %bitcast.34, ...), custom_call_target="tpu_custom_call" | custom-call | tf_op jit(solution)/shard_map/wave/pallas_call | solution.py:307
  18.5 12.6 %all_to_all.20 = f32[4,4,8,8,128]{4,3,2,1,0:T(8,128)S(1)} all-to-all(f32[4,4,8,8,128]{4,3,2,1,0:T(8,128)S(1)} %get-tuple-element.21), channel_id=1, replica_groups=mesh['zh'=4,'y'=4,'zl'=4,'x'=4,'c'=2] {'y'}, dimensions={0} | all-to-all | bytes 1048576 | tf_op jit(solution)/shard_map/all_to_all | solution.py:393
  31.1 0.7 reduce_sum.9
  31.8 13.9 %all-to-all-start.1 = ((f32[4,8,8,128]{3,2,1,0:T(8,128)}), f32[4,8,8,128]{3,2,1,0:T(8,128)S(1)}, u32[]{:S(2)}, u32[]{:S(2)}) async-start(f32[4,8,8,128]{3,2,1,0:T(8,128)} %reduce_sum.9), calls=%async_computation.1 | async-start | bytes 262144 | tf_op jit(solution)/shard_map/all_to_all | solution.py:394
  45.7 0.0 copy-done.10
  45.7 0.1 reshape.33
  45.8 0.1 copy.23
  45.9 0.0 copy-start.4
  45.9 0.0 copy-start.5
  45.9 0.0 copy-start.8
  46.0 13.4 %all-to-all-done.1.pieces = f32[4,8,8,128]{3,2,1,0:T(8,128)S(1)} async-done(((f32[4,8,8,128]{3,2,1,0:T(8,128)}), f32[4,8,8,128]{3,2,1,0:T(8,128)S(1)}, u32[]{:S(2)}, u32[]{:S(2)}) %all-to-all-start.1) | async-done | bytes 131104 | tf_op jit(solution)/shard_map/all_to_all | solution.py:394
  59.3 0.0 copy-done.4
  59.3 0.0 copy-done.5
  59.3 0.0 copy-done.8
  59.3 1.5 %decode.1 = (f32[32,1024]{1,0:T(8,128)S(1)}, f32[16,4,128]{2,1,0:T(4,128)}) custom-call(f32[4,8,8,128]{3,2,1,0:T(8,128)S(1)} %all-to-all-done.1.pieces, bf16[128,512]{1,0:T(8,128)(2,1)S(1)} %copy-done.4, bf16[64,1024]{1,0:T(8,128)(2,1)S(1)} %bitcast.29, f32[2,64,128]{2,1,0:T(8,128)S(1)} %copy-done.5, f32[8,32]{1,0:T(8,128)S(1)} %copy-done.8), custom_call_target="tpu_custom_call" | custom-call | tf_op jit(solution)/shard_map/decode/pallas_call | solution.py:307
  60.8 3.6 %all-to-all-start.2 = ((f32[16,4,128]{2,1,0:T(4,128)}), f32[16,4,128]{2,1,0:T(4,128)S(1)}, u32[]{:S(2)}, u32[]{:S(2)}) async-start(f32[16,4,128]{2,1,0:T(4,128)} %get-tuple-element.23), calls=%async_computation.2 | async-start | bytes 65536 | tf_op jit(solution)/shard_map/all_to_all | solution.py:396
  64.5 0.0 copy-done.11
  64.5 0.1 reshape.32
  64.6 0.1 copy.22
  64.7 11.1 %all-to-all-done.2.pieces = f32[16,4,128]{2,1,0:T(4,128)S(1)} async-done(((f32[16,4,128]{2,1,0:T(4,128)}), f32[16,4,128]{2,1,0:T(4,128)S(1)}, u32[]{:S(2)}, u32[]{:S(2)}) %all-to-all-start.2) | async-done | bytes 32800 | tf_op jit(solution)/shard_map/all_to_all | solution.py:396
  75.8 0.6 share.1
  76.5 12.0 %all-to-all-start.3 = ((f32[32,4,128]{2,1,0:T(4,128)}), f32[32,4,128]{2,1,0:T(4,128)S(1)}, u32[]{:S(2)}, u32[]{:S(2)}) async-start(f32[32,4,128]{2,1,0:T(4,128)} %share.1), calls=%async_computation.3 | async-start | bytes 131072 | tf_op jit(solution)/shard_map/all_to_all | solution.py:398
  88.5 0.0 copy-done.12
  88.5 0.1 broadcast_multiply_fusion
  88.6 0.3 mul.35
  88.9 0.1 copy.24.mix
  89.0 1.1 %latent.1 = f32[512,128]{1,0:T(8,128)} custom-call(f32[64,32]{1,0:T(8,128)S(1)} %copy.24.mix, f32[32,1024]{1,0:T(8,128)S(1)} %get-tuple-element.22.taps), custom_call_target="tpu_custom_call" | custom-call | tf_op jit(solution)/shard_map/latent/pallas_call | solution.py:307
  90.1 5.7 %all-to-all-done.3.pieces = f32[32,4,128]{2,1,0:T(4,128)S(1)} async-done(((f32[32,4,128]{2,1,0:T(4,128)}), f32[32,4,128]{2,1,0:T(4,128)S(1)}, u32[]{:S(2)}, u32[]{:S(2)}) %all-to-all-start.3) | async-done | bytes 65568 | tf_op jit(solution)/shard_map/all_to_all | solution.py:398
  95.8 0.7 total.1
  (5 shorter events, 0.0 us)
Async XLA Ops:
  0.6 11.9 %copy-start.7 = (f32[1,3,256]{2,0,1:T(1,128)S(1)}, f32[1,3,256]{2,0,1:T(1,128)}, u32[]{:S(2)}) copy-start(f32[1,3,256]{2,0,1:T(1,128)} %param.20) | copy-start | bytes 9220
  0.7 13.8 %copy-start = (f32[1,16,64,128]{3,2,1,0:T(8,128)S(1)}, f32[1,16,64,128]{3,2,1,0:T(8,128)}, u32[]{:S(2)}) copy-start(f32[1,16,64,128]{3,2,1,0:T(8,128)} %param.15) | copy-start | bytes 1572868
  0.7 13.8 %copy-start.1 = (f32[16,64,128]{2,1,0:T(8,128)S(1)}, f32[16,64,128]{2,1,0:T(8,128)}, u32[]{:S(2)}) copy-start(f32[16,64,128]{2,1,0:T(8,128)} %cour.1) | copy-start | bytes 1572868
  0.7 13.8 %copy-start.2 = (bf16[384,128]{1,0:T(8,128)(2,1)S(1)}, bf16[384,128]{1,0:T(8,128)(2,1)}, u32[]{:S(2)}) copy-start(bf16[384,128]{1,0:T(8,128)(2,1)} %constant.31.clone.z_in.along_z) | copy-start | bytes 294916
  0.7 13.8 %copy-start.3 = (bf16[64,192]{1,0:T(8,128)(2,1)S(1)}, bf16[64,192]{1,0:T(8,128)(2,1)}, u32[]{:S(2)}) copy-start(bf16[64,192]{1,0:T(8,128)(2,1)} %constant.32.clone.y_in.along_y) | copy-start | bytes 73732
  3.1 9.5 %copy-start.6 = (s32[1,3,256]{2,0,1:T(1,128)S(1)}, s32[1,3,256]{2,0,1:T(1,128)}, u32[]{:S(2)}) copy-start(s32[1,3,256]{2,0,1:T(1,128)} %param.19) | copy-start | bytes 9220
  3.1 11.4 %collective-permute-start = (f32[16,64,128]{2,1,0:T(8,128)S(1)}, f32[16,64,128]{2,1,0:T(8,128)S(1)}, u32[]{:S(2)}, u32[]{:S(2)}) collective-permute-start(f32[16,64,128]{2,1,0:T(8,128)S(1)} %get-tuple-element.17), channel_id=1, source_target_pairs={{1,2},{2,1},{3,4},{4,3},{5,6},{6,5},{7,8},{8,7},{9,10},{10,9},{11,... | collective-permute-start | bytes 1572872 | tf_op jit(solution)/shard_map/ppermute | solution.py:385
  7.6 6.9 %collective-permute-start.1 = (f32[16,64,128]{2,1,0:T(8,128)S(1)}, f32[16,64,128]{2,1,0:T(8,128)S(1)}, u32[]{:S(2)}, u32[]{:S(2)}) collective-permute-start(f32[16,64,128]{2,1,0:T(8,128)S(1)} %get-tuple-element.18), channel_id=1, source_target_pairs={{0,1},{1,0},{2,3},{3,2},{4,5},{5,4},{6,7},{7,6},{8,9},{9,8},{10,11... | collective-permute-start | bytes 1572872 | tf_op jit(solution)/shard_map/ppermute | solution.py:386
  14.4 0.7 copy-start.9
  31.8 13.9 %copy-start.10 = (bf16[8,2,4096]{2,1,0:T(2,128)(2,1)S(1)}, bf16[8,2,4096]{2,1,0:T(2,128)(2,1)}, u32[]{:S(2)}) copy-start(bf16[8,2,4096]{2,1,0:T(2,128)(2,1)} %param.22) | copy-start | bytes 393220
  31.8 27.5 %all-to-all-start.1 = ((f32[4,8,8,128]{3,2,1,0:T(8,128)}), f32[4,8,8,128]{3,2,1,0:T(8,128)S(1)}, u32[]{:S(2)}, u32[]{:S(2)}) async-start(f32[4,8,8,128]{3,2,1,0:T(8,128)} %reduce_sum.9), calls=%async_computation.1 | async-start | bytes 262144 | tf_op jit(solution)/shard_map/all_to_all | solution.py:394
  45.9 13.4 %copy-start.4 = (bf16[128,512]{1,0:T(8,128)(2,1)S(1)}, bf16[128,512]{1,0:T(8,128)(2,1)}, u32[]{:S(2)}) copy-start(bf16[128,512]{1,0:T(8,128)(2,1)} %constant.34.clone.spread) | copy-start | bytes 393220
  45.9 13.4 %copy-start.5 = (f32[2,64,128]{2,1,0:T(8,128)S(1)}, f32[2,64,128]{2,1,0:T(8,128)}, u32[]{:S(2)}) copy-start(f32[2,64,128]{2,1,0:T(8,128)} %constant.35.clone.place) | copy-start | bytes 196612
  45.9 13.4 %copy-start.8 = (f32[8,32]{1,0:T(8,128)S(1)}, f32[8,32]{1,0:T(8,128)}, u32[]{:S(2)}) copy-start(f32[8,32]{1,0:T(8,128)} %constant.36.clone.pick) | copy-start | bytes 3076
  60.8 3.6 %copy-start.11 = (f32[64,8]{0,1:T(8,128)S(1)}, f32[64,8]{0,1:T(8,128)}, u32[]{:S(2)}) copy-start(f32[64,8]{0,1:T(8,128)} %param.23) | copy-start | bytes 6148
  60.8 15.0 %all-to-all-start.2 = ((f32[16,4,128]{2,1,0:T(4,128)}), f32[16,4,128]{2,1,0:T(4,128)S(1)}, u32[]{:S(2)}, u32[]{:S(2)}) async-start(f32[16,4,128]{2,1,0:T(4,128)} %get-tuple-element.23), calls=%async_computation.2 | async-start | bytes 65536 | tf_op jit(solution)/shard_map/all_to_all | solution.py:396
  76.5 12.0 %copy-start.12 = (f32[2,2]{0,1:T(2,128)S(1)}, f32[2,2]{0,1:T(2,128)}, u32[]{:S(2)}) copy-start(f32[2,2]{0,1:T(2,128)} %constant.45) | copy-start | bytes 52
  76.5 19.3 %all-to-all-start.3 = ((f32[32,4,128]{2,1,0:T(4,128)}), f32[32,4,128]{2,1,0:T(4,128)S(1)}, u32[]{:S(2)}, u32[]{:S(2)}) async-start(f32[32,4,128]{2,1,0:T(4,128)} %share.1), calls=%async_computation.3 | async-start | bytes 131072 | tf_op jit(solution)/shard_map/all_to_all | solution.py:398

commit v4 on v3

--- a/solution.py
+++ b/solution.py
@@ -91,6 +91,11 @@
     mid = rest.astype(BF16)
     low = (rest - mid.astype(F32)).astype(BF16)
     return high, mid, low
+
+
+def two_parts(v):
+    high = v.astype(BF16)
+    return high, (v - high.astype(F32)).astype(BF16)
 
 
 def injected(rec, res, first_x, start, planes, steps):
@@ -165,11 +170,15 @@
 
 
 def wave_kernel(
-    first_x, aperture, cur, cour, fwd_in, begun, second, third, outer, inner, along_z, along_y,
-    rows, after, before, far_u, far_c, far_k, near_u, mid, fwd, sem,
+    first_x, cur, cour, span_in, fwd_in, begun, second, third, outer, inner, along_z, along_y,
+    rows, after, before, far_u, far_c, far_k, near_u, mid, fwd, span, sems,
 ):
-    copy = pltpu.make_async_copy(fwd_in, fwd, sem)
-    copy.start()
+    copies = [
+        pltpu.make_async_copy(span_in, span, sems.at[0]),
+        pltpu.make_async_copy(fwd_in, fwd, sems.at[1]),
+    ]
+    for copy in copies:
+        copy.start()
     odd = (first_x[0] >> 4) & 1
     for message, side in ((outer, odd), (inner, 1 - odd)):
         far_u[pl.ds(8 * side, 8)] = message[0:8]
@@ -206,16 +215,17 @@
         far_u[i + 4] = far_u[i + 4] + missing(i - 4, range(0, 4))
         far_u[i + 8] = far_u[i + 8] + missing(i + 16, range(12, 16))
     tz, ty = along_z[...], along_y[...]
-    for group in range(-4, EXT + 4, 4):
-        flat = flat_laplace([step_at(group + e) for e in range(4)], tz, ty)
-        for e in range(4):
+    for group in range(-4, EXT + 4, 8):
+        flat = flat_laplace([step_at(group + e) for e in range(8)], tz, ty)
+        for e in range(8):
             i = group + e
             lap = flat[e] + across(step_at, i)
             value = 2.0 * step_at(i) - now_at(i) + courant_at(i) * lap + second[i + 4]
             mid[i + 4] = value
             if 0 <= i < EXT:
                 before[i] = value
-    copy.wait()
+    for copy in copies:
+        copy.wait()
     lower = lax.broadcasted_iota(jnp.int32, (NY, NZ), 0) % 8 < 4
     for group in range(0, EXT, 4):
         flat = flat_laplace([mid[group + e + 4] for e in range(4)], tz, ty)
@@ -229,7 +239,7 @@
             acc = acc + mid[i + 4] * fwd[1, i].astype(F32)
             acc = acc + value * fwd[2, i].astype(F32)
             at = first_x[0] + i
-            inside = (at >= aperture[0, 0]) & (at < aperture[0, 1])
+            inside = (at >= span[0, 0]) & (at < span[0, 1])
             images.append(jnp.where(inside, cour[i] * acc, 0.0))
         for p in range(2):
             first, next_one = images[2 * p : 2 * p + 2]
@@ -244,7 +254,7 @@
 def decode_kernel(pieces, spread, latent, place, pick, taps, shares):
     tile = ((pieces[0] + pieces[1]) + (pieces[2] + pieces[3])).reshape(64, NZ)
     wide = None
-    for part in three_parts(tile):
+    for part in two_parts(tile):
         piece = jnp.dot(part, spread[...], preferred_element_type=F32)
         wide = piece if wide is None else wide + piece
     for i in range(8):
@@ -253,7 +263,7 @@
                 8 * i : 8 * i + 8, NZ * block : NZ * (block + 1)
             ]
     grad = None
-    for part in three_parts(taps[...]):
+    for part in two_parts(taps[...]):
         piece = lax.dot_general(
             part, latent[...], (((1,), (1,)), ((), ())), preferred_element_type=F32
         )
@@ -271,6 +281,21 @@
     shares[...] = jnp.broadcast_to(packed[None], shares.shape)
 
 
+def near_kernel(pieces, out):
+    out[...] = (pieces[0] + pieces[1]) + (pieces[2] + pieces[3])
+
+
+def store_kernel(one, two, one_out, two_out, sems):
+    copies = [
+        pltpu.make_async_copy(one, one_out, sems.at[0]),
+        pltpu.make_async_copy(two, two_out, sems.at[1]),
+    ]
+    for copy in copies:
+        copy.start()
+    for copy in copies:
+        copy.wait()
+
+
 def latent_kernel(mix, taps, out):
     wide = jnp.dot(
         mix[...], taps[...], preferred_element_type=F32, precision=lax.Precision.HIGHEST
@@ -297,7 +322,7 @@
 HB = pl.BlockSpec(memory_space=pltpu.HBM)
 
 
-def call(kernel, name, args, outs, scratch=(), scalars=0, stay=(), interpret=False):
+def call(kernel, name, args, outs, scratch=(), scalars=0, stay=(), near=(), far=(), interpret=False):
     specs = [SM] * scalars + [VM] * (len(args) - scalars)
     args = list(args)
     for k in stay:
@@ -308,8 +333,11 @@
         kernel,
         name=name,
         in_specs=specs,
-        out_specs=[VM] * len(outs),
-        out_shape=[jax.ShapeDtypeStruct(*o) for o in outs],
+        out_specs=[HB if k in far else VM for k in range(len(outs))],
+        out_shape=[
+            pltpu.VMEM(*o) if k in near and not interpret else jax.ShapeDtypeStruct(*o)
+            for k, o in enumerate(outs)
+        ],
         scratch_shapes=list(scratch),
         compiler_params=pltpu.CompilerParams(vmem_limit_bytes=16 << 20),
         interpret=interpret,
@@ -339,21 +367,34 @@
     return call(inject_kernel, "inject", (first_x, rec, res), outs, scalars=1, **kw)
 
 
-def wave(first_x, aperture, cur, cour, fwd, begun, second, third, outer, inner, **kw):
+def wave(first_x, cur, cour, aperture, fwd, begun, second, third, outer, inner, **kw):
     return call(
         wave_kernel, "wave",
-        (first_x, aperture, cur, cour, fwd, begun, second, third, outer, inner, ALONG_Z, ALONG_Y),
+        (first_x, cur, cour, aperture, fwd, begun, second, third, outer, inner, ALONG_Z, ALONG_Y),
         [((4, 4, 8, 8, NZ), F32), (planes(EXT), F32), (planes(EXT), F32)],
         [pltpu.VMEM(planes(n), F32) for n in (16, 8, 8, 8, 24)]
-        + [pltpu.VMEM(fwd.shape, BF16), pltpu.SemaphoreType.DMA(())],
-        scalars=2, stay=(4,), **kw,
-    )
+        + [
+            pltpu.VMEM(fwd.shape, BF16), pltpu.SMEM((1, 2), jnp.int32),
+            pltpu.SemaphoreType.DMA((2,)),
+        ],
+        scalars=1, stay=(3, 4), near=(0, 1, 2), **kw,
+    )
+
+
+def gather_sum(pieces, **kw):
+    return call(near_kernel, "near", (pieces,), [(pieces.shape[1:], F32)], **kw)[0]
+
+
+def store(one, two, **kw):
+    outs = [(one.shape, F32), (two.shape, F32)]
+    sems = [pltpu.SemaphoreType.DMA((2,))]
+    return call(store_kernel, "store", (one, two), outs, sems, far=(0, 1), **kw)
 
 
 def decode(pieces, latent, **kw):
     return call(
         decode_kernel, "decode", (pieces, SPREAD, latent, PLACE, PICK),
-        [((32, 8 * NZ), F32), ((16, 4, 128), F32)], **kw,
+        [((32, 8 * NZ), F32), ((32, 4, 128), F32)], **kw,
     )
 
 
@@ -388,15 +429,18 @@
     lat = latent_rows(latent)
     mix = mixing(weight)
     rows, after, before = wave(
-        first_x, aperture, cur, courant, forward[0], begun, second, third, outer, inner
-    )
-    near = lax.all_to_all(rows, "y", 0, 0, tiled=True).sum(0)
+        first_x, cur, courant, aperture, forward[0], begun, second, third, outer, inner
+    )
+    near = gather_sum(lax.all_to_all(rows, "y", 0, 0, tiled=True))
     pieces = lax.all_to_all(near, "zh", 0, 0, tiled=True)
+    after, before = store(after, before)
+    pieces, after, before, lat, mix = lax.optimization_barrier((pieces, after, before, lat, mix))
     taps, shares = decode(pieces, lat)
+    latent_grad = latent_out(mix, taps)
+    shares = lax.all_to_all(shares, ("y", "x", "c"), 0, 0, tiled=True)
+    shares, latent_grad = lax.optimization_barrier((shares, latent_grad))
+    shares = call(share_kernel, "share", (shares,), [((16, 4, 128), F32)])[0]
     shares = lax.all_to_all(shares, ("zh", "zl"), 0, 0, tiled=True)
-    shares = call(share_kernel, "share", (shares,), [((32, 4, 128), F32)])[0]
-    shares = lax.all_to_all(shares, ("y", "x", "c"), 0, 0, tiled=True)
-    latent_grad = latent_out(mix, taps)
 
     def last(pieces, out):
         final_kernel(pieces, out, scale=1.0 / math.sqrt(256 * 32 * 64))

time: 97 us -> 93.4 us (0.963)
  blocking collectives: 12.6 us -> 28 us
  waiting for transfers between devices: 30.6 us -> 17.1 us
  starting transfers between devices: 39 us -> 33 us
    all_to_all x1 -> x2, blocking collectives: 12.6 us -> 28 us  [the longest x1 15.4 us: body(): shares = lax.all_to_all(shares, ('zh', 'zl'), 0, 0, tiled=True)]
    all_to_all x1 -> x0, waiting for transfers between devices: 11.1 us -> none  [body(): shares = lax.all_to_all(shares, ('zh', 'zl'), 0, 0, tiled=True)]
    all_to_all x1 -> x0, starting transfers between devices: 3.63 us -> none  [body(): shares = lax.all_to_all(shares, ('zh', 'zl'), 0, 0, tiled=True)]
    all_to_all x1, waiting for transfers between devices: 13.4 us -> 10.5 us  [body(): pieces = lax.all_to_all(near, 'zh', 0, 0, tiled=True)]
    all_to_all x1, starting transfers between devices: 12 us -> 9.66 us  [body(): shares = lax.all_to_all(shares, ('y', 'x', 'c'), 0, 0, tiled=True)]
    pallas_call x7 -> x9, Pallas kernels: 11.1 us -> 11.6 us  [call(): pl.pallas_call(kernel, name=name, in_specs=specs, out_specs=[HB if k in f...]
  transfers between devices with their start and end apart: 5 -> 4, of which waited for: 4 -> 3; matrix products, arithmetic and copies ran while one was open for 1% -> 1% of each run, Pallas kernels for 3% -> 4%
where the time goes in v4:
time: 93.4 us; the launch traced here: 92.9 us
  starting transfers between devices  33 us (35%)
  blocking collectives  28 us (30%)
  waiting for transfers between devices  17.1 us (18%)
  Pallas kernels  11.6 us (12%)
  local copies, waits for them, and re-layouts  2.06 us (2%)
    all_to_all x1, blocking collectives, body(): shares = lax.all_to_all(shares, ('zh', 'zl'), 0, 0, tiled=True)  15.4 us
    all_to_all x1, starting transfers between devices, body(): pieces = lax.all_to_all(near, 'zh', 0, 0, tiled=True)  13.9 us
    all_to_all x1, blocking collectives, body(): near = gather_sum(lax.all_to_all(rows, 'y', 0, 0, tiled=True))  12.6 us
    pallas_call x9, Pallas kernels, call(): pl.pallas_call(kernel, name=name, in_specs=specs, out_specs=[HB if k in f...  11.6 us
    all_to_all x1, waiting for transfers between devices, body(): pieces = lax.all_to_all(near, 'zh', 0, 0, tiled=True)  10.5 us
    all_to_all x1, starting transfers between devices, body(): shares = lax.all_to_all(shares, ('y', 'x', 'c'), 0, 0, tiled=True)  9.66 us
    all_to_all x1, waiting for transfers between devices, body(): shares = lax.all_to_all(shares, ('y', 'x', 'c'), 0, 0, tiled=True)  6.18 us
    ppermute x1, starting transfers between devices, body(): inner = lax.ppermute(inner, SLAB, swaps(range(0, count, 2)))  4.97 us
  transfers between devices with their start and end apart: 4, of which 3 were waited for; matrix products, arithmetic and copies ran while one was open for 1% of the time, Pallas kernels for 4%

profile of v4, /device:TPU:1, one launch (start us, length us, event | category | flops | bytes accessed | tf_op | source)
XLA Modules:
  0.0 92.9 jit_solution(4224166522715584772)
XLA Ops:
  0.6 0.0 copy-start.7
  0.7 0.0 copy-start
  0.7 0.0 copy-start.1
  0.7 0.0 copy-start.2
  0.7 0.0 copy-start.3
  0.7 2.4 %head.1 = (f32[16,64,128]{2,1,0:T(8,128)S(1)}, f32[16,64,128]{2,1,0:T(8,128)S(1)}, f32[16,64,128]{2,1,0:T(8,128)S(1)}) custom-call(s32[1]{0:T(128)} %bitcast.first_x, f32[16,64,128]{2,1,0:T(8,128)} %bitcast.27, f32[16,64,128]{2,1,0:T(8,128)} %bitcast.35, f32[16,64,128]{2,1,0:T(8,128)} %cour.1, s32[3,1,256]{2,1,0:T(1,128)} %bitcast.30, ...), custom_call_target="tpu_custom_call" | custom-call | tf_op jit(solution)/shard_map/head/pallas_call | solution.py:332
  3.1 0.0 copy-start.6
  3.1 4.5 %collective-permute-start = (f32[16,64,128]{2,1,0:T(8,128)S(1)}, f32[16,64,128]{2,1,0:T(8,128)S(1)}, u32[]{:S(2)}, u32[]{:S(2)}) collective-permute-start(f32[16,64,128]{2,1,0:T(8,128)S(1)} %get-tuple-element.26), channel_id=1, source_target_pairs={{1,2},{2,1},{3,4},{4,3},{5,6},{6,5},{7,8},{8,7},{9,10},{10,9},{11,... | collective-permute-start | bytes 1572872 | tf_op jit(solution)/shard_map/ppermute | solution.py:426
  7.6 5.0 %collective-permute-start.1 = (f32[16,64,128]{2,1,0:T(8,128)S(1)}, f32[16,64,128]{2,1,0:T(8,128)S(1)}, u32[]{:S(2)}, u32[]{:S(2)}) collective-permute-start(f32[16,64,128]{2,1,0:T(8,128)S(1)} %get-tuple-element.27), channel_id=1, source_target_pairs={{0,1},{1,0},{2,3},{3,2},{4,5},{5,4},{6,7},{7,6},{8,9},{9,8},{10,11... | collective-permute-start | bytes 1572872 | tf_op jit(solution)/shard_map/ppermute | solution.py:427
  12.6 0.0 copy-done.7
  12.6 0.0 copy-done.6
  12.6 1.4 %inject.1 = (f32[24,64,128]{2,1,0:T(8,128)S(1)}, f32[16,64,128]{2,1,0:T(8,128)S(1)}) custom-call(s32[1]{0:T(128)} %bitcast.first_x, s32[3,1,256]{2,1,0:T(1,128)S(1)} %bitcast.31, f32[3,1,256]{2,1,0:T(1,128)S(1)} %bitcast.33), custom_call_target="tpu_custom_call" | custom-call | tf_op jit(solution)/shard_map/inject/pallas_call | solution.py:332
  14.0 0.4 collective-permute-done.outer
  14.4 0.0 collective-permute-done.1.inner
  14.4 0.0 copy-done
  14.4 0.0 copy-done.1
  14.4 0.0 copy-done.2
  14.5 0.0 copy-done.3
  14.5 3.0 %wave.1 = (f32[4,4,8,8,128]{4,3,2,1,0:T(8,128)S(1)}, f32[16,64,128]{2,1,0:T(8,128)S(1)}, f32[16,64,128]{2,1,0:T(8,128)S(1)}) custom-call(s32[1]{0:T(128)} %bitcast.first_x, f32[16,64,128]{2,1,0:T(8,128)S(1)} %bitcast.28, f32[16,64,128]{2,1,0:T(8,128)S(1)} %copy-done.1, s32[1,2]{1,0:T(1,128)} %span_in.1, bf16[3,16,64,128]{3,2,1,0:T(8,128)(2,1)} %bitcast.34, ...), custom_call_target="tpu_custom_call" | custom-call | tf_op jit(solution)/shard_map/wave/pallas_call | solution.py:332
  17.5 12.6 %all_to_all.20.pieces = f32[4,4,8,8,128]{4,3,2,1,0:T(8,128)S(1)} all-to-all(f32[4,4,8,8,128]{4,3,2,1,0:T(8,128)S(1)} %get-tuple-element.28), channel_id=1, replica_groups=mesh['zh'=4,'y'=4,'zl'=4,'x'=4,'c'=2] {'y'}, dimensions={0} | all-to-all | bytes 1048576 | tf_op jit(solution)/shard_map/all_to_all | solution.py:434
  30.1 0.7 near.1
  30.8 13.9 %all-to-all-start.1 = ((f32[4,8,8,128]{3,2,1,0:T(8,128)}), f32[4,8,8,128]{3,2,1,0:T(8,128)S(1)}, u32[]{:S(2)}, u32[]{:S(2)}) async-start(f32[4,8,8,128]{3,2,1,0:T(8,128)} %near.1), calls=%async_computation.1 | async-start | bytes 262144 | tf_op jit(solution)/shard_map/all_to_all | solution.py:435
  44.7 0.0 copy-done.10
  44.7 0.1 reshape.34
  44.8 0.0 copy-start.11
  44.8 0.1 copy.23
  44.9 0.6 copy-done.11
  45.5 0.1 broadcast_multiply_fusion
  45.6 0.0 copy-start.9
  45.6 0.3 mul.35
  45.9 0.6 copy-done.9
  46.5 0.1 reshape.32
  46.7 0.1 copy.22
  46.8 0.0 copy-start.4
  46.8 0.0 copy-start.5
  46.8 1.0 %store.1 = (f32[16,64,128]{2,1,0:T(8,128)}, f32[16,64,128]{2,1,0:T(8,128)}) custom-call(f32[16,64,128]{2,1,0:T(8,128)S(1)} %get-tuple-element.29.one, f32[16,64,128]{2,1,0:T(8,128)S(1)} %get-tuple-element.30.two), custom_call_target="tpu_custom_call" | custom-call | tf_op jit(solution)/shard_map/store/pallas_call | solution.py:332
  47.8 0.0 copy-start.8
  47.8 10.5 %all-to-all-done.1.pieces = f32[4,8,8,128]{3,2,1,0:T(8,128)S(1)} async-done(((f32[4,8,8,128]{3,2,1,0:T(8,128)}), f32[4,8,8,128]{3,2,1,0:T(8,128)S(1)}, u32[]{:S(2)}, u32[]{:S(2)}) %all-to-all-start.1) | async-done | bytes 131104 | tf_op jit(solution)/shard_map/all_to_all | solution.py:435
  58.3 0.0 copy-done.4
  58.3 0.0 copy-done.5
  58.3 0.0 copy-done.8
  58.3 1.4 %decode.1 = (f32[32,1024]{1,0:T(8,128)S(1)}, f32[32,4,128]{2,1,0:T(4,128)}) custom-call(f32[4,8,8,128]{3,2,1,0:T(8,128)S(1)} %all-to-all-done.1.pieces, bf16[128,512]{1,0:T(8,128)(2,1)S(1)} %copy-done.4, bf16[64,1024]{1,0:T(8,128)(2,1)S(1)} %bitcast.29, f32[2,64,128]{2,1,0:T(8,128)S(1)} %copy-done.5, f32[8,32]{1,0:T(8,128)S(1)} %copy-done.8), custom_call_target="tpu_custom_call" | custom-call | tf_op jit(solution)/shard_map/decode/pallas_call | solution.py:332
  59.7 9.7 %all-to-all-start.2 = ((f32[32,4,128]{2,1,0:T(4,128)}), f32[32,4,128]{2,1,0:T(4,128)S(1)}, u32[]{:S(2)}, u32[]{:S(2)}) async-start(f32[32,4,128]{2,1,0:T(4,128)} %get-tuple-element.37), calls=%async_computation.2 | async-start | bytes 131072 | tf_op jit(solution)/shard_map/all_to_all | solution.py:440
  69.4 0.1 copy.24.mix
  69.5 1.1 %latent.1 = f32[512,128]{1,0:T(8,128)} custom-call(f32[64,32]{1,0:T(8,128)S(1)} %copy.24.mix, f32[32,1024]{1,0:T(8,128)S(1)} %get-tuple-element.39.taps), custom_call_target="tpu_custom_call" | custom-call | tf_op jit(solution)/shard_map/latent/pallas_call | solution.py:332
  70.5 6.2 %all-to-all-done.2.pieces = f32[32,4,128]{2,1,0:T(4,128)S(1)} async-done(((f32[32,4,128]{2,1,0:T(4,128)}), f32[32,4,128]{2,1,0:T(4,128)S(1)}, u32[]{:S(2)}, u32[]{:S(2)}) %all-to-all-start.2) | async-done | bytes 65568 | tf_op jit(solution)/shard_map/all_to_all | solution.py:440
  76.7 15.4 %all_to_all.21.pieces = f32[16,4,128]{2,1,0:T(4,128)S(1)} all-to-all(f32[16,4,128]{2,1,0:T(4,128)S(1)} %share.1), channel_id=1, replica_groups=mesh['zh'=4,'y'=4,'zl'=4,'x'=4,'c'=2] {'zh','zl'}, dimensions={0} | all-to-all | bytes 65536 | tf_op jit(solution)/shard_map/all_to_all | solution.py:443
  92.2 0.7 total.1
  (3 shorter events, 0.1 us)
Async XLA Ops:
  0.6 11.9 %copy-start.7 = (f32[1,3,256]{2,0,1:T(1,128)S(1)}, f32[1,3,256]{2,0,1:T(1,128)}, u32[]{:S(2)}) copy-start(f32[1,3,256]{2,0,1:T(1,128)} %param.20) | copy-start | bytes 9220
  0.7 13.8 %copy-start = (f32[1,16,64,128]{3,2,1,0:T(8,128)S(1)}, f32[1,16,64,128]{3,2,1,0:T(8,128)}, u32[]{:S(2)}) copy-start(f32[1,16,64,128]{3,2,1,0:T(8,128)} %param.15) | copy-start | bytes 1572868
  0.7 13.8 %copy-start.1 = (f32[16,64,128]{2,1,0:T(8,128)S(1)}, f32[16,64,128]{2,1,0:T(8,128)}, u32[]{:S(2)}) copy-start(f32[16,64,128]{2,1,0:T(8,128)} %cour.1) | copy-start | bytes 1572868
  0.7 13.8 %copy-start.2 = (bf16[384,128]{1,0:T(8,128)(2,1)S(1)}, bf16[384,128]{1,0:T(8,128)(2,1)}, u32[]{:S(2)}) copy-start(bf16[384,128]{1,0:T(8,128)(2,1)} %constant.29.clone.z_in.along_z) | copy-start | bytes 294916
  0.7 13.8 %copy-start.3 = (bf16[64,192]{1,0:T(8,128)(2,1)S(1)}, bf16[64,192]{1,0:T(8,128)(2,1)}, u32[]{:S(2)}) copy-start(bf16[64,192]{1,0:T(8,128)(2,1)} %constant.30.clone.y_in.along_y) | copy-start | bytes 73732
  3.1 9.5 %copy-start.6 = (s32[1,3,256]{2,0,1:T(1,128)S(1)}, s32[1,3,256]{2,0,1:T(1,128)}, u32[]{:S(2)}) copy-start(s32[1,3,256]{2,0,1:T(1,128)} %param.19) | copy-start | bytes 9220
  3.1 11.4 %collective-permute-start = (f32[16,64,128]{2,1,0:T(8,128)S(1)}, f32[16,64,128]{2,1,0:T(8,128)S(1)}, u32[]{:S(2)}, u32[]{:S(2)}) collective-permute-start(f32[16,64,128]{2,1,0:T(8,128)S(1)} %get-tuple-element.26), channel_id=1, source_target_pairs={{1,2},{2,1},{3,4},{4,3},{5,6},{6,5},{7,8},{8,7},{9,10},{10,9},{11,... | collective-permute-start | bytes 1572872 | tf_op jit(solution)/shard_map/ppermute | solution.py:426
  7.6 6.9 %collective-permute-start.1 = (f32[16,64,128]{2,1,0:T(8,128)S(1)}, f32[16,64,128]{2,1,0:T(8,128)S(1)}, u32[]{:S(2)}, u32[]{:S(2)}) collective-permute-start(f32[16,64,128]{2,1,0:T(8,128)S(1)} %get-tuple-element.27), channel_id=1, source_target_pairs={{0,1},{1,0},{2,3},{3,2},{4,5},{5,4},{6,7},{7,6},{8,9},{9,8},{10,11... | collective-permute-start | bytes 1572872 | tf_op jit(solution)/shard_map/ppermute | solution.py:427
  30.8 13.9 %copy-start.10 = (f32[64,8]{0,1:T(8,128)S(1)}, f32[64,8]{0,1:T(8,128)}, u32[]{:S(2)}) copy-start(f32[64,8]{0,1:T(8,128)} %param.23) | copy-start | bytes 6148
  30.8 27.5 %all-to-all-start.1 = ((f32[4,8,8,128]{3,2,1,0:T(8,128)}), f32[4,8,8,128]{3,2,1,0:T(8,128)S(1)}, u32[]{:S(2)}, u32[]{:S(2)}) async-start(f32[4,8,8,128]{3,2,1,0:T(8,128)} %near.1), calls=%async_computation.1 | async-start | bytes 262144 | tf_op jit(solution)/shard_map/all_to_all | solution.py:435
  44.8 0.7 copy-start.11
  45.6 0.9 copy-start.9
  46.8 11.5 %copy-start.4 = (bf16[128,512]{1,0:T(8,128)(2,1)S(1)}, bf16[128,512]{1,0:T(8,128)(2,1)}, u32[]{:S(2)}) copy-start(bf16[128,512]{1,0:T(8,128)(2,1)} %constant.32.clone.spread) | copy-start | bytes 393220
  46.8 11.5 %copy-start.5 = (f32[2,64,128]{2,1,0:T(8,128)S(1)}, f32[2,64,128]{2,1,0:T(8,128)}, u32[]{:S(2)}) copy-start(f32[2,64,128]{2,1,0:T(8,128)} %constant.33.clone.place) | copy-start | bytes 196612
  47.8 10.5 %copy-start.8 = (f32[8,32]{1,0:T(8,128)S(1)}, f32[8,32]{1,0:T(8,128)}, u32[]{:S(2)}) copy-start(f32[8,32]{1,0:T(8,128)} %constant.34.clone.pick) | copy-start | bytes 3076
  59.7 17.0 %all-to-all-start.2 = ((f32[32,4,128]{2,1,0:T(4,128)}), f32[32,4,128]{2,1,0:T(4,128)S(1)}, u32[]{:S(2)}, u32[]{:S(2)}) async-start(f32[32,4,128]{2,1,0:T(4,128)} %get-tuple-element.37), calls=%async_computation.2 | async-start | bytes 131072 | tf_op jit(solution)/shard_map/all_to_all | solution.py:440

commit v5 on v4

--- a/solution.py
+++ b/solution.py
@@ -47,20 +47,14 @@
             for h in range(2):
                 spread[2 * k + c, h, c, h, k] = 1.0
     spread = spread.reshape(NZ, 4 * NZ).astype(BF16)
-    place = np.zeros((2, 64, 128), np.float32)
-    for h in range(2):
-        for j in range(2):
-            for t in range(32):
-                place[h, 32 * j + t, 2 * t + h] = 1.0
-                place[h, 32 * j + t, 64 + 2 * t + h] = 1.0
-    pick = np.zeros((8, 32), np.float32)
-    for row in range(32):
+    pick = np.zeros((8, 16), np.float32)
+    for row in range(16):
         c, a, b = (row >> 3) & 1, (row >> 2) & 1, row & 1
         pick[4 * a + 2 * b + c, row] = 1.0
-    return along_z, along_y, spread, place, pick
-
-
-ALONG_Z, ALONG_Y, SPREAD, PLACE, PICK = constants()
+    return along_z, along_y, spread, pick
+
+
+ALONG_Z, ALONG_Y, SPREAD, PICK = constants()
 
 
 def flat_laplace(planes, along_z, along_y):
@@ -163,22 +157,21 @@
         message[12:16] = cour[pl.ds(12 * side, 4)]
 
 
-def inject_kernel(first_x, rec, res, second, third):
+def inject_kernel(first_x, fwd_in, rec, res, second, third, fwd, sem):
+    copy = pltpu.make_async_copy(fwd_in, fwd, sem)
+    copy.start()
     one, two = injected(rec[...], res[...], first_x[0], -4, EXT + 8, (1, 2))
     second[...] = one.reshape(EXT + 8, NY, NZ)
     third[...] = two.reshape(EXT + 8, NY, NZ)[4:20]
+    copy.wait()
 
 
 def wave_kernel(
-    first_x, cur, cour, span_in, fwd_in, begun, second, third, outer, inner, along_z, along_y,
-    rows, after, before, far_u, far_c, far_k, near_u, mid, fwd, span, sems,
+    first_x, cur, cour, span_in, fwd, begun, second, third, outer, inner, along_z, along_y,
+    rows, after, before, far_u, far_c, far_k, near_u, mid, span, sem,
 ):
-    copies = [
-        pltpu.make_async_copy(span_in, span, sems.at[0]),
-        pltpu.make_async_copy(fwd_in, fwd, sems.at[1]),
-    ]
-    for copy in copies:
-        copy.start()
+    copy = pltpu.make_async_copy(span_in, span, sem)
+    copy.start()
     odd = (first_x[0] >> 4) & 1
     for message, side in ((outer, odd), (inner, 1 - odd)):
         far_u[pl.ds(8 * side, 8)] = message[0:8]
@@ -224,9 +217,8 @@
             mid[i + 4] = value
             if 0 <= i < EXT:
                 before[i] = value
-    for copy in copies:
-        copy.wait()
-    lower = lax.broadcasted_iota(jnp.int32, (NY, NZ), 0) % 8 < 4
+    copy.wait()
+    lower = lax.broadcasted_iota(jnp.int32, (8, 8, NZ), 1) < 4
     for group in range(0, EXT, 4):
         flat = flat_laplace([mid[group + e + 4] for e in range(4)], tz, ty)
         images = []
@@ -242,42 +234,50 @@
             inside = (at >= span[0, 0]) & (at < span[0, 1])
             images.append(jnp.where(inside, cour[i] * acc, 0.0))
         for p in range(2):
-            first, next_one = images[2 * p : 2 * p + 2]
-            even = jnp.where(lower, first, pltpu.roll(next_one, 4, 0)).reshape(4, 2, 8, NZ)
-            odds = jnp.where(lower, pltpu.roll(first, NY - 4, 0), next_one).reshape(4, 2, 8, NZ)
+            first, next_one = (v.reshape(8, 8, NZ) for v in images[2 * p : 2 * p + 2])
+            turned = pltpu.roll(next_one, 4, 1)
+            even = jnp.where(lower, first, turned).reshape(4, 2, 8, NZ)
+            odds = jnp.where(lower, turned, first).reshape(4, 2, 8, NZ)
             for far in range(4):
                 for half in range(2):
                     rows[2 * half, far, group // 2 + p] = even[far, half]
                     rows[2 * half + 1, far, group // 2 + p] = odds[far, half]
 
 
-def decode_kernel(pieces, spread, latent, place, pick, taps, shares):
-    tile = ((pieces[0] + pieces[1]) + (pieces[2] + pieces[3])).reshape(64, NZ)
-    wide = None
-    for part in two_parts(tile):
-        piece = jnp.dot(part, spread[...], preferred_element_type=F32)
-        wide = piece if wide is None else wide + piece
-    for i in range(8):
-        for block in range(4):
-            taps[8 * block : 8 * block + 8, NZ * i : NZ * (i + 1)] = wide[
-                8 * i : 8 * i + 8, NZ * block : NZ * (block + 1)
-            ]
-    grad = None
-    for part in two_parts(taps[...]):
-        piece = lax.dot_general(
-            part, latent[...], (((1,), (1,)), ((), ())), preferred_element_type=F32
-        )
-        grad = piece if grad is None else grad + piece
-    tap_j = (lax.broadcasted_iota(jnp.int32, (32, 64), 0) >> 1) & 1
-    lane_j = lax.broadcasted_iota(jnp.int32, (32, 64), 1) >> 5
-    grad = jnp.where(tap_j == lane_j, grad, 0.0)
-    exact = dict(preferred_element_type=F32, precision=lax.Precision.HIGHEST)
-    moved = jnp.concatenate(
-        [jnp.dot(grad[:16], place[0], **exact), jnp.dot(grad[16:], place[1], **exact)], axis=0
-    )
-    total = jnp.dot(pick[...], moved, **exact)
-    left = lax.broadcasted_iota(jnp.int32, (4, 128), 1) < 64
-    packed = jnp.where(left, total[0:4], total[4:8])
+def decode_kernel(odd_y, pieces, spread, latent, pick, tile, shares):
+    total = (pieces[0] + pieces[1]) + (pieces[2] + pieces[3])
+    total = jnp.where(odd_y[0] == 1, pltpu.roll(total, 4, 1), total).reshape(64, NZ)
+    tile[...] = total
+    wide = jnp.dot(
+        jnp.concatenate(two_parts(total), axis=0), spread[...], preferred_element_type=F32
+    )
+    taps = jnp.concatenate(
+        [
+            jnp.concatenate(
+                [
+                    wide[64 * part + 8 * i : 64 * part + 8 * i + 8, NZ * c : NZ * (c + 1)]
+                    for i in range(8)
+                ],
+                axis=1,
+            )
+            for part in range(2)
+            for c in range(2)
+        ],
+        axis=0,
+    ).astype(BF16)
+    grad = lax.dot_general(
+        taps, latent[...], (((1,), (1,)), ((), ())), preferred_element_type=F32
+    )
+    grad = grad[0:16] + grad[16:32]
+    tap_j = (lax.broadcasted_iota(jnp.int32, (16, NZ), 0) >> 1) & 1
+    lane_j = lax.broadcasted_iota(jnp.int32, (16, NZ), 1) >> 6
+    grad = jnp.dot(
+        pick[...], jnp.where(tap_j == lane_j, grad, 0.0),
+        preferred_element_type=F32, precision=lax.Precision.HIGHEST,
+    )
+    grad = grad + pltpu.roll(grad, 64, 1)
+    left = lax.broadcasted_iota(jnp.int32, (4, NZ), 1) < 64
+    packed = jnp.where(left, grad[0:4], grad[4:8])
     shares[...] = jnp.broadcast_to(packed[None], shares.shape)
 
 
@@ -296,12 +296,21 @@
         copy.wait()
 
 
-def latent_kernel(mix, taps, out):
-    wide = jnp.dot(
+def latent_kernel(mix, tile, spread, out, taps):
+    wide = None
+    for part in two_parts(tile[...]):
+        piece = jnp.dot(part, spread[...], preferred_element_type=F32)
+        wide = piece if wide is None else wide + piece
+    for i in range(8):
+        for block in range(4):
+            taps[8 * block : 8 * block + 8, NZ * i : NZ * (i + 1)] = wide[
+                8 * i : 8 * i + 8, NZ * block : NZ * (block + 1)
+            ]
+    mixed = jnp.dot(
         mix[...], taps[...], preferred_element_type=F32, precision=lax.Precision.HIGHEST
     )
     for i in range(8):
-        out[64 * i : 64 * (i + 1)] = wide[:, NZ * i : NZ * (i + 1)]
+        out[64 * i : 64 * (i + 1)] = mixed[:, NZ * i : NZ * (i + 1)]
 
 
 def share_kernel(pieces, shares):
@@ -358,13 +367,16 @@
             pltpu.VMEM(res.shape, F32), pltpu.VMEM(ALONG_Z.shape, BF16),
             pltpu.VMEM(ALONG_Y.shape, BF16), pltpu.SemaphoreType.DMA((7,)),
         ],
-        scalars=1, stay=range(1, 8), **kw,
-    )
-
-
-def inject(first_x, rec, res, **kw):
-    outs = [(planes(EXT + 8), F32), (planes(EXT), F32)]
-    return call(inject_kernel, "inject", (first_x, rec, res), outs, scalars=1, **kw)
+        scalars=1, stay=range(1, 8), near=(0, 1, 2), **kw,
+    )
+
+
+def inject(first_x, fwd, rec, res, **kw):
+    outs = [(planes(EXT + 8), F32), (planes(EXT), F32), (fwd.shape, BF16)]
+    return call(
+        inject_kernel, "inject", (first_x, fwd, rec, res), outs,
+        [pltpu.SemaphoreType.DMA(())], scalars=1, stay=(1,), near=(0, 1, 2), **kw,
+    )
 
 
 def wave(first_x, cur, cour, aperture, fwd, begun, second, third, outer, inner, **kw):
@@ -374,15 +386,15 @@
         [((4, 4, 8, 8, NZ), F32), (planes(EXT), F32), (planes(EXT), F32)],
         [pltpu.VMEM(planes(n), F32) for n in (16, 8, 8, 8, 24)]
         + [
-            pltpu.VMEM(fwd.shape, BF16), pltpu.SMEM((1, 2), jnp.int32),
-            pltpu.SemaphoreType.DMA((2,)),
+            pltpu.SMEM((1, 2), jnp.int32), pltpu.SemaphoreType.DMA(()),
         ],
-        scalars=1, stay=(3, 4), near=(0, 1, 2), **kw,
+        scalars=1, stay=(3,), near=(0, 1, 2), **kw,
     )
 
 
 def gather_sum(pieces, **kw):
-    return call(near_kernel, "near", (pieces,), [(pieces.shape[1:], F32)], **kw)[0]
+    outs = [(pieces.shape[1:], F32)]
+    return call(near_kernel, "near", (pieces,), outs, near=(0,), **kw)[0]
 
 
 def store(one, two, **kw):
@@ -391,15 +403,16 @@
     return call(store_kernel, "store", (one, two), outs, sems, far=(0, 1), **kw)
 
 
-def decode(pieces, latent, **kw):
+def decode(odd_y, pieces, latent, **kw):
     return call(
-        decode_kernel, "decode", (pieces, SPREAD, latent, PLACE, PICK),
-        [((32, 8 * NZ), F32), ((32, 4, 128), F32)], **kw,
+        decode_kernel, "decode", (odd_y, pieces, SPREAD[:, : 2 * NZ], latent, PICK),
+        [((64, NZ), F32), ((32, 4, NZ), F32)], scalars=1, near=(0, 1), **kw,
     )
 
 
 def latent_rows(latent):
-    return latent.reshape(8, 2, 32, NZ).transpose(1, 2, 0, 3).reshape(64, 8 * NZ)
+    cells = latent.reshape(8, 2, 64, NZ // 2).transpose(1, 2, 0, 3)
+    return jnp.pad(cells, ((0, 0), (0, 0), (0, 0), (0, NZ // 2))).reshape(NZ, 8 * NZ)
 
 
 def mixing(weight):
@@ -408,8 +421,11 @@
     return (taps[:, None, :, :, :, None, :] * same).reshape(64, 32)
 
 
-def latent_out(mix, taps, **kw):
-    flat = call(latent_kernel, "latent", (mix, taps), [((512, NZ), F32)], **kw)[0]
+def latent_out(mix, tile, **kw):
+    flat = call(
+        latent_kernel, "latent", (mix, tile, SPREAD), [((512, NZ), F32)],
+        [pltpu.VMEM((32, 8 * NZ), F32)], **kw,
+    )[0]
     return flat.reshape(8, 32, 2, NZ).transpose(0, 2, 1, 3).reshape(8, 2, 4096)
 
 
@@ -425,18 +441,19 @@
     count = lax.axis_size(SLAB)
     outer = lax.ppermute(outer, SLAB, swaps(range(1, count - 1, 2)))
     inner = lax.ppermute(inner, SLAB, swaps(range(0, count, 2)))
-    second, third = inject(first_x, rec, res)
+    second, third, fwd = inject(first_x, forward[0], rec, res)
     lat = latent_rows(latent)
     mix = mixing(weight)
     rows, after, before = wave(
-        first_x, cur, courant, aperture, forward[0], begun, second, third, outer, inner
+        first_x, cur, courant, aperture, fwd, begun, second, third, outer, inner
     )
     near = gather_sum(lax.all_to_all(rows, "y", 0, 0, tiled=True))
     pieces = lax.all_to_all(near, "zh", 0, 0, tiled=True)
     after, before = store(after, before)
     pieces, after, before, lat, mix = lax.optimization_barrier((pieces, after, before, lat, mix))
-    taps, shares = decode(pieces, lat)
-    latent_grad = latent_out(mix, taps)
+    odd_y = (lax.axis_index("y") & 1).astype(jnp.int32).reshape(1)
+    tile, shares = decode(odd_y, pieces, lat)
+    latent_grad = latent_out(mix, tile)
     shares = lax.all_to_all(shares, ("y", "x", "c"), 0, 0, tiled=True)
     shares, latent_grad = lax.optimization_barrier((shares, latent_grad))
     shares = call(share_kernel, "share", (shares,), [((16, 4, 128), F32)])[0]

time: 93.4 us -> 92.8 us (level)
  no operation moved by 1% of the time
where the time goes in v5:
time: 92.8 us; the launch traced here: 92.3 us
  starting transfers between devices  33.3 us (36%)
  blocking collectives  28 us (30%)
  waiting for transfers between devices  16.6 us (18%)
  Pallas kernels  11.1 us (12%)
  local copies, waits for them, and re-layouts  2.32 us (2%)
    all_to_all x1, blocking collectives, body(): shares = lax.all_to_all(shares, ('zh', 'zl'), 0, 0, tiled=True)  15.4 us
    all_to_all x1, starting transfers between devices, body(): pieces = lax.all_to_all(near, 'zh', 0, 0, tiled=True)  13.9 us
    all_to_all x1, blocking collectives, body(): near = gather_sum(lax.all_to_all(rows, 'y', 0, 0, tiled=True))  12.6 us
    pallas_call x9, Pallas kernels, call(): pl.pallas_call(kernel, name=name, in_specs=specs, out_specs=[HB if k in f...  11.1 us
    all_to_all x1, waiting for transfers between devices, body(): pieces = lax.all_to_all(near, 'zh', 0, 0, tiled=True)  10.2 us
    all_to_all x1, starting transfers between devices, body(): shares = lax.all_to_all(shares, ('y', 'x', 'c'), 0, 0, tiled=True)  9.78 us
    all_to_all x1, waiting for transfers between devices, body(): shares = lax.all_to_all(shares, ('y', 'x', 'c'), 0, 0, tiled=True)  6.02 us
    ppermute x1, starting transfers between devices, body(): inner = lax.ppermute(inner, SLAB, swaps(range(0, count, 2)))  4.97 us
  transfers between devices with their start and end apart: 4, of which 3 were waited for; matrix products, arithmetic and copies ran while one was open for 1% of the time, Pallas kernels for 4%

profile of v5, /device:TPU:1, one launch (start us, length us, event | category | flops | bytes accessed | tf_op | source)
XLA Modules:
  0.0 92.3 jit_solution(1869480922907905938)
XLA Ops:
  0.6 0.0 copy-start.6
  0.7 0.0 copy-start.7
  0.7 0.0 copy-start.1
  0.7 2.3 %head.1 = (f32[16,64,128]{2,1,0:T(8,128)S(1)}, f32[16,64,128]{2,1,0:T(8,128)S(1)}, f32[16,64,128]{2,1,0:T(8,128)S(1)}) custom-call(s32[1]{0:T(128)} %bitcast.first_x, f32[16,64,128]{2,1,0:T(8,128)} %bitcast.30, f32[16,64,128]{2,1,0:T(8,128)} %bitcast.40, f32[16,64,128]{2,1,0:T(8,128)} %cour.1, s32[3,1,256]{2,1,0:T(1,128)} %bitcast.33, ...), custom_call_target="tpu_custom_call" | custom-call | tf_op jit(solution)/shard_map/head/pallas_call | solution.py:341
  3.0 0.0 copy-start
  3.0 4.6 %collective-permute-start = (f32[16,64,128]{2,1,0:T(8,128)S(1)}, f32[16,64,128]{2,1,0:T(8,128)S(1)}, u32[]{:S(2)}, u32[]{:S(2)}) collective-permute-start(f32[16,64,128]{2,1,0:T(8,128)S(1)} %get-tuple-element.28), channel_id=1, source_target_pairs={{1,2},{2,1},{3,4},{4,3},{5,6},{6,5},{7,8},{8,7},{9,10},{10,9},{11,... | collective-permute-start | bytes 1572872 | tf_op jit(solution)/shard_map/ppermute | solution.py:442
  7.7 5.0 %collective-permute-start.1 = (f32[16,64,128]{2,1,0:T(8,128)S(1)}, f32[16,64,128]{2,1,0:T(8,128)S(1)}, u32[]{:S(2)}, u32[]{:S(2)}) collective-permute-start(f32[16,64,128]{2,1,0:T(8,128)S(1)} %get-tuple-element.29), channel_id=1, source_target_pairs={{0,1},{1,0},{2,3},{3,2},{4,5},{5,4},{6,7},{7,6},{8,9},{9,8},{10,11... | collective-permute-start | bytes 1572872 | tf_op jit(solution)/shard_map/ppermute | solution.py:443
  12.7 0.0 copy-done.6
  12.7 0.0 copy-done.7
  12.7 0.0 copy-start.2
  12.7 0.0 copy-start.3
  12.7 1.4 %inject.1 = (f32[24,64,128]{2,1,0:T(8,128)S(1)}, f32[16,64,128]{2,1,0:T(8,128)S(1)}, bf16[3,16,64,128]{3,2,1,0:T(8,128)(2,1)S(1)}) custom-call(s32[1]{0:T(128)} %bitcast.first_x, bf16[3,16,64,128]{3,2,1,0:T(8,128)(2,1)} %bitcast.39, s32[3,1,256]{2,1,0:T(1,128)S(1)} %bitcast.34, f32[3,1,256]{2,1,0:T(1,128)S(1)} %bitcast.36), custom_call_target="tpu_custom_call" | custom-call | tf_op jit(solution)/shard_map/inject/pallas_call | solution.py:341
  14.1 0.4 collective-permute-done.outer
  14.5 0.0 collective-permute-done.1.inner
  14.5 0.0 copy-done.1
  14.5 0.0 copy-done
  14.5 0.0 copy-done.2
  14.5 0.0 copy-done.3
  14.6 2.5 %wave.1 = (f32[4,4,8,8,128]{4,3,2,1,0:T(8,128)S(1)}, f32[16,64,128]{2,1,0:T(8,128)S(1)}, f32[16,64,128]{2,1,0:T(8,128)S(1)}) custom-call(s32[1]{0:T(128)} %bitcast.first_x, f32[16,64,128]{2,1,0:T(8,128)S(1)} %bitcast.31, f32[16,64,128]{2,1,0:T(8,128)S(1)} %copy-done.1, s32[1,2]{1,0:T(1,128)} %span_in.1, bf16[3,16,64,128]{3,2,1,0:T(8,128)(2,1)S(1)} %get-tuple-element.24.fwd, ...), custom_call_target="tpu_custom_call" | custom-call | tf_op jit(solution)/shard_map/wave/pallas_call | solution.py:341
  17.1 12.6 %all_to_all.20.pieces = f32[4,4,8,8,128]{4,3,2,1,0:T(8,128)S(1)} all-to-all(f32[4,4,8,8,128]{4,3,2,1,0:T(8,128)S(1)} %get-tuple-element.30), channel_id=1, replica_groups=mesh['zh'=4,'y'=4,'zl'=4,'x'=4,'c'=2] {'y'}, dimensions={0} | all-to-all | bytes 1048576 | tf_op jit(solution)/shard_map/all_to_all | solution.py:450
  29.7 0.7 near.1
  30.4 13.9 %all-to-all-start.1 = ((f32[4,8,8,128]{3,2,1,0:T(8,128)}), f32[4,8,8,128]{3,2,1,0:T(8,128)S(1)}, u32[]{:S(2)}, u32[]{:S(2)}) async-start(f32[4,8,8,128]{3,2,1,0:T(8,128)} %near.1), calls=%async_computation.1 | async-start | bytes 262144 | tf_op jit(solution)/shard_map/all_to_all | solution.py:451
  44.3 0.0 copy-done.9
  44.3 0.2 reshape.35
  44.5 0.2 copy.30
  44.7 0.1 pad.4
  44.8 0.0 copy-start.10
  44.8 0.6 copy-done.10
  45.4 0.1 reshape.37
  45.6 0.0 copy-start.11
  45.6 0.1 copy.23
  45.7 0.6 copy-done.11
  46.3 0.1 broadcast_multiply_fusion
  46.4 0.3 mul.35
  46.7 0.0 copy-start.5
  46.7 1.0 %store.1 = (f32[16,64,128]{2,1,0:T(8,128)}, f32[16,64,128]{2,1,0:T(8,128)}) custom-call(f32[16,64,128]{2,1,0:T(8,128)S(1)} %get-tuple-element.31.one, f32[16,64,128]{2,1,0:T(8,128)S(1)} %get-tuple-element.32.two), custom_call_target="tpu_custom_call" | custom-call | tf_op jit(solution)/shard_map/store/pallas_call | solution.py:341
  47.7 0.0 copy-start.8
  47.7 10.2 %all-to-all-done.1.pieces = f32[4,8,8,128]{3,2,1,0:T(8,128)S(1)} async-done(((f32[4,8,8,128]{3,2,1,0:T(8,128)}), f32[4,8,8,128]{3,2,1,0:T(8,128)S(1)}, u32[]{:S(2)}, u32[]{:S(2)}) %all-to-all-start.1) | async-done | bytes 131104 | tf_op jit(solution)/shard_map/all_to_all | solution.py:451
  57.9 0.0 copy-done.5
  57.9 0.0 copy-done.8
  57.9 1.1 %decode.1 = (f32[64,128]{1,0:T(8,128)S(1)}, f32[32,4,128]{2,1,0:T(4,128)}) custom-call(s32[1]{0:T(128)} %bitcast.10.odd_y, f32[4,8,8,128]{3,2,1,0:T(8,128)S(1)} %all-to-all-done.1.pieces, bf16[128,256]{1,0:T(8,128)(2,1)S(1)} %copy-done.5, bf16[128,1024]{1,0:T(8,128)(2,1)S(1)} %bitcast.32, f32[8,16]{1,0:T(8,128)S(1)} %copy-done.8), custom_call_target="tpu_custom_call" | custom-call | tf_op jit(solution)/shard_map/decode/pallas_call | solution.py:341
  59.1 9.8 %all-to-all-start.2 = ((f32[32,4,128]{2,1,0:T(4,128)}), f32[32,4,128]{2,1,0:T(4,128)S(1)}, u32[]{:S(2)}, u32[]{:S(2)}) async-start(f32[32,4,128]{2,1,0:T(4,128)} %get-tuple-element.39), calls=%async_computation.2 | async-start | bytes 131072 | tf_op jit(solution)/shard_map/all_to_all | solution.py:457
  68.9 0.1 copy.24.mix
  68.9 0.0 copy-done.4
  68.9 1.2 %latent.1 = f32[512,128]{1,0:T(8,128)} custom-call(f32[64,32]{1,0:T(8,128)S(1)} %copy.24.mix, f32[64,128]{1,0:T(8,128)S(1)} %get-tuple-element.41.tile, bf16[128,512]{1,0:T(8,128)(2,1)S(1)} %copy-done.4), custom_call_target="tpu_custom_call" | custom-call | tf_op jit(solution)/shard_map/latent/pallas_call | solution.py:341
  70.2 6.0 %all-to-all-done.2.pieces = f32[32,4,128]{2,1,0:T(4,128)S(1)} async-done(((f32[32,4,128]{2,1,0:T(4,128)}), f32[32,4,128]{2,1,0:T(4,128)S(1)}, u32[]{:S(2)}, u32[]{:S(2)}) %all-to-all-start.2) | async-done | bytes 65568 | tf_op jit(solution)/shard_map/all_to_all | solution.py:457
  76.2 15.4 %all_to_all.21.pieces = f32[16,4,128]{2,1,0:T(4,128)S(1)} all-to-all(f32[16,4,128]{2,1,0:T(4,128)S(1)} %share.1), channel_id=1, replica_groups=mesh['zh'=4,'y'=4,'zl'=4,'x'=4,'c'=2] {'zh','zl'}, dimensions={0} | all-to-all | bytes 65536 | tf_op jit(solution)/shard_map/all_to_all | solution.py:460
  91.7 0.7 total.1
  (4 shorter events, 0.1 us)
Async XLA Ops:
  0.6 12.0 %copy-start.6 = (s32[1,3,256]{2,0,1:T(1,128)S(1)}, s32[1,3,256]{2,0,1:T(1,128)}, u32[]{:S(2)}) copy-start(s32[1,3,256]{2,0,1:T(1,128)} %param.19) | copy-start | bytes 9220
  0.7 12.0 %copy-start.7 = (f32[1,3,256]{2,0,1:T(1,128)S(1)}, f32[1,3,256]{2,0,1:T(1,128)}, u32[]{:S(2)}) copy-start(f32[1,3,256]{2,0,1:T(1,128)} %param.20) | copy-start | bytes 9220
  0.7 13.9 %copy-start.1 = (f32[16,64,128]{2,1,0:T(8,128)S(1)}, f32[16,64,128]{2,1,0:T(8,128)}, u32[]{:S(2)}) copy-start(f32[16,64,128]{2,1,0:T(8,128)} %cour.1) | copy-start | bytes 1572868
  3.0 11.5 %copy-start = (f32[1,16,64,128]{3,2,1,0:T(8,128)S(1)}, f32[1,16,64,128]{3,2,1,0:T(8,128)}, u32[]{:S(2)}) copy-start(f32[1,16,64,128]{3,2,1,0:T(8,128)} %param.15) | copy-start | bytes 1572868
  3.0 11.5 %collective-permute-start = (f32[16,64,128]{2,1,0:T(8,128)S(1)}, f32[16,64,128]{2,1,0:T(8,128)S(1)}, u32[]{:S(2)}, u32[]{:S(2)}) collective-permute-start(f32[16,64,128]{2,1,0:T(8,128)S(1)} %get-tuple-element.28), channel_id=1, source_target_pairs={{1,2},{2,1},{3,4},{4,3},{5,6},{6,5},{7,8},{8,7},{9,10},{10,9},{11,... | collective-permute-start | bytes 1572872 | tf_op jit(solution)/shard_map/ppermute | solution.py:442
  7.7 6.9 %collective-permute-start.1 = (f32[16,64,128]{2,1,0:T(8,128)S(1)}, f32[16,64,128]{2,1,0:T(8,128)S(1)}, u32[]{:S(2)}, u32[]{:S(2)}) collective-permute-start(f32[16,64,128]{2,1,0:T(8,128)S(1)} %get-tuple-element.29), channel_id=1, source_target_pairs={{0,1},{1,0},{2,3},{3,2},{4,5},{5,4},{6,7},{7,6},{8,9},{9,8},{10,11... | collective-permute-start | bytes 1572872 | tf_op jit(solution)/shard_map/ppermute | solution.py:443
  12.7 1.9 %copy-start.2 = (bf16[384,128]{1,0:T(8,128)(2,1)S(1)}, bf16[384,128]{1,0:T(8,128)(2,1)}, u32[]{:S(2)}) copy-start(bf16[384,128]{1,0:T(8,128)(2,1)} %constant.38.clone.z_in.along_z) | copy-start | bytes 294916
  12.7 1.9 %copy-start.3 = (bf16[64,192]{1,0:T(8,128)(2,1)S(1)}, bf16[64,192]{1,0:T(8,128)(2,1)}, u32[]{:S(2)}) copy-start(bf16[64,192]{1,0:T(8,128)(2,1)} %constant.39.clone.y_in.along_y) | copy-start | bytes 73732
  30.4 13.9 %copy-start.9 = (bf16[8,2,4096]{2,1,0:T(2,128)(2,1)S(1)}, bf16[8,2,4096]{2,1,0:T(2,128)(2,1)}, u32[]{:S(2)}) copy-start(bf16[8,2,4096]{2,1,0:T(2,128)(2,1)} %param.22) | copy-start | bytes 393220
  30.4 27.5 %all-to-all-start.1 = ((f32[4,8,8,128]{3,2,1,0:T(8,128)}), f32[4,8,8,128]{3,2,1,0:T(8,128)S(1)}, u32[]{:S(2)}, u32[]{:S(2)}) async-start(f32[4,8,8,128]{3,2,1,0:T(8,128)} %near.1), calls=%async_computation.1 | async-start | bytes 262144 | tf_op jit(solution)/shard_map/all_to_all | solution.py:451
  44.8 0.7 copy-start.10
  45.6 0.7 copy-start.11
  46.7 11.2 %copy-start.5 = (bf16[128,256]{1,0:T(8,128)(2,1)S(1)}, bf16[128,256]{1,0:T(8,128)(2,1)}, u32[]{:S(2)}) copy-start(bf16[128,256]{1,0:T(8,128)(2,1)} %constant.41.clone.spread) | copy-start | bytes 196612
  47.7 10.2 %copy-start.8 = (f32[8,16]{1,0:T(8,128)S(1)}, f32[8,16]{1,0:T(8,128)}, u32[]{:S(2)}) copy-start(f32[8,16]{1,0:T(8,128)} %constant.42.clone.pick) | copy-start | bytes 1540
  59.1 9.9 %copy-start.4 = (bf16[128,512]{1,0:T(8,128)(2,1)S(1)}, bf16[128,512]{1,0:T(8,128)(2,1)}, u32[]{:S(2)}) copy-start(bf16[128,512]{1,0:T(8,128)(2,1)} %constant.43.clone.spread) | copy-start | bytes 393220
  59.1 17.1 %all-to-all-start.2 = ((f32[32,4,128]{2,1,0:T(4,128)}), f32[32,4,128]{2,1,0:T(4,128)S(1)}, u32[]{:S(2)}, u32[]{:S(2)}) async-start(f32[32,4,128]{2,1,0:T(4,128)} %get-tuple-element.39), calls=%async_computation.2 | async-start | bytes 131072 | tf_op jit(solution)/shard_map/all_to_all | solution.py:457

commit v6 on v5

--- a/solution.py
+++ b/solution.py
@@ -90,6 +90,18 @@
 def two_parts(v):
     high = v.astype(BF16)
     return high, (v - high.astype(F32)).astype(BF16)
+
+
+def slab_start():
+    return lax.axis_index(SLAB) * EXT
+
+
+def core():
+    return lax.axis_index("c")
+
+
+def odd_y():
+    return lax.axis_index("y") & 1
 
 
 def injected(rec, res, first_x, start, planes, steps):
@@ -115,7 +127,7 @@
 
 
 def head_kernel(
-    first_x, cur_in, prev_in, cour_in, rec_in, res_in, z_in, y_in, outer, inner, begun,
+    cur_in, prev_in, cour_in, rec_in, res_in, z_in, y_in, outer, inner, begun,
     cur, prev, cour, rec, res, along_z, along_y, sems,
 ):
     copies = [
@@ -139,7 +151,7 @@
     cur[20:24] = zero
     copies[0].wait()
     copies[1].wait()
-    (added,) = injected(rec[...], res[...], first_x[0], 0, EXT, (0,))
+    (added,) = injected(rec[...], res[...], slab_start(), 0, EXT, (0,))
     for copy in copies[2:]:
         copy.wait()
     tz, ty = along_z[...], along_y[...]
@@ -150,29 +162,30 @@
             lap = flat[e] + across(lambda at: cur[at + 4], i)
             value = 2.0 * cur[i + 4] - prev[i] + cour[i] * lap
             begun[i] = value + added[NY * i : NY * (i + 1)]
-    odd = (first_x[0] >> 4) & 1
+    odd = core()
     for message, side in ((outer, odd), (inner, 1 - odd)):
         message[0:8] = begun[pl.ds(8 * side, 8)]
         message[8:12] = cur[pl.ds(4 + 12 * side, 4)]
         message[12:16] = cour[pl.ds(12 * side, 4)]
 
 
-def inject_kernel(first_x, fwd_in, rec, res, second, third, fwd, sem):
+def inject_kernel(fwd_in, rec, res, second, third, fwd, sem):
     copy = pltpu.make_async_copy(fwd_in, fwd, sem)
     copy.start()
-    one, two = injected(rec[...], res[...], first_x[0], -4, EXT + 8, (1, 2))
+    one, two = injected(rec[...], res[...], slab_start(), -4, EXT + 8, (1, 2))
     second[...] = one.reshape(EXT + 8, NY, NZ)
     third[...] = two.reshape(EXT + 8, NY, NZ)[4:20]
     copy.wait()
 
 
 def wave_kernel(
-    first_x, cur, cour, span_in, fwd, begun, second, third, outer, inner, along_z, along_y,
+    cur, cour, span_in, fwd, begun, second, third, outer, inner, along_z, along_y,
     rows, after, before, far_u, far_c, far_k, near_u, mid, span, sem,
 ):
+    first_x = slab_start()
     copy = pltpu.make_async_copy(span_in, span, sem)
     copy.start()
-    odd = (first_x[0] >> 4) & 1
+    odd = core()
     for message, side in ((outer, odd), (inner, 1 - odd)):
         far_u[pl.ds(8 * side, 8)] = message[0:8]
         far_c[pl.ds(4 * side, 4)] = message[8:12]
@@ -230,7 +243,7 @@
             acc = step_at(i) * fwd[0, i].astype(F32)
             acc = acc + mid[i + 4] * fwd[1, i].astype(F32)
             acc = acc + value * fwd[2, i].astype(F32)
-            at = first_x[0] + i
+            at = first_x + i
             inside = (at >= span[0, 0]) & (at < span[0, 1])
             images.append(jnp.where(inside, cour[i] * acc, 0.0))
         for p in range(2):
@@ -244,9 +257,9 @@
                     rows[2 * half + 1, far, group // 2 + p] = odds[far, half]
 
 
-def decode_kernel(odd_y, pieces, spread, latent, pick, tile, shares):
+def decode_kernel(pieces, spread, latent, pick, tile, shares):
     total = (pieces[0] + pieces[1]) + (pieces[2] + pieces[3])
-    total = jnp.where(odd_y[0] == 1, pltpu.roll(total, 4, 1), total).reshape(64, NZ)
+    total = jnp.where(odd_y() == 1, pltpu.roll(total, 4, 1), total).reshape(64, NZ)
     tile[...] = total
     wide = jnp.dot(
         jnp.concatenate(two_parts(total), axis=0), spread[...], preferred_element_type=F32
@@ -325,14 +338,13 @@
 
 
 VM = pl.BlockSpec(memory_space=pltpu.VMEM)
-SM = pl.BlockSpec(memory_space=pltpu.SMEM)
 
 
 HB = pl.BlockSpec(memory_space=pltpu.HBM)
 
 
-def call(kernel, name, args, outs, scratch=(), scalars=0, stay=(), near=(), far=(), interpret=False):
-    specs = [SM] * scalars + [VM] * (len(args) - scalars)
+def call(kernel, name, args, outs, scratch=(), stay=(), near=(), far=(), interpret=False):
+    specs = [VM] * len(args)
     args = list(args)
     for k in stay:
         specs[k] = HB
@@ -357,9 +369,9 @@
     return (count, NY, NZ)
 
 
-def head(first_x, cur, prev, cour, rec, res, **kw):
+def head(cur, prev, cour, rec, res, **kw):
     return call(
-        head_kernel, "head", (first_x, cur, prev, cour, rec, res, ALONG_Z, ALONG_Y),
+        head_kernel, "head", (cur, prev, cour, rec, res, ALONG_Z, ALONG_Y),
         [(planes(EXT), F32)] * 3,
         [
             pltpu.VMEM(planes(EXT + 8), F32), pltpu.VMEM(planes(EXT), F32),
@@ -367,28 +379,28 @@
             pltpu.VMEM(res.shape, F32), pltpu.VMEM(ALONG_Z.shape, BF16),
             pltpu.VMEM(ALONG_Y.shape, BF16), pltpu.SemaphoreType.DMA((7,)),
         ],
-        scalars=1, stay=range(1, 8), near=(0, 1, 2), **kw,
-    )
-
-
-def inject(first_x, fwd, rec, res, **kw):
+        stay=range(7), near=(0, 1, 2), **kw,
+    )
+
+
+def inject(fwd, rec, res, **kw):
     outs = [(planes(EXT + 8), F32), (planes(EXT), F32), (fwd.shape, BF16)]
     return call(
-        inject_kernel, "inject", (first_x, fwd, rec, res), outs,
-        [pltpu.SemaphoreType.DMA(())], scalars=1, stay=(1,), near=(0, 1, 2), **kw,
-    )
-
-
-def wave(first_x, cur, cour, aperture, fwd, begun, second, third, outer, inner, **kw):
+        inject_kernel, "inject", (fwd, rec, res), outs,
+        [pltpu.SemaphoreType.DMA(())], stay=(0,), near=(0, 1, 2), **kw,
+    )
+
+
+def wave(cur, cour, aperture, fwd, begun, second, third, outer, inner, **kw):
     return call(
         wave_kernel, "wave",
-        (first_x, cur, cour, aperture, fwd, begun, second, third, outer, inner, ALONG_Z, ALONG_Y),
+        (cur, cour, aperture, fwd, begun, second, third, outer, inner, ALONG_Z, ALONG_Y),
         [((4, 4, 8, 8, NZ), F32), (planes(EXT), F32), (planes(EXT), F32)],
         [pltpu.VMEM(planes(n), F32) for n in (16, 8, 8, 8, 24)]
         + [
             pltpu.SMEM((1, 2), jnp.int32), pltpu.SemaphoreType.DMA(()),
         ],
-        scalars=1, stay=(3,), near=(0, 1, 2), **kw,
+        stay=(2,), near=(0, 1, 2), **kw,
     )
 
 
@@ -403,10 +415,10 @@
     return call(store_kernel, "store", (one, two), outs, sems, far=(0, 1), **kw)
 
 
-def decode(odd_y, pieces, latent, **kw):
+def decode(pieces, latent, **kw):
     return call(
-        decode_kernel, "decode", (odd_y, pieces, SPREAD[:, : 2 * NZ], latent, PICK),
-        [((64, NZ), F32), ((32, 4, NZ), F32)], scalars=1, near=(0, 1), **kw,
+        decode_kernel, "decode", (pieces, SPREAD[:, : 2 * NZ], latent, PICK),
+        [((64, NZ), F32), ((32, 4, NZ), F32)], near=(0, 1), **kw,
     )
 
 
@@ -434,25 +446,23 @@
 
 
 def body(wave_now, wave_prev, courant, forward, receivers, residual, aperture, latent, weight):
-    first_x = (lax.axis_index(SLAB) * EXT).astype(jnp.int32).reshape(1)
     cur, prev = wave_now[0], wave_prev[0]
     rec, res = receivers.transpose(1, 0, 2), residual.transpose(1, 0, 2)
-    outer, inner, begun = head(first_x, cur, prev, courant, rec, res)
+    outer, inner, begun = head(cur, prev, courant, rec, res)
     count = lax.axis_size(SLAB)
     outer = lax.ppermute(outer, SLAB, swaps(range(1, count - 1, 2)))
     inner = lax.ppermute(inner, SLAB, swaps(range(0, count, 2)))
-    second, third, fwd = inject(first_x, forward[0], rec, res)
+    second, third, fwd = inject(forward[0], rec, res)
     lat = latent_rows(latent)
     mix = mixing(weight)
     rows, after, before = wave(
-        first_x, cur, courant, aperture, fwd, begun, second, third, outer, inner
+        cur, courant, aperture, fwd, begun, second, third, outer, inner
     )
     near = gather_sum(lax.all_to_all(rows, "y", 0, 0, tiled=True))
     pieces = lax.all_to_all(near, "zh", 0, 0, tiled=True)
     after, before = store(after, before)
     pieces, after, before, lat, mix = lax.optimization_barrier((pieces, after, before, lat, mix))
-    odd_y = (lax.axis_index("y") & 1).astype(jnp.int32).reshape(1)
-    tile, shares = decode(odd_y, pieces, lat)
+    tile, shares = decode(pieces, lat)
     latent_grad = latent_out(mix, tile)
     shares = lax.all_to_all(shares, ("y", "x", "c"), 0, 0, tiled=True)
     shares, latent_grad = lax.optimization_barrier((shares, latent_grad))

time: 92.8 us -> 92.7 us (level)
  no operation moved by 1% of the time
where the time goes in v6:
time: 92.7 us; the launch traced here: 92.2 us
  starting transfers between devices  33.3 us (36%)
  blocking collectives  28.1 us (30%)
  waiting for transfers between devices  16.6 us (18%)
  Pallas kernels  10.9 us (12%)
  local copies, waits for them, and re-layouts  2.32 us (3%)
    all_to_all x1, blocking collectives, body(): shares = lax.all_to_all(shares, ('zh', 'zl'), 0, 0, tiled=True)  15.5 us
    all_to_all x1, starting transfers between devices, body(): pieces = lax.all_to_all(near, 'zh', 0, 0, tiled=True)  13.9 us
    all_to_all x1, blocking collectives, body(): near = gather_sum(lax.all_to_all(rows, 'y', 0, 0, tiled=True))  12.6 us
    pallas_call x9, Pallas kernels, call(): pl.pallas_call(kernel, name=name, in_specs=specs, out_specs=[HB if k in f...  10.9 us
    all_to_all x1, waiting for transfers between devices, body(): pieces = lax.all_to_all(near, 'zh', 0, 0, tiled=True)  10.2 us
    all_to_all x1, starting transfers between devices, body(): shares = lax.all_to_all(shares, ('y', 'x', 'c'), 0, 0, tiled=True)  9.78 us
    all_to_all x1, waiting for transfers between devices, body(): shares = lax.all_to_all(shares, ('y', 'x', 'c'), 0, 0, tiled=True)  6.02 us
    ppermute x1, starting transfers between devices, body(): inner = lax.ppermute(inner, SLAB, swaps(range(0, count, 2)))  4.97 us
  transfers between devices with their start and end apart: 4, of which 3 were waited for; matrix products, arithmetic and copies ran while one was open for 1% of the time, Pallas kernels for 4%

profile of v6, /device:TPU:1, one launch (start us, length us, event | category | flops | bytes accessed | tf_op | source)
XLA Modules:
  0.0 92.2 jit_solution(14860595497674828402)
XLA Ops:
  0.6 0.0 copy-start.6
  0.6 0.0 copy-start.7
  0.7 0.0 copy-start.1
  0.7 2.3 %head.1 = (f32[16,64,128]{2,1,0:T(8,128)S(1)}, f32[16,64,128]{2,1,0:T(8,128)S(1)}, f32[16,64,128]{2,1,0:T(8,128)S(1)}) custom-call(f32[16,64,128]{2,1,0:T(8,128)} %bitcast.28, f32[16,64,128]{2,1,0:T(8,128)} %bitcast.39, f32[16,64,128]{2,1,0:T(8,128)} %cour.1, s32[3,1,256]{2,1,0:T(1,128)} %bitcast.31, f32[3,1,256]{2,1,0:T(1,128)} %bitcast.33, ...), custom_call_target="tpu_custom_call" | custom-call | tf_op jit(solution)/shard_map/head/pallas_call | solution.py:353
  3.0 0.0 copy-start
  3.0 4.6 %collective-permute-start = (f32[16,64,128]{2,1,0:T(8,128)S(1)}, f32[16,64,128]{2,1,0:T(8,128)S(1)}, u32[]{:S(2)}, u32[]{:S(2)}) collective-permute-start(f32[16,64,128]{2,1,0:T(8,128)S(1)} %get-tuple-element.28), channel_id=1, source_target_pairs={{1,2},{2,1},{3,4},{4,3},{5,6},{6,5},{7,8},{8,7},{9,10},{10,9},{11,... | collective-permute-start | bytes 1572872 | tf_op jit(solution)/shard_map/ppermute | solution.py:453
  7.7 5.0 %collective-permute-start.1 = (f32[16,64,128]{2,1,0:T(8,128)S(1)}, f32[16,64,128]{2,1,0:T(8,128)S(1)}, u32[]{:S(2)}, u32[]{:S(2)}) collective-permute-start(f32[16,64,128]{2,1,0:T(8,128)S(1)} %get-tuple-element.29), channel_id=1, source_target_pairs={{0,1},{1,0},{2,3},{3,2},{4,5},{5,4},{6,7},{7,6},{8,9},{9,8},{10,11... | collective-permute-start | bytes 1572872 | tf_op jit(solution)/shard_map/ppermute | solution.py:454
  12.6 0.0 copy-done.6
  12.6 0.0 copy-done.7
  12.7 0.0 copy-start.2
  12.7 0.0 copy-start.4
  12.7 1.4 %inject.1 = (f32[24,64,128]{2,1,0:T(8,128)S(1)}, f32[16,64,128]{2,1,0:T(8,128)S(1)}, bf16[3,16,64,128]{3,2,1,0:T(8,128)(2,1)S(1)}) custom-call(bf16[3,16,64,128]{3,2,1,0:T(8,128)(2,1)} %bitcast.37, s32[3,1,256]{2,1,0:T(1,128)S(1)} %bitcast.32, f32[3,1,256]{2,1,0:T(1,128)S(1)} %bitcast.34), custom_call_target="tpu_custom_call" | custom-call | tf_op jit(solution)/shard_map/inject/pallas_call | solution.py:353
  14.1 0.4 collective-permute-done.outer
  14.5 0.0 collective-permute-done.1.inner
  14.5 0.0 copy-done.1
  14.5 0.0 copy-done
  14.5 0.0 copy-done.2
  14.5 0.0 copy-done.4
  14.5 2.4 %wave.1 = (f32[4,4,8,8,128]{4,3,2,1,0:T(8,128)S(1)}, f32[16,64,128]{2,1,0:T(8,128)S(1)}, f32[16,64,128]{2,1,0:T(8,128)S(1)}) custom-call(f32[16,64,128]{2,1,0:T(8,128)S(1)} %bitcast.29, f32[16,64,128]{2,1,0:T(8,128)S(1)} %copy-done.1, s32[1,2]{1,0:T(1,128)} %span_in.1, bf16[3,16,64,128]{3,2,1,0:T(8,128)(2,1)S(1)} %get-tuple-element.24.fwd, ...), custom_call_target="tpu_custom_call" | custom-call | tf_op jit(solution)/shard_map/wave/pallas_call | solution.py:353
  17.0 12.6 %all_to_all.20.pieces = f32[4,4,8,8,128]{4,3,2,1,0:T(8,128)S(1)} all-to-all(f32[4,4,8,8,128]{4,3,2,1,0:T(8,128)S(1)} %get-tuple-element.30), channel_id=1, replica_groups=mesh['zh'=4,'y'=4,'zl'=4,'x'=4,'c'=2] {'y'}, dimensions={0} | all-to-all | bytes 1048576 | tf_op jit(solution)/shard_map/all_to_all | solution.py:461
  29.6 0.7 near.1
  30.3 13.9 %all-to-all-start.1 = ((f32[4,8,8,128]{3,2,1,0:T(8,128)}), f32[4,8,8,128]{3,2,1,0:T(8,128)S(1)}, u32[]{:S(2)}, u32[]{:S(2)}) async-start(f32[4,8,8,128]{3,2,1,0:T(8,128)} %near.1), calls=%async_computation.1 | async-start | bytes 262144 | tf_op jit(solution)/shard_map/all_to_all | solution.py:462
  44.1 0.0 copy-done.9
  44.1 0.2 reshape.28
  44.4 0.2 copy.30
  44.5 0.1 pad.4
  44.6 0.0 copy-start.10
  44.7 0.6 copy-done.10
  45.3 0.1 reshape.30
  45.4 0.0 copy-start.11
  45.4 0.1 copy.23
  45.5 0.6 copy-done.11
  46.1 0.1 broadcast_multiply_fusion
  46.2 0.3 mul.23
  46.5 0.0 copy-start.5
  46.5 1.0 %store.1 = (f32[16,64,128]{2,1,0:T(8,128)}, f32[16,64,128]{2,1,0:T(8,128)}) custom-call(f32[16,64,128]{2,1,0:T(8,128)S(1)} %get-tuple-element.31.one, f32[16,64,128]{2,1,0:T(8,128)S(1)} %get-tuple-element.32.two), custom_call_target="tpu_custom_call" | custom-call | tf_op jit(solution)/shard_map/store/pallas_call | solution.py:353
  47.5 0.0 copy-start.8
  47.5 10.2 %all-to-all-done.1.pieces = f32[4,8,8,128]{3,2,1,0:T(8,128)S(1)} async-done(((f32[4,8,8,128]{3,2,1,0:T(8,128)}), f32[4,8,8,128]{3,2,1,0:T(8,128)S(1)}, u32[]{:S(2)}, u32[]{:S(2)}) %all-to-all-start.1) | async-done | bytes 131104 | tf_op jit(solution)/shard_map/all_to_all | solution.py:462
  57.8 0.0 copy-done.5
  57.8 0.0 copy-done.8
  57.8 1.1 %decode.1 = (f32[64,128]{1,0:T(8,128)S(1)}, f32[32,4,128]{2,1,0:T(4,128)}) custom-call(f32[4,8,8,128]{3,2,1,0:T(8,128)S(1)} %all-to-all-done.1.pieces, bf16[128,256]{1,0:T(8,128)(2,1)S(1)} %copy-done.5, bf16[128,1024]{1,0:T(8,128)(2,1)S(1)} %bitcast.30, f32[8,16]{1,0:T(8,128)S(1)} %copy-done.8), custom_call_target="tpu_custom_call" | custom-call | tf_op jit(solution)/shard_map/decode/pallas_call | solution.py:353
  58.9 9.8 %all-to-all-start.2 = ((f32[32,4,128]{2,1,0:T(4,128)}), f32[32,4,128]{2,1,0:T(4,128)S(1)}, u32[]{:S(2)}, u32[]{:S(2)}) async-start(f32[32,4,128]{2,1,0:T(4,128)} %get-tuple-element.39), calls=%async_computation.2 | async-start | bytes 131072 | tf_op jit(solution)/shard_map/all_to_all | solution.py:467
  68.7 0.1 copy.24.mix
  68.8 0.0 copy-done.3
  68.8 1.2 %latent.1 = f32[512,128]{1,0:T(8,128)} custom-call(f32[64,32]{1,0:T(8,128)S(1)} %copy.24.mix, f32[64,128]{1,0:T(8,128)S(1)} %get-tuple-element.41.tile, bf16[128,512]{1,0:T(8,128)(2,1)S(1)} %copy-done.3), custom_call_target="tpu_custom_call" | custom-call | tf_op jit(solution)/shard_map/latent/pallas_call | solution.py:353
  70.0 6.0 %all-to-all-done.2.pieces = f32[32,4,128]{2,1,0:T(4,128)S(1)} async-done(((f32[32,4,128]{2,1,0:T(4,128)}), f32[32,4,128]{2,1,0:T(4,128)S(1)}, u32[]{:S(2)}, u32[]{:S(2)}) %all-to-all-start.2) | async-done | bytes 65568 | tf_op jit(solution)/shard_map/all_to_all | solution.py:467
  76.1 15.5 %all_to_all.21.pieces = f32[16,4,128]{2,1,0:T(4,128)S(1)} all-to-all(f32[16,4,128]{2,1,0:T(4,128)S(1)} %share.1), channel_id=1, replica_groups=mesh['zh'=4,'y'=4,'zl'=4,'x'=4,'c'=2] {'zh','zl'}, dimensions={0} | all-to-all | bytes 65536 | tf_op jit(solution)/shard_map/all_to_all | solution.py:470
  91.5 0.7 total.1
  (4 shorter events, 0.1 us)
Async XLA Ops:
  0.6 12.0 %copy-start.6 = (s32[1,3,256]{2,0,1:T(1,128)S(1)}, s32[1,3,256]{2,0,1:T(1,128)}, u32[]{:S(2)}) copy-start(s32[1,3,256]{2,0,1:T(1,128)} %param.19) | copy-start | bytes 9220
  0.6 12.0 %copy-start.7 = (f32[1,3,256]{2,0,1:T(1,128)S(1)}, f32[1,3,256]{2,0,1:T(1,128)}, u32[]{:S(2)}) copy-start(f32[1,3,256]{2,0,1:T(1,128)} %param.20) | copy-start | bytes 9220
  0.7 13.9 %copy-start.1 = (f32[16,64,128]{2,1,0:T(8,128)S(1)}, f32[16,64,128]{2,1,0:T(8,128)}, u32[]{:S(2)}) copy-start(f32[16,64,128]{2,1,0:T(8,128)} %cour.1) | copy-start | bytes 1572868
  3.0 11.5 %copy-start = (f32[1,16,64,128]{3,2,1,0:T(8,128)S(1)}, f32[1,16,64,128]{3,2,1,0:T(8,128)}, u32[]{:S(2)}) copy-start(f32[1,16,64,128]{3,2,1,0:T(8,128)} %param.15) | copy-start | bytes 1572868
  3.0 11.5 %collective-permute-start = (f32[16,64,128]{2,1,0:T(8,128)S(1)}, f32[16,64,128]{2,1,0:T(8,128)S(1)}, u32[]{:S(2)}, u32[]{:S(2)}) collective-permute-start(f32[16,64,128]{2,1,0:T(8,128)S(1)} %get-tuple-element.28), channel_id=1, source_target_pairs={{1,2},{2,1},{3,4},{4,3},{5,6},{6,5},{7,8},{8,7},{9,10},{10,9},{11,... | collective-permute-start | bytes 1572872 | tf_op jit(solution)/shard_map/ppermute | solution.py:453
  7.7 6.9 %collective-permute-start.1 = (f32[16,64,128]{2,1,0:T(8,128)S(1)}, f32[16,64,128]{2,1,0:T(8,128)S(1)}, u32[]{:S(2)}, u32[]{:S(2)}) collective-permute-start(f32[16,64,128]{2,1,0:T(8,128)S(1)} %get-tuple-element.29), channel_id=1, source_target_pairs={{0,1},{1,0},{2,3},{3,2},{4,5},{5,4},{6,7},{7,6},{8,9},{9,8},{10,11... | collective-permute-start | bytes 1572872 | tf_op jit(solution)/shard_map/ppermute | solution.py:454
  12.7 1.9 %copy-start.2 = (bf16[384,128]{1,0:T(8,128)(2,1)S(1)}, bf16[384,128]{1,0:T(8,128)(2,1)}, u32[]{:S(2)}) copy-start(bf16[384,128]{1,0:T(8,128)(2,1)} %constant.15.clone.z_in.along_z) | copy-start | bytes 294916
  12.7 1.9 %copy-start.4 = (bf16[64,192]{1,0:T(8,128)(2,1)S(1)}, bf16[64,192]{1,0:T(8,128)(2,1)}, u32[]{:S(2)}) copy-start(bf16[64,192]{1,0:T(8,128)(2,1)} %constant.16.clone.y_in.along_y) | copy-start | bytes 73732
  30.3 13.9 %copy-start.9 = (bf16[8,2,4096]{2,1,0:T(2,128)(2,1)S(1)}, bf16[8,2,4096]{2,1,0:T(2,128)(2,1)}, u32[]{:S(2)}) copy-start(bf16[8,2,4096]{2,1,0:T(2,128)(2,1)} %param.22) | copy-start | bytes 393220
  30.3 27.5 %all-to-all-start.1 = ((f32[4,8,8,128]{3,2,1,0:T(8,128)}), f32[4,8,8,128]{3,2,1,0:T(8,128)S(1)}, u32[]{:S(2)}, u32[]{:S(2)}) async-start(f32[4,8,8,128]{3,2,1,0:T(8,128)} %near.1), calls=%async_computation.1 | async-start | bytes 262144 | tf_op jit(solution)/shard_map/all_to_all | solution.py:462
  44.6 0.7 copy-start.10
  45.4 0.7 copy-start.11
  46.5 11.2 %copy-start.5 = (bf16[128,256]{1,0:T(8,128)(2,1)S(1)}, bf16[128,256]{1,0:T(8,128)(2,1)}, u32[]{:S(2)}) copy-start(bf16[128,256]{1,0:T(8,128)(2,1)} %constant.18.clone.spread) | copy-start | bytes 196612
  47.5 10.2 %copy-start.8 = (f32[8,16]{1,0:T(8,128)S(1)}, f32[8,16]{1,0:T(8,128)}, u32[]{:S(2)}) copy-start(f32[8,16]{1,0:T(8,128)} %constant.19.clone.pick) | copy-start | bytes 1540
  58.9 9.9 %copy-start.3 = (bf16[128,512]{1,0:T(8,128)(2,1)S(1)}, bf16[128,512]{1,0:T(8,128)(2,1)}, u32[]{:S(2)}) copy-start(bf16[128,512]{1,0:T(8,128)(2,1)} %constant.20.clone.spread) | copy-start | bytes 393220
  58.9 17.1 %all-to-all-start.2 = ((f32[32,4,128]{2,1,0:T(4,128)}), f32[32,4,128]{2,1,0:T(4,128)S(1)}, u32[]{:S(2)}, u32[]{:S(2)}) async-start(f32[32,4,128]{2,1,0:T(4,128)} %get-tuple-element.39), calls=%async_computation.2 | async-start | bytes 131072 | tf_op jit(solution)/shard_map/all_to_all | solution.py:467
